TPU v7x, 32 devices: a whole 2x2x4 slice. The times are simulated.
32 devices in a mesh: lat: 4 (over x, core), lon: 8 (over z, y).
Axes of the slice: x: 2, y: 2, z: 4, core: 2. Of those that a mesh axis runs over, the one named last changes fastest.
Arguments:
- source: float32 [1024, 16384], P('lat', 'lon'), may hold values from -80 to 80
- flags: int32 [8, 128], P('lat', 'lon'), may hold values from 0 to 2
Outputs:
- solution: float32 [1024, 16384], P('lat', 'lon')
- residual: float32 [1024, 16384], P('lat', 'lon')
All inputs are finite; a program needn't handle non-finite values.
Results may differ from a plain program's by a relative error of at most 0.0001.
Values sent between devices are 32-bit elements; how exact they have to be, the bound alone decides.
No kernel may reach another device: no remote copies, remote signals or barrier semaphores. Data moves between devices by JAX's collectives and lax.ppermute only.
A program may use at most 64 MiB of HBM per device.

v0:
```python
import math

import jax
import jax.numpy as jnp
from jax import lax
from jax.sharding import PartitionSpec as P

ITERS = 2


ARC_SPAN = 2.0 * math.pi / 3.0


def extended(block, sides, width, periodic):
    for axis, dim in sides:
        count = lax.axis_size(axis)
        forward = [(i, i + 1) for i in range(count - 1)]
        if periodic:
            forward.append((count - 1, 0))
        backward = [(target, source) for source, target in forward]
        low = lax.ppermute(
            lax.slice_in_dim(block, block.shape[dim] - width, None, axis=dim), axis, forward
        )
        high = lax.ppermute(lax.slice_in_dim(block, 0, width, axis=dim), axis, backward)
        block = jnp.concatenate([low, block, high], axis=dim)
    return block


def geometry(start, count, total_rows):
    row_ids = start + jnp.arange(count, dtype=jnp.int32)
    row_pos = row_ids.astype(jnp.float32)
    east_west = jnp.cos((row_pos + 0.5) / total_rows * ARC_SPAN - 0.5 * ARC_SPAN)[:, None]
    upper = jnp.cos(row_pos / total_rows * ARC_SPAN - 0.5 * ARC_SPAN)[:, None]
    lower = jnp.cos((row_pos + 1.0) / total_rows * ARC_SPAN - 0.5 * ARC_SPAN)[:, None]
    inside = ((row_ids >= 0) & (row_ids < total_rows)).astype(jnp.float32)[:, None]
    return (east_west, upper, lower, inside)


def screen_cells(tiles):
    values = jnp.where(tiles == 0, 0.05, jnp.where(tiles == 1, 0.4, 2.0)).astype(jnp.float32)
    tile_rows, tile_cols = values.shape
    spread = jnp.broadcast_to(values[:, None, :, None], (tile_rows, 128, tile_cols, 128))
    return spread.reshape(tile_rows * 128, tile_cols * 128)


def stencil(value, above, below, west_side, east_side, coeffs):
    diag, east_west, upper, lower = coeffs
    return diag * value - east_west * (east_side + west_side) - upper * above - lower * below


def classic_apply(value, coeffs):
    banded = extended(value, (("lat", 0),), 1, False)
    widened = extended(value, (("lon", 1),), 1, True)
    return stencil(value, banded[:-2], banded[2:], widened[:, :-2], widened[:, 2:], coeffs)


def classic_total(left, right):
    return lax.psum(jnp.sum(left * right), ("lat", "lon"))


def per_device(source, flags):
    band_rows, sector_cols = source.shape
    total_rows = band_rows * lax.axis_size("lat")
    first_row = lax.axis_index("lat") * band_rows
    east_west, upper, lower, inside = geometry(first_row, band_rows, total_rows)
    diag = screen_cells(flags) + 2.0 * east_west + upper + lower
    coeffs = (diag, east_west, upper, lower)
    solution = jnp.zeros_like(source)
    remain = source
    precond = remain / diag
    search = precond
    energy = classic_total(remain, precond)
    for step in range(ITERS):
        image = classic_apply(search, coeffs)
        alpha = energy / classic_total(search, image)
        solution = solution + alpha * search
        remain = remain - alpha * image
        if step + 1 < ITERS:
            precond = remain / diag
            fresh = classic_total(remain, precond)
            search = precond + fresh / energy * search
            energy = fresh
    return (solution, remain)


def solution(mesh):
    in_specs = (P("lat", "lon"), P("lat", "lon"))
    out_specs = (P("lat", "lon"), P("lat", "lon"))
    return jax.shard_map(
        per_device, mesh=mesh, in_specs=in_specs, out_specs=out_specs, check_vma=False
    )
```

profile of v0, /device:TPU:0, one launch (start us, length us, event | category | flops | bytes accessed | tf_op | source)
XLA Modules:
  0.0 182.4 jit_solution(11717256058555288643)
XLA Ops:
  0.6 0.0 copy-start.3
  0.7 0.1 add_cosine_fusion
  0.8 0.8 compare_select_fusion.1
  1.6 0.2 broadcast_in_dim.24
  1.8 0.5 copy-done.3
  2.2 0.9 fusion.17
  3.1 0.0 copy-start
  3.2 2.4 %collective-permute-start.2 = (f32[1,2048]{1,0:T(1,128)S(1)}, f32[1,2048]{1,0:T(1,128)S(1)}, u32[]{:S(2)}, u32[]{:S(2)}) collective-permute-start(f32[1,2048]{1,0:T(1,128)S(1)} %get-tuple-element.17), channel_id=1, source_target_pairs={{0,8},{8,16},{16,24},{1,9},{9,17},{17,25},{2,10},{10,18},{18,26},{... | collective-permute-start | bytes 24584 | tf_op jit(solution)/shard_map/ppermute | solution.py:21
  5.5 1.3 collective-permute-start.3
  6.8 0.1 fusion.22
  6.9 5.4 %collective-permute-start = (f32[256,1]{1,0:T(8,128)S(1)}, f32[256,1]{1,0:T(8,128)S(1)}, u32[]{:S(2)}, u32[]{:S(2)}) collective-permute-start(f32[256,1]{1,0:T(8,128)S(1)} %get-tuple-element.15), channel_id=1, source_target_pairs={{1,0},{2,1},{3,2},{4,3},{5,4},{6,5},{7,6},{0,7},{9,8},{10,9},{11,1... | collective-permute-start | bytes 3080 | tf_op jit(solution)/shard_map/ppermute | solution.py:24
  12.4 0.0 collective-permute-start.1
  12.4 2.5 %collective-permute-done = f32[256,1]{1,0:T(8,128)S(1)} collective-permute-done((f32[256,1]{1,0:T(8,128)S(1)}, f32[256,1]{1,0:T(8,128)S(1)}, u32[]{:S(2)}, u32[]{:S(2)}) %collective-permute-start) | collective-permute-done | bytes 1056 | tf_op jit(solution)/shard_map/ppermute | solution.py:24
  14.9 5.4 %collective-permute-done.1 = f32[256,1]{1,0:T(8,128)S(1)} collective-permute-done((f32[256,1]{1,0:T(8,128)S(1)}, f32[256,1]{1,0:T(8,128)S(1)}, u32[]{:S(2)}, u32[]{:S(2)}) %collective-permute-start.1) | collective-permute-done | bytes 1056 | tf_op jit(solution)/shard_map/ppermute | solution.py:21
  20.3 0.0 collective-permute-done.2
  20.3 5.0 %multiply_reduce_fusion.2 = (f32[]{:T(128)}, f32[]{:T(128)}, f32[256,2048]{1,0:T(8,128)}) fusion(f32[256,2048]{1,0:T(8,128)S(1)} %fusion.17, f32[256,2048]{1,0:T(8,128)S(1)} %copy-done.3, f32[1,2048]{1,0:T(1,128)S(1)} %collective-permute-done.3, f32[1,2048]{1,0:T(1,128)S(1)} %collective-permute-done.2, f32[256,1]{1,0:T(8,128)S(1)} %collective-permute-done.1, ...), kind=kLoop, calls=%fused_computation.31 | loop fusion | flops 9961470 | bytes 8411144 | tf_op jit(solution)/shard_map/reduce_sum | solution.py:58
  25.3 38.9 %all-reduce = (f32[]{:T(128)}, f32[]{:T(128)}) all-reduce(f32[]{:T(128)} %get-tuple-element.3, f32[]{:T(128)} %get-tuple-element.2), channel_id=1, replica_groups=mesh['lat'=4,'lon'=8] {'lat','lon'}, use_global_device_ids=true, to_apply=%region_1.2 | all-reduce | flops 2 | bytes 16 | tf_op jit(solution)/shard_map/psum | solution.py:58
  65.5 5.1 %multiply_reduce_fusion.1 = (f32[]{:T(128)}, f32[256,2048]{1,0:T(8,128)}) fusion(f32[256]{0:T(256)S(1)} %get-tuple-element.19, f32[256]{0:T(256)S(1)} %get-tuple-element.20, f32[256]{0:T(256)S(1)} %broadcast_multiply_fusion, f32[32,8,16,128]{3,2,1,0:T(8,128)S(1)} %bitcast.24, f32[256,2048]{1,0:T(8,128)} %param.2, f32[256,2048]{1,0:T(8,128)} %get-tuple-element.10, ...), kind=kLoop, calls=%fused_computation.29 | loop fusion | flops 4194303 | bytes 8391688 | tf_op jit(solution)/shard_map/reduce_sum | solution.py:58
  70.5 43.2 %psum.30 = f32[]{:T(128)} all-reduce(f32[]{:T(128)} %get-tuple-element.8), channel_id=1, replica_groups=mesh['lat'=4,'lon'=8] {'lat','lon'}, use_global_device_ids=true, to_apply=%region_5.6 | all-reduce | flops 1 | bytes 8 | tf_op jit(solution)/shard_map/psum | solution.py:58
  115.1 3.2 %multiply_add_fusion.1 = f32[256,2048]{1,0:T(8,128)S(1)} fusion(f32[256,2048]{1,0:T(8,128)} %copy-done, f32[]{:T(128)S(6)} %div.21, f32[256,2048]{1,0:T(8,128)} %get-tuple-element.9, f32[256]{0:T(256)S(1)} %get-tuple-element.19, f32[256]{0:T(256)S(1)} %get-tuple-element.20, f32[256]{0:T(256)S(1)} %broadcast_multiply_fusion, f32[32,8,16,128]{3,2,1,0:T(8,128)S(1)} %bitcast.25), kind=kLoop, calls=%fused_computation.28 | loop fusion | flops 3145728 | bytes 8391684 | tf_op jit(solution)/shard_map/add | solution.py:81
  118.2 0.0 copy-start.1
  118.3 1.3 collective-permute-start.6
  119.6 1.3 collective-permute-start.7
  120.9 0.1 fusion.20
  121.0 3.6 %collective-permute-start.4 = (f32[256,1]{1,0:T(8,128)S(1)}, f32[256,1]{1,0:T(8,128)S(1)}, u32[]{:S(2)}, u32[]{:S(2)}) collective-permute-start(f32[256,1]{1,0:T(8,128)S(1)} %get-tuple-element.11), channel_id=1, source_target_pairs={{1,0},{2,1},{3,2},{4,3},{5,4},{6,5},{7,6},{0,7},{9,8},{10,9},{11,1... | collective-permute-start | bytes 3080 | tf_op jit(solution)/shard_map/ppermute | solution.py:24
  124.6 0.0 collective-permute-start.5
  124.6 3.3 %collective-permute-done.4 = f32[256,1]{1,0:T(8,128)S(1)} collective-permute-done((f32[256,1]{1,0:T(8,128)S(1)}, f32[256,1]{1,0:T(8,128)S(1)}, u32[]{:S(2)}, u32[]{:S(2)}) %collective-permute-start.4) | collective-permute-done | bytes 1056 | tf_op jit(solution)/shard_map/ppermute | solution.py:24
  127.9 5.4 %collective-permute-done.5 = f32[256,1]{1,0:T(8,128)S(1)} collective-permute-done((f32[256,1]{1,0:T(8,128)S(1)}, f32[256,1]{1,0:T(8,128)S(1)}, u32[]{:S(2)}, u32[]{:S(2)}) %collective-permute-start.5) | collective-permute-done | bytes 1056 | tf_op jit(solution)/shard_map/ppermute | solution.py:21
  133.3 4.8 %multiply_reduce_fusion = (f32[]{:T(128)}, f32[256,2048]{1,0:T(8,128)}) fusion(f32[256,2048]{1,0:T(8,128)S(1)} %multiply_add_fusion.1, f32[1,2048]{1,0:T(1,128)S(1)} %collective-permute-done.7, f32[1,2048]{1,0:T(1,128)S(1)} %collective-permute-done.6, f32[256,1]{1,0:T(8,128)S(1)} %collective-permute-done.5, f32[256,1]{1,0:T(8,128)S(1)} %collective-permute-done.4, ...), kind=kLoop, calls=%fused_computation.27 | loop fusion | flops 8912895 | bytes 6313988 | tf_op jit(solution)/shard_map/reduce_sum | solution.py:58
  138.1 37.2 %psum.31 = f32[]{:T(128)} all-reduce(f32[]{:T(128)} %get-tuple-element.6), channel_id=1, replica_groups=mesh['lat'=4,'lon'=8] {'lat','lon'}, use_global_device_ids=true, to_apply=%region_7.8 | all-reduce | flops 1 | bytes 8 | tf_op jit(solution)/shard_map/psum | solution.py:58
  176.6 4.2 %multiply_add_fusion = f32[256,2048]{1,0:T(8,128)} fusion(f32[256,2048]{1,0:T(8,128)} %copy-done.1, f32[256,2048]{1,0:T(8,128)} %copy-done, f32[]{:T(128)S(6)} %div.22, f32[]{:T(128)S(6)} %div.19), kind=kLoop, calls=%fused_computation.26 | loop fusion | flops 1572864 | bytes 6291464 | tf_op jit(solution)/shard_map/add | solution.py:76
  180.8 1.6 multiply_subtract_fusion
  (13 shorter events, 0.1 us)
Async XLA Ops:
  0.6 1.6 copy-start.3
  3.1 22.1 %copy-start = (f32[256,2048]{1,0:T(8,128)}, f32[256,2048]{1,0:T(8,128)S(1)}, u32[]{:S(2)}) copy-start(f32[256,2048]{1,0:T(8,128)S(1)} %fusion.17) | copy-start | bytes 6291460
  3.2 17.1 %collective-permute-start.2 = (f32[1,2048]{1,0:T(1,128)S(1)}, f32[1,2048]{1,0:T(1,128)S(1)}, u32[]{:S(2)}, u32[]{:S(2)}) collective-permute-start(f32[1,2048]{1,0:T(1,128)S(1)} %get-tuple-element.17), channel_id=1, source_target_pairs={{0,8},{8,16},{16,24},{1,9},{9,17},{17,25},{2,10},{10,18},{18,26},{... | collective-permute-start | bytes 24584 | tf_op jit(solution)/shard_map/ppermute | solution.py:21
  5.5 14.7 %collective-permute-start.3 = (f32[1,2048]{1,0:T(1,128)S(1)}, f32[1,2048]{1,0:T(1,128)S(1)}, u32[]{:S(2)}, u32[]{:S(2)}) collective-permute-start(f32[1,2048]{1,0:T(1,128)S(1)} %get-tuple-element.18), channel_id=1, source_target_pairs={{8,0},{16,8},{24,16},{9,1},{17,9},{25,17},{10,2},{18,10},{26,18},{... | collective-permute-start | bytes 24584 | tf_op jit(solution)/shard_map/ppermute | solution.py:24
  6.9 8.0 %collective-permute-start = (f32[256,1]{1,0:T(8,128)S(1)}, f32[256,1]{1,0:T(8,128)S(1)}, u32[]{:S(2)}, u32[]{:S(2)}) collective-permute-start(f32[256,1]{1,0:T(8,128)S(1)} %get-tuple-element.15), channel_id=1, source_target_pairs={{1,0},{2,1},{3,2},{4,3},{5,4},{6,5},{7,6},{0,7},{9,8},{10,9},{11,1... | collective-permute-start | bytes 3080 | tf_op jit(solution)/shard_map/ppermute | solution.py:24
  12.4 7.9 %collective-permute-start.1 = (f32[256,1]{1,0:T(8,128)S(1)}, f32[256,1]{1,0:T(8,128)S(1)}, u32[]{:S(2)}, u32[]{:S(2)}) collective-permute-start(f32[256,1]{1,0:T(8,128)S(1)} %get-tuple-element.16), channel_id=1, source_target_pairs={{0,1},{1,2},{2,3},{3,4},{4,5},{5,6},{6,7},{7,0},{8,9},{9,10},{10,1... | collective-permute-start | bytes 3080 | tf_op jit(solution)/shard_map/ppermute | solution.py:21
  118.2 19.9 %copy-start.1 = (f32[256,2048]{1,0:T(8,128)}, f32[256,2048]{1,0:T(8,128)S(1)}, u32[]{:S(2)}) copy-start(f32[256,2048]{1,0:T(8,128)S(1)} %multiply_add_fusion.1) | copy-start | bytes 6291460
  118.3 15.0 %collective-permute-start.6 = (f32[1,2048]{1,0:T(1,128)S(1)}, f32[1,2048]{1,0:T(1,128)S(1)}, u32[]{:S(2)}, u32[]{:S(2)}) collective-permute-start(f32[1,2048]{1,0:T(1,128)S(1)} %get-tuple-element.13), channel_id=1, source_target_pairs={{0,8},{8,16},{16,24},{1,9},{9,17},{17,25},{2,10},{10,18},{18,26},{... | collective-permute-start | bytes 24584 | tf_op jit(solution)/shard_map/ppermute | solution.py:21
  119.6 13.7 %collective-permute-start.7 = (f32[1,2048]{1,0:T(1,128)S(1)}, f32[1,2048]{1,0:T(1,128)S(1)}, u32[]{:S(2)}, u32[]{:S(2)}) collective-permute-start(f32[1,2048]{1,0:T(1,128)S(1)} %get-tuple-element.14), channel_id=1, source_target_pairs={{8,0},{16,8},{24,16},{9,1},{17,9},{25,17},{10,2},{18,10},{26,18},{... | collective-permute-start | bytes 24584 | tf_op jit(solution)/shard_map/ppermute | solution.py:24
  121.0 6.9 %collective-permute-start.4 = (f32[256,1]{1,0:T(8,128)S(1)}, f32[256,1]{1,0:T(8,128)S(1)}, u32[]{:S(2)}, u32[]{:S(2)}) collective-permute-start(f32[256,1]{1,0:T(8,128)S(1)} %get-tuple-element.11), channel_id=1, source_target_pairs={{1,0},{2,1},{3,2},{4,3},{5,4},{6,5},{7,6},{0,7},{9,8},{10,9},{11,1... | collective-permute-start | bytes 3080 | tf_op jit(solution)/shard_map/ppermute | solution.py:24
  124.6 8.7 %collective-permute-start.5 = (f32[256,1]{1,0:T(8,128)S(1)}, f32[256,1]{1,0:T(8,128)S(1)}, u32[]{:S(2)}, u32[]{:S(2)}) collective-permute-start(f32[256,1]{1,0:T(8,128)S(1)} %get-tuple-element.12), channel_id=1, source_target_pairs={{0,1},{1,2},{2,3},{3,4},{4,5},{5,6},{6,7},{7,0},{8,9},{9,10},{10,1... | collective-permute-start | bytes 3080 | tf_op jit(solution)/shard_map/ppermute | solution.py:21
  176.6 4.2 %copy-start.2 = (f32[256,2048]{1,0:T(8,128)S(1)}, f32[256,2048]{1,0:T(8,128)}, u32[]{:S(2)}) copy-start(f32[256,2048]{1,0:T(8,128)} %get-tuple-element.9) | copy-start | bytes 6291460
  176.6 4.2 %copy-start.4 = (f32[256,2048]{1,0:T(8,128)S(1)}, f32[256,2048]{1,0:T(8,128)}, u32[]{:S(2)}) copy-start(f32[256,2048]{1,0:T(8,128)} %get-tuple-element.7) | copy-start | bytes 6291460
where the time goes:
time: 184 us; the launch traced here: 182 us
  blocking collectives  119 us (65%)
  other arithmetic  25.7 us (14%)
  waiting for transfers between devices  16.6 us (9%)
  starting transfers between devices  15.3 us (8%)
  between operations  4.68 us (3%)
    psum x3, blocking collectives, classic_total(): return lax.psum(jnp.sum(left * right), ('lat', 'lon'))  119 us
    reduce_sum x3, other arithmetic, classic_total(): return lax.psum(jnp.sum(left * right), ('lat', 'lon'))  14.9 us
    ppermute x4, starting transfers between devices, extended(): lax.ppermute(lax.slice_in_dim(block, 0, width, axis=dim), axis, backward)  11.6 us
    ppermute x4, waiting for transfers between devices, extended(): lax.ppermute(lax.slice_in_dim(block, block.shape[dim] - width, None, axis...  10.8 us
    ppermute x4, waiting for transfers between devices, extended(): lax.ppermute(lax.slice_in_dim(block, 0, width, axis=dim), axis, backward)  5.8 us
    add x1, other arithmetic, per_device(): solution = solution + alpha * search  4.19 us
  transfers between devices with their start and end apart: 8, of which 4 were waited for; matrix products, arithmetic and copies ran while one was open for 0% of the time, Pallas kernels for 0%

commit v1 on v0

v1 whole, which is shorter than its diff:
```python
import math

import jax
import jax.numpy as jnp
from jax import lax
from jax.sharding import PartitionSpec as P

ARC_SPAN = 2.0 * math.pi / 3.0


def shifted(block, axis, periodic):
    count = lax.axis_size(axis)
    forward = [(i, i + 1) for i in range(count - 1)]
    if periodic:
        forward.append((count - 1, 0))
    backward = [(target, source) for source, target in forward]
    return forward, backward


def halos(value):
    up, down = shifted(value, "lat", False)
    east, west = shifted(value, "lon", True)
    above = lax.ppermute(value[-1:], "lat", up)
    below = lax.ppermute(value[:1], "lat", down)
    cols = value[:, -1].reshape(1, -1), value[:, 0].reshape(1, -1)
    west_side = lax.ppermute(cols[0], "lon", east)
    east_side = lax.ppermute(cols[1], "lon", west)
    return above, below, west_side.reshape(-1, 1), east_side.reshape(-1, 1)


def geometry(start, count, total_rows):
    row_pos = (start + jnp.arange(count, dtype=jnp.int32)).astype(jnp.float32)
    east_west = jnp.cos((row_pos + 0.5) / total_rows * ARC_SPAN - 0.5 * ARC_SPAN)[:, None]
    upper = jnp.cos(row_pos / total_rows * ARC_SPAN - 0.5 * ARC_SPAN)[:, None]
    lower = jnp.cos((row_pos + 1.0) / total_rows * ARC_SPAN - 0.5 * ARC_SPAN)[:, None]
    return east_west, upper, lower


def screen_cells(tiles):
    values = jnp.where(tiles == 0, 0.05, jnp.where(tiles == 1, 0.4, 2.0)).astype(jnp.float32)
    tile_rows, tile_cols = values.shape
    spread = jnp.broadcast_to(values[:, None, :, None], (tile_rows, 128, tile_cols, 128))
    return spread.reshape(tile_rows * 128, tile_cols * 128)


def neighbours(value, coeffs):
    east_west, upper, lower = coeffs
    above, below, west, east = halos(value)
    above = jnp.concatenate([above, value[:-1]], axis=0)
    below = jnp.concatenate([value[1:], below], axis=0)
    west = jnp.concatenate([west, value[:, :-1]], axis=1)
    east = jnp.concatenate([value[:, 1:], east], axis=1)
    return east_west * (east + west) + upper * above + lower * below


def total(parts):
    value = jnp.pad(jnp.stack(parts)[None, :], ((0, 0), (0, 128 - len(parts))))
    for axis in ("lat", "lon"):
        count = lax.axis_size(axis)
        step = 1
        while step < count:
            value = value + lax.ppermute(value, axis, [(i, i ^ step) for i in range(count)])
            step *= 2
    return [value[0, i] for i in range(len(parts))]


def per_device(source, flags):
    band_rows, sector_cols = source.shape
    total_rows = band_rows * lax.axis_size("lat")
    coeffs = geometry(lax.axis_index("lat") * band_rows, band_rows, total_rows)
    east_west, upper, lower = coeffs
    diag = screen_cells(flags) + 2.0 * east_west + upper + lower
    inverse = 1.0 / diag
    base = source * inverse
    first = source - neighbours(base, coeffs)
    scaled = first * inverse
    second = first - neighbours(scaled, coeffs)
    sums = total(
        [
            jnp.sum(source * base),
            jnp.sum(base * first),
            jnp.sum(scaled * first),
            jnp.sum(scaled * second),
        ]
    )
    alpha = sums[0] / sums[1]
    fresh = alpha * alpha * sums[2] - 2.0 * alpha * sums[1] + sums[0]
    grow = 1.0 + fresh / sums[0]
    bend = grow * grow * sums[1] - 2.0 * grow * alpha * sums[2] + alpha * alpha * sums[3]
    beta = fresh / bend
    near, far = alpha + beta * grow, alpha * beta
    return near * base - far * scaled, source - near * first + far * second


def solution(mesh):
    in_specs = (P("lat", "lon"), P("lat", "lon"))
    out_specs = (P("lat", "lon"), P("lat", "lon"))
    return jax.shard_map(
        per_device, mesh=mesh, in_specs=in_specs, out_specs=out_specs, check_vma=False
    )
```

time: 184 us -> 82.7 us (0.45)
  blocking collectives: 119 us -> 0 us
  local copies, waits for them, and re-layouts: 0.92 us -> 13.2 us
  starting transfers between devices: 15.3 us -> 25.4 us
  waiting for transfers between devices: 16.6 us -> 12.4 us
    psum x3 -> x0, blocking collectives: 119 us -> none  [classic_total(): return lax.psum(jnp.sum(left * right), ('lat', 'lon'))]
    slice x4 -> x9, local copies, waits for them, and re-layouts: 0.22 us -> 11.5 us  [the longest x2 5.51 us: neighbours(): east = jnp.concatenate([value[:, 1:], east], axis=1)]
    ppermute x8 -> x13, starting transfers between devices: 15.3 us -> 25.4 us  [the longest x2 10.6 us: halos(): east_side = lax.ppermute(cols[1], 'lon', west)]
    mul x0 -> x2, other arithmetic: none -> 7.96 us  [the longest x1 7.03 us: per_device(): scaled = first * inverse]
    reduce_sum x3 -> x1, other arithmetic: 14.9 us -> 8.17 us  [per_device(): jnp.sum(source * base)]
    add x2 -> x6, other arithmetic: 7.38 us -> 1.93 us  [the longest x1 1.92 us: per_device(): return (near * base - far * scaled, source - near * first + far * second)]
    ppermute x8 -> x13, waiting for transfers between devices: 16.6 us -> 12.4 us  [the longest x5 12.2 us: total(): lax.ppermute(value, axis, [(i, i ^ step) for i in range(count)])]
    broadcast_in_dim x0 -> x1, other arithmetic: none -> 2.56 us  [total(): value = jnp.pad(jnp.stack(parts)[None, :], ((0, 0), (0, 128 - len(parts))))]
  transfers between devices with their start and end apart: 8 -> 13, of which waited for: 4 -> 6; matrix products, arithmetic and copies ran while one was open for 0% -> 10% of each run, Pallas kernels for 0% -> 0%
where the time goes in v1:
time: 82.7 us; the launch traced here: 82.4 us
  starting transfers between devices  25.4 us (31%)
  other arithmetic  25.1 us (30%)
  local copies, waits for them, and re-layouts  13.2 us (16%)
  waiting for transfers between devices  12.4 us (15%)
  between operations  6.38 us (8%)
    ppermute x5, waiting for transfers between devices, total(): lax.ppermute(value, axis, [(i, i ^ step) for i in range(count)])  12.2 us
    ppermute x2, starting transfers between devices, halos(): east_side = lax.ppermute(cols[1], 'lon', west)  10.6 us
    reduce_sum x1, other arithmetic, per_device(): jnp.sum(source * base)  8.17 us
    mul x1, other arithmetic, per_device(): scaled = first * inverse  7.03 us
    ppermute x5, starting transfers between devices, total(): lax.ppermute(value, axis, [(i, i ^ step) for i in range(count)])  6.23 us
    ppermute x2, starting transfers between devices, halos(): above = lax.ppermute(value[-1:], 'lat', up)  5.92 us
    slice x2, local copies, waits for them, and re-layouts, neighbours(): east = jnp.concatenate([value[:, 1:], east], axis=1)  5.51 us
    slice x2, local copies, waits for them, and re-layouts, neighbours(): above = jnp.concatenate([above, value[:-1]], axis=0)  4.91 us
  transfers between devices with their start and end apart: 13, of which 6 were waited for; matrix products, arithmetic and copies ran while one was open for 10% of the time, Pallas kernels for 0%

profile of v1, /device:TPU:0, one launch (start us, length us, event | category | flops | bytes accessed | tf_op | source)
XLA Modules:
  0.0 82.4 jit_solution(3046730710762124392)
XLA Ops:
  0.8 0.8 compare_select_fusion.1
  1.6 0.2 broadcast_in_dim.27
  1.8 0.5 copy-done.1
  2.2 0.9 %fusion.12 = f32[256,2048]{1,0:T(8,128)S(1)} fusion(f32[256,2048]{1,0:T(8,128)S(1)} %copy-done.1, f32[256]{0:T(256)S(1)} %get-tuple-element.29, f32[256]{0:T(256)S(1)} %get-tuple-element.30, f32[256]{0:T(256)S(1)} %broadcast_multiply_fusion, f32[32,8,16,128]{3,2,1,0:T(8,128)S(1)} %bitcast.32), kind=kLoop, calls=%fused_computation.38 | loop fusion | flops 2621440 | bytes 6294528 | tf_op jit(solution)/shard_map/mul | solution.py:74
  3.2 0.2 slice_reduce_fusion.2
  3.4 6.1 %collective-permute-start = (f32[1,256]{1,0:T(1,128)S(1)}, f32[1,256]{1,0:T(1,128)S(1)}, u32[]{:S(2)}, u32[]{:S(2)}) collective-permute-start(f32[1,256]{1,0:T(1,128)S(1)} %bitcast.35), channel_id=1, source_target_pairs={{1,0},{2,1},{3,2},{4,3},{5,4},{6,5},{7,6},{0,7},{9,8},{10,9},{11,1... | collective-permute-start | bytes 3080 | tf_op jit(solution)/shard_map/ppermute | solution.py:27
  9.5 1.5 %collective-permute-start.2 = (f32[1,2048]{1,0:T(1,128)S(1)}, f32[1,2048]{1,0:T(1,128)S(1)}, u32[]{:S(2)}, u32[]{:S(2)}) collective-permute-start(f32[1,2048]{1,0:T(1,128)S(1)} %get-tuple-element.21), channel_id=1, source_target_pairs={{0,8},{8,16},{16,24},{1,9},{9,17},{17,25},{2,10},{10,18},{18,26},{... | collective-permute-start | bytes 24584 | tf_op jit(solution)/shard_map/ppermute | solution.py:23
  11.0 1.3 %collective-permute-start.3 = (f32[1,2048]{1,0:T(1,128)S(1)}, f32[1,2048]{1,0:T(1,128)S(1)}, u32[]{:S(2)}, u32[]{:S(2)}) collective-permute-start(f32[1,2048]{1,0:T(1,128)S(1)} %get-tuple-element.22), channel_id=1, source_target_pairs={{8,0},{16,8},{24,16},{9,1},{17,9},{25,17},{10,2},{18,10},{26,18},{... | collective-permute-start | bytes 24584 | tf_op jit(solution)/shard_map/ppermute | solution.py:24
  12.3 2.4 %fusion.20 = (f32[255,2048]{1,0:T(8,128)}, f32[255,2048]{1,0:T(8,128)}) fusion(f32[256,2048]{1,0:T(8,128)S(1)} %fusion.12), kind=kLoop, calls=%fused_computation.44 | loop fusion | bytes 8355840 | tf_op jit(solution)/shard_map/slice | solution.py:49
  14.7 2.7 %fusion.18 = (f32[256,2047]{1,0:T(8,128)}, f32[256,2047]{1,0:T(8,128)}) fusion(f32[256,2048]{1,0:T(8,128)S(1)} %fusion.12), kind=kLoop, calls=%fused_computation.42 | loop fusion | bytes 8384512 | tf_op jit(solution)/shard_map/slice | solution.py:52
  17.8 7.0 %fusion.11 = (f32[256,2048]{1,0:T(8,128)S(1)}, f32[256,2048]{1,0:T(8,128)}) fusion(f32[256]{0:T(256)S(1)} %get-tuple-element.29, f32[256]{0:T(256)S(1)} %get-tuple-element.30, f32[256]{0:T(256)S(1)} %broadcast_multiply_fusion, f32[32,8,16,128]{3,2,1,0:T(8,128)} %bitcast.33, f32[256,2048]{1,0:T(8,128)} %param.2, f32[1,2048]{1,0:T(1,128)S(1)} %collective-permute-done.3, ...), kind=kLoop, calls=%fused_computation.37 | loop fusion | flops 8388608 | bytes 16781312 | tf_op jit(solution)/shard_map/mul | solution.py:76
  24.8 0.2 slice_reduce_fusion
  25.1 2.5 %fusion.17 = (f32[255,2048]{1,0:T(8,128)}, f32[255,2048]{1,0:T(8,128)}) fusion(f32[256,2048]{1,0:T(8,128)S(1)} %get-tuple-element.11), kind=kLoop, calls=%fused_computation.41 | loop fusion | bytes 8355840 | tf_op jit(solution)/shard_map/slice | solution.py:49
  27.6 4.6 %collective-permute-start.4 = (f32[1,256]{1,0:T(1,128)S(1)}, f32[1,256]{1,0:T(1,128)S(1)}, u32[]{:S(2)}, u32[]{:S(2)}) collective-permute-start(f32[1,256]{1,0:T(1,128)S(1)} %bitcast.36), channel_id=1, source_target_pairs={{1,0},{2,1},{3,2},{4,3},{5,4},{6,5},{7,6},{0,7},{9,8},{10,9},{11,1... | collective-permute-start | bytes 3080 | tf_op jit(solution)/shard_map/ppermute | solution.py:27
  32.1 4.5 %collective-permute-start.6 = (f32[1,2048]{1,0:T(1,128)S(1)}, f32[1,2048]{1,0:T(1,128)S(1)}, u32[]{:S(2)}, u32[]{:S(2)}) collective-permute-start(f32[1,2048]{1,0:T(1,128)S(1)} %get-tuple-element.15), channel_id=1, source_target_pairs={{0,8},{8,16},{16,24},{1,9},{9,17},{17,25},{2,10},{10,18},{18,26},{... | collective-permute-start | bytes 24584 | tf_op jit(solution)/shard_map/ppermute | solution.py:23
  36.6 1.3 %collective-permute-start.7 = (f32[1,2048]{1,0:T(1,128)S(1)}, f32[1,2048]{1,0:T(1,128)S(1)}, u32[]{:S(2)}, u32[]{:S(2)}) collective-permute-start(f32[1,2048]{1,0:T(1,128)S(1)} %get-tuple-element.16), channel_id=1, source_target_pairs={{8,0},{16,8},{24,16},{9,1},{17,9},{25,17},{10,2},{18,10},{26,18},{... | collective-permute-start | bytes 24584 | tf_op jit(solution)/shard_map/ppermute | solution.py:24
  37.9 2.8 %fusion.15 = (f32[256,2047]{1,0:T(8,128)}, f32[256,2047]{1,0:T(8,128)}) fusion(f32[256,2048]{1,0:T(8,128)S(1)} %get-tuple-element.11), kind=kLoop, calls=%fused_computation.39 | loop fusion | bytes 8384512 | tf_op jit(solution)/shard_map/slice | solution.py:52
  41.0 0.2 collective-permute-done.7
  41.2 8.2 %multiply_reduce_fusion.3 = (f32[]{:T(128)}, f32[]{:T(128)}, f32[]{:T(128)}, f32[]{:T(128)}, f32[256,2048]{1,0:T(8,128)}) fusion(f32[256,2048]{1,0:T(8,128)} %param.2, f32[256,2048]{1,0:T(8,128)S(1)} %fusion.12, f32[256,2048]{1,0:T(8,128)} %get-tuple-element.12, f32[256,2048]{1,0:T(8,128)} %copy-done, f32[1,2048]{1,0:T(1,128)S(1)} %collective-permute-done.7, ...), kind=kLoop, calls=%fused_computation.23 | loop fusion | flops 9961468 | bytes 18877456 | tf_op jit(solution)/shard_map/reduce_sum | solution.py:80
  49.3 2.6 %maximum_bitcast_fusion = f32[1,4]{1,0:T(1,128)S(1)} fusion(f32[1]{0:T(128)} %bitcast.7, f32[1]{0:T(128)} %bitcast.4, f32[1]{0:T(128)} %bitcast.3, f32[1]{0:T(128)} %bitcast), kind=kLoop, calls=%fused_computation.34 | loop fusion | flops 12 | bytes 32 | tf_op jit(solution)/shard_map/broadcast_in_dim | solution.py:57
  51.9 2.5 %collective-permute-start.8 = (f32[1,128]{1,0:T(1,128)S(1)}, f32[1,128]{1,0:T(1,128)S(1)}, u32[]{:S(2)}, u32[]{:S(2)}) collective-permute-start(f32[1,128]{1,0:T(1,128)S(1)} %pad.4), channel_id=1, source_target_pairs={{0,8},{8,0},{16,24},{24,16},{1,9},{9,1},{17,25},{25,17},{2,10},{10... | collective-permute-start | bytes 1544 | tf_op jit(solution)/shard_map/ppermute | solution.py:62
  54.4 0.8 collective-permute-done.8
  55.2 1.9 %collective-permute-start.9 = (f32[1,128]{1,0:T(1,128)S(1)}, f32[1,128]{1,0:T(1,128)S(1)}, u32[]{:S(2)}, u32[]{:S(2)}) collective-permute-start(f32[1,128]{1,0:T(1,128)S(1)} %pad_add_fusion), channel_id=1, source_target_pairs={{0,16},{8,24},{16,0},{24,8},{1,17},{9,25},{17,1},{25,9},{2,18},{10... | collective-permute-start | bytes 1544 | tf_op jit(solution)/shard_map/ppermute | solution.py:62
  57.2 1.6 %collective-permute-done.9 = f32[1,128]{1,0:T(1,128)S(1)} collective-permute-done((f32[1,128]{1,0:T(1,128)S(1)}, f32[1,128]{1,0:T(1,128)S(1)}, u32[]{:S(2)}, u32[]{:S(2)}) %collective-permute-start.9) | collective-permute-done | bytes 544 | tf_op jit(solution)/shard_map/ppermute | solution.py:62
  58.8 3.5 %collective-permute-done.10 = f32[1,128]{1,0:T(1,128)S(1)} collective-permute-done((f32[1,128]{1,0:T(1,128)S(1)}, f32[1,128]{1,0:T(1,128)S(1)}, u32[]{:S(2)}, u32[]{:S(2)}) %collective-permute-start.10) | collective-permute-done | bytes 544 | tf_op jit(solution)/shard_map/ppermute | solution.py:62
  62.3 3.5 %collective-permute-done.11 = f32[1,128]{1,0:T(1,128)S(1)} collective-permute-done((f32[1,128]{1,0:T(1,128)S(1)}, f32[1,128]{1,0:T(1,128)S(1)}, u32[]{:S(2)}, u32[]{:S(2)}) %collective-permute-start.11) | collective-permute-done | bytes 544 | tf_op jit(solution)/shard_map/ppermute | solution.py:62
  65.9 1.8 %collective-permute-start.12 = (f32[1,128]{1,0:T(1,128)S(1)}, f32[1,128]{1,0:T(1,128)S(1)}, u32[]{:S(2)}, u32[]{:S(2)}) collective-permute-start(f32[1,128]{1,0:T(1,128)S(1)} %add.155), channel_id=1, source_target_pairs={{0,4},{1,5},{2,6},{3,7},{4,0},{5,1},{6,2},{7,3},{8,12},{9,13},{10,... | collective-permute-start | bytes 1544 | tf_op jit(solution)/shard_map/ppermute | solution.py:62
  67.7 2.6 %collective-permute-done.12 = f32[1,128]{1,0:T(1,128)S(1)} collective-permute-done((f32[1,128]{1,0:T(1,128)S(1)}, f32[1,128]{1,0:T(1,128)S(1)}, u32[]{:S(2)}, u32[]{:S(2)}) %collective-permute-start.12) | collective-permute-done | bytes 544 | tf_op jit(solution)/shard_map/ppermute | solution.py:62
  70.3 0.6 fusion.21
  76.5 3.6 %multiply_subtract_fusion = f32[256,2048]{1,0:T(8,128)} fusion(f32[256,2048]{1,0:T(8,128)} %copy-done, f32[256,2048]{1,0:T(8,128)S(1)} %fusion.12, f32[]{:T(128)S(6)} %mul.186, f32[]{:T(128)S(6)} %add.160), kind=kLoop, calls=%fused_computation.19 | loop fusion | flops 1572864 | bytes 6291464 | tf_op jit(solution)/shard_map/sub | solution.py:92
  80.1 0.4 copy-done.5
  80.5 1.9 %multiply_add_fusion = f32[256,2048]{1,0:T(8,128)} fusion(f32[256,2048]{1,0:T(8,128)S(1)} %copy-done.5, f32[256,2048]{1,0:T(8,128)S(1)} %copy-done.2, f32[256,2048]{1,0:T(8,128)S(1)} %copy-done.3, f32[]{:T(128)S(6)} %mul.186, f32[]{:T(128)S(6)} %add.160), kind=kLoop, calls=%fused_computation.18 | loop fusion | flops 2097152 | bytes 8388616 | tf_op jit(solution)/shard_map/add | solution.py:92
  (36 shorter events, 0.8 us)
Async XLA Ops:
  0.6 1.6 %copy-start.1 = (f32[256,2048]{1,0:T(8,128)S(1)}, f32[256,2048]{1,0:T(8,128)}, u32[]{:S(2)}) copy-start(f32[256,2048]{1,0:T(8,128)} %param.2) | copy-start | bytes 6291460
  1.8 1.4 %copy-start.4 = (f32[2,128,16,128]{3,2,1,0:T(8,128)}, f32[2,128,16,128]{3,2,1,0:T(8,128)S(1)}, u32[]{:S(2)}) copy-start(f32[2,128,16,128]{3,2,1,0:T(8,128)S(1)} %broadcast_in_dim.27) | copy-start | bytes 6291460
  3.4 14.2 %collective-permute-start = (f32[1,256]{1,0:T(1,128)S(1)}, f32[1,256]{1,0:T(1,128)S(1)}, u32[]{:S(2)}, u32[]{:S(2)}) collective-permute-start(f32[1,256]{1,0:T(1,128)S(1)} %bitcast.35), channel_id=1, source_target_pairs={{1,0},{2,1},{3,2},{4,3},{5,4},{6,5},{7,6},{0,7},{9,8},{10,9},{11,1... | collective-permute-start | bytes 3080 | tf_op jit(solution)/shard_map/ppermute | solution.py:27
  9.5 8.0 %collective-permute-start.1 = (f32[1,256]{1,0:T(1,128)S(1)}, f32[1,256]{1,0:T(1,128)S(1)}, u32[]{:S(2)}, u32[]{:S(2)}) collective-permute-start(f32[1,256]{1,0:T(1,128)S(1)} %bitcast.37), channel_id=1, source_target_pairs={{0,1},{1,2},{2,3},{3,4},{4,5},{5,6},{6,7},{7,0},{8,9},{9,10},{10,1... | collective-permute-start | bytes 3080 | tf_op jit(solution)/shard_map/ppermute | solution.py:26
  9.5 8.3 %collective-permute-start.2 = (f32[1,2048]{1,0:T(1,128)S(1)}, f32[1,2048]{1,0:T(1,128)S(1)}, u32[]{:S(2)}, u32[]{:S(2)}) collective-permute-start(f32[1,2048]{1,0:T(1,128)S(1)} %get-tuple-element.21), channel_id=1, source_target_pairs={{0,8},{8,16},{16,24},{1,9},{9,17},{17,25},{2,10},{10,18},{18,26},{... | collective-permute-start | bytes 24584 | tf_op jit(solution)/shard_map/ppermute | solution.py:23
  11.0 6.8 %collective-permute-start.3 = (f32[1,2048]{1,0:T(1,128)S(1)}, f32[1,2048]{1,0:T(1,128)S(1)}, u32[]{:S(2)}, u32[]{:S(2)}) collective-permute-start(f32[1,2048]{1,0:T(1,128)S(1)} %get-tuple-element.22), channel_id=1, source_target_pairs={{8,0},{16,8},{24,16},{9,1},{17,9},{25,17},{10,2},{18,10},{26,18},{... | collective-permute-start | bytes 24584 | tf_op jit(solution)/shard_map/ppermute | solution.py:24
  24.8 13.0 %copy-start = (f32[256,2048]{1,0:T(8,128)}, f32[256,2048]{1,0:T(8,128)S(1)}, u32[]{:S(2)}) copy-start(f32[256,2048]{1,0:T(8,128)S(1)} %get-tuple-element.11) | copy-start | bytes 6291460
  27.6 13.3 %collective-permute-start.4 = (f32[1,256]{1,0:T(1,128)S(1)}, f32[1,256]{1,0:T(1,128)S(1)}, u32[]{:S(2)}, u32[]{:S(2)}) collective-permute-start(f32[1,256]{1,0:T(1,128)S(1)} %bitcast.36), channel_id=1, source_target_pairs={{1,0},{2,1},{3,2},{4,3},{5,4},{6,5},{7,6},{0,7},{9,8},{10,9},{11,1... | collective-permute-start | bytes 3080 | tf_op jit(solution)/shard_map/ppermute | solution.py:27
  32.1 8.6 %collective-permute-start.5 = (f32[1,256]{1,0:T(1,128)S(1)}, f32[1,256]{1,0:T(1,128)S(1)}, u32[]{:S(2)}, u32[]{:S(2)}) collective-permute-start(f32[1,256]{1,0:T(1,128)S(1)} %bitcast.38), channel_id=1, source_target_pairs={{0,1},{1,2},{2,3},{3,4},{4,5},{5,6},{6,7},{7,0},{8,9},{9,10},{10,1... | collective-permute-start | bytes 3080 | tf_op jit(solution)/shard_map/ppermute | solution.py:26
  32.1 8.9 %collective-permute-start.6 = (f32[1,2048]{1,0:T(1,128)S(1)}, f32[1,2048]{1,0:T(1,128)S(1)}, u32[]{:S(2)}, u32[]{:S(2)}) collective-permute-start(f32[1,2048]{1,0:T(1,128)S(1)} %get-tuple-element.15), channel_id=1, source_target_pairs={{0,8},{8,16},{16,24},{1,9},{9,17},{17,25},{2,10},{10,18},{18,26},{... | collective-permute-start | bytes 24584 | tf_op jit(solution)/shard_map/ppermute | solution.py:23
  36.6 4.6 %collective-permute-start.7 = (f32[1,2048]{1,0:T(1,128)S(1)}, f32[1,2048]{1,0:T(1,128)S(1)}, u32[]{:S(2)}, u32[]{:S(2)}) collective-permute-start(f32[1,2048]{1,0:T(1,128)S(1)} %get-tuple-element.16), channel_id=1, source_target_pairs={{8,0},{16,8},{24,16},{9,1},{17,9},{25,17},{10,2},{18,10},{26,18},{... | collective-permute-start | bytes 24584 | tf_op jit(solution)/shard_map/ppermute | solution.py:24
  51.9 3.3 %collective-permute-start.8 = (f32[1,128]{1,0:T(1,128)S(1)}, f32[1,128]{1,0:T(1,128)S(1)}, u32[]{:S(2)}, u32[]{:S(2)}) collective-permute-start(f32[1,128]{1,0:T(1,128)S(1)} %pad.4), channel_id=1, source_target_pairs={{0,8},{8,0},{16,24},{24,16},{1,9},{9,1},{17,25},{25,17},{2,10},{10... | collective-permute-start | bytes 1544 | tf_op jit(solution)/shard_map/ppermute | solution.py:62
  55.2 3.5 %collective-permute-start.9 = (f32[1,128]{1,0:T(1,128)S(1)}, f32[1,128]{1,0:T(1,128)S(1)}, u32[]{:S(2)}, u32[]{:S(2)}) collective-permute-start(f32[1,128]{1,0:T(1,128)S(1)} %pad_add_fusion), channel_id=1, source_target_pairs={{0,16},{8,24},{16,0},{24,8},{1,17},{9,25},{17,1},{25,9},{2,18},{10... | collective-permute-start | bytes 1544 | tf_op jit(solution)/shard_map/ppermute | solution.py:62
  58.8 3.5 %collective-permute-start.10 = (f32[1,128]{1,0:T(1,128)S(1)}, f32[1,128]{1,0:T(1,128)S(1)}, u32[]{:S(2)}, u32[]{:S(2)}) collective-permute-start(f32[1,128]{1,0:T(1,128)S(1)} %add.153), channel_id=1, source_target_pairs={{0,1},{1,0},{2,3},{3,2},{4,5},{5,4},{6,7},{7,6},{8,9},{9,8},{10,11... | collective-permute-start | bytes 1544 | tf_op jit(solution)/shard_map/ppermute | solution.py:62
  62.3 3.5 %collective-permute-start.11 = (f32[1,128]{1,0:T(1,128)S(1)}, f32[1,128]{1,0:T(1,128)S(1)}, u32[]{:S(2)}, u32[]{:S(2)}) collective-permute-start(f32[1,128]{1,0:T(1,128)S(1)} %add.154), channel_id=1, source_target_pairs={{0,2},{1,3},{2,0},{3,1},{4,6},{5,7},{6,4},{7,5},{8,10},{9,11},{10,... | collective-permute-start | bytes 1544 | tf_op jit(solution)/shard_map/ppermute | solution.py:62
  65.9 4.4 %collective-permute-start.12 = (f32[1,128]{1,0:T(1,128)S(1)}, f32[1,128]{1,0:T(1,128)S(1)}, u32[]{:S(2)}, u32[]{:S(2)}) collective-permute-start(f32[1,128]{1,0:T(1,128)S(1)} %add.155), channel_id=1, source_target_pairs={{0,4},{1,5},{2,6},{3,7},{4,0},{5,1},{6,2},{7,3},{8,12},{9,13},{10,... | collective-permute-start | bytes 1544 | tf_op jit(solution)/shard_map/ppermute | solution.py:62
  76.5 3.6 %copy-start.2 = (f32[256,2048]{1,0:T(8,128)S(1)}, f32[256,2048]{1,0:T(8,128)}, u32[]{:S(2)}) copy-start(f32[256,2048]{1,0:T(8,128)} %param.2) | copy-start | bytes 6291460
  76.5 3.6 %copy-start.3 = (f32[256,2048]{1,0:T(8,128)S(1)}, f32[256,2048]{1,0:T(8,128)}, u32[]{:S(2)}) copy-start(f32[256,2048]{1,0:T(8,128)} %get-tuple-element.12) | copy-start | bytes 6291460
  76.5 4.0 %copy-start.5 = (f32[256,2048]{1,0:T(8,128)S(1)}, f32[256,2048]{1,0:T(8,128)}, u32[]{:S(2)}) copy-start(f32[256,2048]{1,0:T(8,128)} %get-tuple-element.10) | copy-start | bytes 6291460

commit v2 on v0

v2 whole, which is shorter than its diff:
```python
import functools
import math

import jax
import jax.numpy as jnp
from jax import lax
from jax.experimental import pallas as pl
from jax.experimental.pallas import tpu as pltpu
from jax.sharding import PartitionSpec as P

ARC_SPAN = 2.0 * math.pi / 3.0
TILE = 128
SUB = 8
VMEM_SPEC = pl.BlockSpec(memory_space=pltpu.VMEM)
SMEM_SPEC = pl.BlockSpec(memory_space=pltpu.SMEM)
Z0, U0, V0, Z1, U1, V1, I0, I1 = range(8)
EAST_WEST, UPPER, LOWER, INNER = range(4)


def coefficient_table(total_rows):
    row_pos = jnp.arange(total_rows, dtype=jnp.int32).astype(jnp.float32)
    east_west = jnp.cos((row_pos + 0.5) / total_rows * ARC_SPAN - 0.5 * ARC_SPAN)
    upper = jnp.cos(row_pos / total_rows * ARC_SPAN - 0.5 * ARC_SPAN)
    lower = jnp.cos((row_pos + 1.0) / total_rows * ARC_SPAN - 0.5 * ARC_SPAN)
    inner = jnp.where(row_pos == total_rows - 1, 0.0, lower)
    zero = jnp.zeros_like(lower)
    return jnp.stack([east_west, upper, lower, inner, zero, zero, zero, zero])


def fold(row):
    total = row[:, :TILE]
    for start in range(TILE, row.shape[1], TILE):
        total = total + row[:, start : start + TILE]
    return total


def wide(cell, width=TILE):
    return jnp.broadcast_to(cell, (cell.shape[0], width))


def after(row):
    return pltpu.roll(row, row.shape[1] - 1, 1)


def before(row):
    return pltpu.roll(row, 1, 1)


def lane_ids(rows, width=TILE):
    return lax.broadcasted_iota(jnp.int32, (rows, width), 1)


def local_kernel(flags, tabs, src, z, u, w, v, pack, inv, ew_t, up_t, lo_t):
    rows, cols = src.shape
    tiles = cols // TILE
    blocks = TILE // SUB
    start = pl.multiple_of(lax.axis_index("lat") * rows, rows)
    band = jnp.transpose(tabs[:, pl.ds(start, rows)])
    ew = wide(band[:, EAST_WEST : EAST_WEST + 1])
    up = wide(band[:, UPPER : UPPER + 1])
    lo = wide(band[:, LOWER : LOWER + 1])
    ew_t[...] = ew
    up_t[...] = up
    lo_t[...] = lo
    for kind, screen in enumerate((0.05, 0.4, 2.0)):
        inv[kind] = 1.0 / (screen + 2.0 * ew + up + lo)
    nothing = jnp.zeros((SUB, cols), jnp.float32)
    for padded in (z, u):
        padded[:SUB] = nothing
        padded[rows + SUB :] = nothing
    zero = jnp.zeros((SUB, TILE), jnp.float32)
    row_id = lax.broadcasted_iota(jnp.int32, (SUB, TILE), 0)
    lane = lane_ids(SUB)
    kinds = [
        [
            jnp.where(flags[band_row, c] == 0, 0, jnp.where(flags[band_row, c] == 1, 1, 2))
            for c in range(tiles)
        ]
        for band_row in range(rows // TILE)
    ]

    def columns(c):
        return pl.ds(c * TILE, TILE)

    def around(field, at, c, here, west, east, coeffs):
        prev = field[pl.ds(at, SUB), columns(c)]
        later = field[pl.ds(at + 2 * SUB, SUB), columns(c)]
        above = pltpu.roll(jnp.where(row_id == SUB - 1, prev, here), 1, 0)
        below = pltpu.roll(jnp.where(row_id == 0, later, here), SUB - 1, 0)
        right = pltpu.roll(jnp.where(lane == 0, east, here), TILE - 1, 1)
        left = pltpu.roll(jnp.where(lane == TILE - 1, west, here), 1, 1)
        e, a, b = coeffs
        return e * (right + left) + a * above + b * below

    def sweep(body, count):
        sums = (zero,) * count
        for band_row in range(rows // TILE):

            def step(k, carry, band_row=band_row):
                at = pl.multiple_of(band_row * TILE + k * SUB, SUB)
                return body(at, kinds[band_row], carry)

            sums = lax.fori_loop(0, blocks, step, sums)
        return sums

    def first_pass(at, kind, carry):
        (m0,) = carry
        for c in range(tiles):
            b = src[pl.ds(at, SUB), columns(c)]
            value = b * inv[kind[c], pl.ds(at, SUB), :]
            z[pl.ds(at + SUB, SUB), columns(c)] = value
            m0 = m0 + b * value
        return (m0,)

    def second_pass(at, kind, carry):
        m1, m2 = carry
        here_rows = pl.ds(at, SUB)
        coeffs = ew_t[here_rows, :], up_t[here_rows, :], lo_t[here_rows, :]
        line = [zero] + [z[pl.ds(at + SUB, SUB), columns(c)] for c in range(tiles)] + [zero]
        for c in range(tiles):
            here = line[c + 1]
            near = around(z, at, c, here, line[c], line[c + 2], coeffs)
            image = src[here_rows, columns(c)] - near
            scaled = image * inv[kind[c], here_rows, :]
            w[here_rows, columns(c)] = image
            u[pl.ds(at + SUB, SUB), columns(c)] = scaled
            m1 = m1 + here * image
            m2 = m2 + scaled * image
        return m1, m2

    def third_pass(at, kind, carry):
        (m3,) = carry
        here_rows = pl.ds(at, SUB)
        coeffs = ew_t[here_rows, :], up_t[here_rows, :], lo_t[here_rows, :]
        line = [zero] + [u[pl.ds(at + SUB, SUB), columns(c)] for c in range(tiles)] + [zero]
        for c in range(tiles):
            here = line[c + 1]
            near = around(u, at, c, here, line[c], line[c + 2], coeffs)
            image = w[here_rows, columns(c)] - near
            v[here_rows, columns(c)] = image
            m3 = m3 + here * image
        return (m3,)

    (m0,) = sweep(first_pass, 1)
    m1, m2 = sweep(second_pass, 2)
    (m3,) = sweep(third_pass, 1)

    last = rows - 1
    pack[Z0 : Z0 + 1, :cols] = z[SUB : SUB + 1, :]
    pack[U0 : U0 + 1, :cols] = u[SUB : SUB + 1, :]
    pack[V0 : V0 + 1, :cols] = v[:1, :]
    pack[Z1 : Z1 + 1, :cols] = z[last + SUB : last + SUB + 1, :]
    pack[U1 : U1 + 1, :cols] = u[last + SUB : last + SUB + 1, :]
    pack[V1 : V1 + 1, :cols] = v[last:, :]
    for c in range(tiles):
        pack[I0 : I0 + 1, c * TILE : (c + 1) * TILE] = inv[kinds[0][c], :1, :]
        pack[I1 : I1 + 1, c * TILE : (c + 1) * TILE] = inv[kinds[-1][c], last:, :]

    for band_row in range(rows // TILE):
        here_rows = slice(band_row * TILE, (band_row + 1) * TILE)
        inner_rows = slice(band_row * TILE + SUB, (band_row + 1) * TILE + SUB)
        east = slice(cols - TILE, cols)
        ids = lane_ids(TILE)
        mix = inv[kinds[band_row][-1], here_rows, :]
        mix = jnp.where(ids == I0, inv[kinds[band_row][0], here_rows, :], mix)
        mix = jnp.where(ids == V1, pltpu.roll(v[here_rows, east], V1 + 1, 1), mix)
        mix = jnp.where(ids == U1, pltpu.roll(u[inner_rows, east], U1 + 1, 1), mix)
        mix = jnp.where(ids == Z1, pltpu.roll(z[inner_rows, east], Z1 + 1, 1), mix)
        mix = jnp.where(ids == V0, pltpu.roll(v[here_rows, :TILE], V0, 1), mix)
        mix = jnp.where(ids == U0, pltpu.roll(u[inner_rows, :TILE], U0, 1), mix)
        mix = jnp.where(ids == Z0, z[inner_rows, :TILE], mix)
        at = cols + band_row * TILE
        pack[:, at : at + TILE] = jnp.transpose(mix)[:SUB, :]

    at = cols + rows
    pack[:, at:] = zero
    for i, m in enumerate((m0, m1, m2, m3)):
        pack[i : i + 1, at:] = jnp.sum(m, axis=0, keepdims=True)


def sides(own, other, index, stage):
    size = 2**stage
    lower = lax.rem(lax.div(index, size), 2)
    inside = lax.rem(index, size)
    here, there = own[...], other[...]
    first = jnp.where(lower == 0, here, there)
    second = jnp.where(lower == 0, there, here)
    at_end = (lower == 0) & (inside == size - 1)
    at_start = (lower == 1) & (inside == 0)
    return first, second, at_end, at_start


def row_of(pack, i, start, stop):
    return pack[i : i + 1, start:stop]


def add_moments(out, at, first, second, changes):
    width = first.shape[1]
    out[:, at : at + TILE] = first[:, width - TILE :] + second[:, width - TILE :]
    for i, change in enumerate(changes):
        out[i + 1 : i + 2, at : at + TILE] += change


def lat_kernel(stage, final, cols, tabs, own, other, ext_in, out, ext):
    height = own.shape[1] - cols - TILE
    index = lax.axis_index("lat")
    top, bottom, at_end, at_start = sides(own, other, index, stage)
    size = 2**stage
    border = pl.multiple_of((lax.div(index, 2 * size) * 2 * size + size) * (height // size), TILE)
    low = tabs[:, pl.ds(border, TILE)]
    high = tabs[:, pl.ds(border - TILE, TILE)]
    cross = wide(low[UPPER : UPPER + 1, :1], cols)
    ew_b = wide(low[EAST_WEST : EAST_WEST + 1, :1])
    ew_t = wide(high[EAST_WEST : EAST_WEST + 1, TILE - 1 :])
    next_b = wide(low[LOWER : LOWER + 1, :1])
    next_t = wide(high[UPPER : UPPER + 1, TILE - 1 :])

    zt, ut, vt, it = (row_of(top, i, 0, cols) for i in (Z1, U1, V1, I1))
    zb, ub, vb, ib = (row_of(bottom, i, 0, cols) for i in (Z0, U0, V0, I0))
    et, eb = -cross * zb, -cross * zt
    dt, db = it * et, ib * eb
    full_t, full_b = ut + dt, ub + db
    inside = lane_ids(1, cols) < cols - 1
    pair_t = jnp.where(inside, dt * after(dt), 0.0)
    pair_b = jnp.where(inside, db * after(db), 0.0)
    twice = fold(zt * et)
    second = fold((2.0 * ut + dt) * et + (2.0 * ub + db) * eb)
    third = fold(dt * (2.0 * vt + et) + db * (2.0 * vb + eb) - 2.0 * cross * full_t * full_b)
    third = third - 2.0 * (ew_t * fold(pair_t) + ew_b * fold(pair_b))

    base = 0 if final else cols
    if not final:
        top_rows = (lax.broadcasted_iota(jnp.int32, (SUB, cols), 0) < Z1) | (
            lax.broadcasted_iota(jnp.int32, (SUB, cols), 0) == I0
        )
        out[:, :cols] = jnp.where(top_rows, top[:, :cols], bottom[:, :cols])
    out[:, base : base + height] = top[:, cols : cols + height]
    out[:, base + height : base + 2 * height] = bottom[:, cols : cols + height]
    add_moments(out, base + 2 * height, top, bottom, (2.0 * twice, second, third))

    lane = lane_ids(1)
    upper_at = base + height - TILE
    lower_at = base + height
    c = cross[:, :TILE]
    for edge, inner, u_row, v_row in ((0, 1, U0, V0), (cols - 1, cols - 2, U1, V1)):

        def pick(row, place):
            return wide(row[:, place : place + 1])

        d_top, d_bottom = pick(dt, edge), pick(db, edge)
        v_top = pick(et, edge) - ew_t * pick(dt, inner) - c * pick(full_b, edge)
        v_bottom = pick(eb, edge) - ew_b * pick(db, inner) - c * pick(full_t, edge)
        out[u_row : u_row + 1, upper_at : upper_at + TILE] += jnp.where(
            lane == TILE - 1, d_top, 0.0
        )
        out[u_row : u_row + 1, lower_at : lower_at + TILE] += jnp.where(lane == 0, d_bottom, 0.0)
        out[v_row : v_row + 1, upper_at : upper_at + TILE] += jnp.where(
            lane == TILE - 1, v_top, jnp.where(lane == TILE - 2, -next_t * d_top, 0.0)
        )
        out[v_row : v_row + 1, lower_at : lower_at + TILE] += jnp.where(
            lane == 0, v_bottom, jnp.where(lane == 1, -next_b * d_bottom, 0.0)
        )

    if stage == 0:
        ext[...] = jnp.zeros((SUB, cols), jnp.float32)
    else:
        ext[...] = ext_in[...]

    @pl.when(at_start)
    def _():
        ext[0:1, :] = zt
        ext[1:2, :] = full_t
        ext[2:3, :] = it

    @pl.when(at_end)
    def _():
        ext[3:4, :] = zb
        ext[4:5, :] = full_b
        ext[5:6, :] = ib


def column_border(west, east, tabs):
    height = west.shape[1] - TILE
    zw, uw, vw, iw = (row_of(west, i, 0, height) for i in (Z1, U1, V1, I1))
    ze, ue, ve, ie = (row_of(east, i, 0, height) for i in (Z0, U0, V0, I0))
    ew = tabs[EAST_WEST : EAST_WEST + 1, :]
    inner = tabs[INNER : INNER + 1, :]
    to_w, to_e = -ew * ze, -ew * zw
    dw, de = iw * to_w, ie * to_e
    full_w, full_e = uw + dw, ue + de
    first = 2.0 * fold(zw * to_w)
    second = fold((2.0 * uw + dw) * to_w + (2.0 * ue + de) * to_e)
    third = fold(
        dw * (2.0 * vw + to_w)
        + de * (2.0 * ve + to_e)
        - 2.0 * inner * (dw * after(dw) + de * after(de))
        - 2.0 * ew * full_w * full_e
    )
    return (first, second, third), (zw, full_w), (ze, full_e)


def lon_kernel(stage, tabs, own, other, ext_in, out, ext):
    height = own.shape[1] - TILE
    west, east, at_end, at_start = sides(own, other, lax.axis_index("lon"), stage)
    changes, from_west, from_east = column_border(west, east, tabs)
    ids = lax.broadcasted_iota(jnp.int32, (SUB, height), 0)
    out[:, :height] = jnp.where((ids < Z1) | (ids == I0), west[:, :height], east[:, :height])
    add_moments(out, height, west, east, changes)
    if stage == 0:
        ext[...] = jnp.zeros((SUB, height), jnp.float32)
    else:
        ext[...] = ext_in[...]

    @pl.when(at_start)
    def _():
        ext[0:1, :], ext[1:2, :] = from_west

    @pl.when(at_end)
    def _():
        ext[2:3, :], ext[3:4, :] = from_east


def last_kernel(
    stage, chunk, tabs, own, other, ext_in, edges, row_ext, src, z, u, w, v,
    out_x, out_r, mom, ext, field_x, field_r, cols_t, sems,
):
    rows, cols = src.shape
    height = own.shape[1] - TILE
    tiles = cols // TILE
    sectors = lax.axis_size("lon")
    index = lax.axis_index("lon")
    west, east, at_end, at_start = sides(own, other, index, stage)
    changes, from_west, from_east = column_border(west, east, tabs)
    wrap, round_west, round_east = column_border(east, west, tabs)
    add_moments(mom, 0, west, east, [a + b for a, b in zip(changes, wrap)])
    if stage == 0:
        ext[...] = jnp.zeros((SUB, height), jnp.float32)
    else:
        ext[...] = ext_in[...]

    @pl.when(at_start)
    def _():
        ext[0:1, :], ext[1:2, :] = from_west

    @pl.when(at_end)
    def _():
        ext[2:3, :], ext[3:4, :] = from_east

    @pl.when(index == 0)
    def _():
        ext[0:1, :], ext[1:2, :] = round_west

    @pl.when(index == sectors - 1)
    def _():
        ext[2:3, :], ext[3:4, :] = round_east

    sums = jnp.broadcast_to(jnp.sum(mom[...], axis=1, keepdims=True), (SUB, TILE))
    m0, m1, m2, m3 = (sums[i : i + 1, :] for i in range(4))
    alpha = m0 / m1
    fresh = alpha * alpha * m2 - 2.0 * alpha * m1 + m0
    grow = 1.0 + fresh / m0
    bend = grow * grow * m1 - 2.0 * grow * alpha * m2 + alpha * alpha * m3
    beta = fresh / bend
    near1, far1 = alpha + beta * grow, alpha * beta
    near = jnp.broadcast_to(near1, (SUB, TILE))
    far = jnp.broadcast_to(far1, (SUB, TILE))

    lat = lax.axis_index("lat")
    start = pl.multiple_of(lat * rows, rows)
    here = pl.ds(start, rows)
    ew = tabs[EAST_WEST : EAST_WEST + 1, here]
    up = tabs[UPPER : UPPER + 1, here]
    lo = tabs[LOWER : LOWER + 1, here]
    row_lane = lane_ids(1, rows)
    near_r = jnp.concatenate([near1] * (rows // TILE), axis=1)
    far_r = jnp.concatenate([far1] * (rows // TILE), axis=1)
    mods = []
    for z_row, inv_row in ((0, I0), (2, I1)):
        e = -ew * ext[z_row : z_row + 1, here]
        d = edges[inv_row : inv_row + 1, cols : cols + rows] * e
        above = jnp.where(row_lane == 0, 0.0, before(d))
        below = jnp.where(row_lane == rows - 1, 0.0, after(d))
        dv = e - up * above - lo * below - ew * ext[z_row + 1 : z_row + 2, here]
        mods += [-far_r * d, far_r * dv - near_r * e, -far_r * ew * d]
    mods += [jnp.zeros((1, rows), jnp.float32)] * 2
    cols_t[...] = jnp.transpose(jnp.concatenate(mods, axis=0))

    near_c = jnp.concatenate([near1] * tiles, axis=1)
    far_c = jnp.concatenate([far1] * tiles, axis=1)
    col_lane = lane_ids(1, cols)
    first = tabs[:, pl.ds(start, TILE)]
    final = tabs[:, pl.ds(start + rows - TILE, TILE)]
    clamp_n = pl.multiple_of(jnp.maximum(start - TILE, 0), TILE)
    clamp_s = pl.multiple_of(jnp.minimum(start + rows, height - TILE), TILE)
    tab_n, tab_s = tabs[:, pl.ds(clamp_n, TILE)], tabs[:, pl.ds(clamp_s, TILE)]
    ext_n, ext_s = ext[:, pl.ds(clamp_n, TILE)], ext[:, pl.ds(clamp_s, TILE)]
    row_mods = []
    for which in range(2):
        at = 3 * which
        if which == 0:
            lane = 0
            own_tab, next_tab, next_ext, next_lane = first, tab_n, ext_n, TILE - 1
            cross_row, inner_row, inv_row = UPPER, LOWER, I0
        else:
            lane = TILE - 1
            own_tab, next_tab, next_ext, next_lane = final, tab_s, ext_s, 0
            cross_row, inner_row, inv_row = LOWER, UPPER, I1

        def scalar(tab, row, place):
            return wide(tab[row : row + 1, place : place + 1], cols)

        cross = scalar(own_tab, cross_row, lane)
        inner = scalar(own_tab, inner_row, lane)
        ew_own = scalar(own_tab, EAST_WEST, lane)
        ew_next = scalar(next_tab, EAST_WEST, next_lane)
        z_next = row_ext[at : at + 1, :]
        u_next = row_ext[at + 1 : at + 2, :]
        i_next = row_ext[at + 2 : at + 3, :]
        corner = jnp.where(col_lane == 0, scalar(next_ext, 0, next_lane), 0.0)
        corner = jnp.where(col_lane == cols - 1, scalar(next_ext, 2, next_lane), corner)
        u_next = u_next - i_next * ew_next * corner
        e = -cross * z_next
        d = edges[inv_row : inv_row + 1, :cols] * e
        right = jnp.where(col_lane == cols - 1, 0.0, after(d))
        left = jnp.where(col_lane == 0, 0.0, before(d))
        dv = e - ew_own * (right + left) - cross * u_next
        row_mods.append((-far_c * d, far_c * dv - near_c * e, -far_c * inner * d))

    lane = lane_ids(SUB)
    blocks = chunk // SUB

    def copies(i):
        part = pl.ds(pl.multiple_of(i * chunk, SUB), chunk)
        return (
            pltpu.make_async_copy(field_x.at[part, :], out_x.at[part, :], sems.at[0]),
            pltpu.make_async_copy(field_r.at[part, :], out_r.at[part, :], sems.at[1]),
        )

    def step(k, carry):
        at = pl.multiple_of(k * SUB, SUB)
        here = pl.ds(at, SUB)
        lines = cols_t[here, :]
        for c in range(tiles):
            part = pl.ds(c * TILE, TILE)
            x = near * z[pl.ds(at + SUB, SUB), part] - far * u[pl.ds(at + SUB, SUB), part]
            r = src[here, part] - near * w[here, part] + far * v[here, part]
            if c == 0:
                x = x + jnp.where(lane == 0, wide(lines[:, 0:1]), 0.0)
                r = r + jnp.where(
                    lane == 0, wide(lines[:, 1:2]), jnp.where(lane == 1, wide(lines[:, 2:3]), 0.0)
                )
            if c == tiles - 1:
                x = x + jnp.where(lane == TILE - 1, wide(lines[:, 3:4]), 0.0)
                r = r + jnp.where(
                    lane == TILE - 1,
                    wide(lines[:, 4:5]),
                    jnp.where(lane == TILE - 2, wide(lines[:, 5:6]), 0.0),
                )
            field_x[here, part] = x
            field_r[here, part] = r
        return carry

    parts = rows // chunk
    for i in range(parts):
        lax.fori_loop(i * blocks, (i + 1) * blocks, step, 0)
        if i == 0:
            dx, dr, dr_next = row_mods[0]
            field_x[0:1, :] += dx
            field_r[0:1, :] += dr
            field_r[1:2, :] += dr_next
        if i == parts - 1:
            dx, dr, dr_next = row_mods[1]
            field_x[rows - 1 : rows, :] += dx
            field_r[rows - 1 : rows, :] += dr
            field_r[rows - 2 : rows - 1, :] += dr_next
        for copy in copies(i):
            copy.start()
    for i in range(parts):
        for copy in copies(i):
            copy.wait()


def shape(*dims):
    return jax.ShapeDtypeStruct(dims, jnp.float32)


def call(kernel, name, out_shape, n_in, smem=0, out_specs=None, scratch=(), limit=32):
    return pl.pallas_call(
        kernel,
        name=name,
        out_shape=out_shape,
        in_specs=[SMEM_SPEC] * smem + [VMEM_SPEC] * (n_in - smem),
        out_specs=out_specs or [VMEM_SPEC] * len(out_shape),
        scratch_shapes=list(scratch),
        compiler_params=pltpu.CompilerParams(vmem_limit_bytes=limit << 20),
    )


def per_device(source, flags):
    rows, cols = source.shape
    bands, sectors = lax.axis_size("lat"), lax.axis_size("lon")
    height = rows * bands
    tabs = coefficient_table(height)
    z, u, w, v, edges = call(
        local_kernel,
        "local",
        [
            shape(rows + 2 * SUB, cols),
            shape(rows + 2 * SUB, cols),
            shape(rows, cols),
            shape(rows, cols),
            shape(SUB, cols + rows + TILE),
        ],
        3,
        smem=1,
        scratch=[pltpu.VMEM((3, rows, TILE), jnp.float32)]
        + [pltpu.VMEM((rows, TILE), jnp.float32)] * 3,
    )(flags, tabs, source)

    def swap(pack, axis, stage):
        count = lax.axis_size(axis)
        return lax.ppermute(pack, axis, [(i, i ^ (1 << stage)) for i in range(count)])

    lat_stages = bands.bit_length() - 1
    lon_stages = sectors.bit_length() - 1
    pack, row_ext = edges, edges
    for stage in range(lat_stages):
        final = stage == lat_stages - 1
        tall = (rows << (stage + 1)) + TILE + (0 if final else cols)
        pack, row_ext = call(
            functools.partial(lat_kernel, stage, final, cols),
            f"lat_merge{stage}",
            [shape(SUB, tall), shape(SUB, cols)],
            4,
        )(tabs, pack, swap(pack, "lat", stage), row_ext)
    col_ext = pack
    for stage in range(lon_stages - 1):
        pack, col_ext = call(
            functools.partial(lon_kernel, stage),
            f"lon_merge{stage}",
            [shape(SUB, height + TILE), shape(SUB, height)],
            4,
        )(tabs, pack, swap(pack, "lon", stage), col_ext)
    stage = lon_stages - 1
    any_spec = pl.BlockSpec(memory_space=pl.ANY)
    x, r = call(
        functools.partial(last_kernel, stage, 32),
        "combine",
        [shape(rows, cols), shape(rows, cols)],
        11,
        out_specs=[any_spec, any_spec],
        scratch=[
            pltpu.VMEM((SUB, TILE), jnp.float32),
            pltpu.VMEM((SUB, height), jnp.float32),
            pltpu.VMEM((rows, cols), jnp.float32),
            pltpu.VMEM((rows, cols), jnp.float32),
            pltpu.VMEM((rows, SUB), jnp.float32),
            pltpu.SemaphoreType.DMA((2,)),
        ],
    )(tabs, pack, swap(pack, "lon", stage), col_ext, edges, row_ext, source, z, u, w, v)
    return x, r


def solution(mesh):
    in_specs = (P("lat", "lon"), P("lat", "lon"))
    out_specs = (P("lat", "lon"), P("lat", "lon"))
    return jax.shard_map(
        per_device, mesh=mesh, in_specs=in_specs, out_specs=out_specs, check_vma=False
    )
```

time: 184 us -> 37.5 us (0.20)
  blocking collectives: 119 us -> 0 us
  other arithmetic: 25.7 us -> 0.37 us
  Pallas kernels: 0 us -> 13.7 us
  waiting for transfers between devices: 16.6 us -> 10 us
  starting transfers between devices: 15.3 us -> 10.3 us
  between operations: 4.68 us -> 0.68 us
    psum x3 -> x0, blocking collectives: 119 us -> none  [classic_total(): return lax.psum(jnp.sum(left * right), ('lat', 'lon'))]
    reduce_sum x3 -> x0, other arithmetic: 14.9 us -> none  [classic_total(): return lax.psum(jnp.sum(left * right), ('lat', 'lon'))]
    pallas_call x0 -> x6, Pallas kernels: none -> 13.7 us  [the longest x1 9.08 us: per_device(): call(local_kernel, 'local', [shape(rows + 2 * SUB, cols), shape(rows + 2...]
    add x2 -> x0, other arithmetic: 7.38 us -> none  [the longest x1 4.19 us: per_device(): solution = solution + alpha * search]
    ppermute x8 -> x5, waiting for transfers between devices: 16.6 us -> 10 us  [swap(): return lax.ppermute(pack, axis, [(i, i ^ 1 << stage) for i in range(count)])]
    ppermute x8 -> x5, starting transfers between devices: 15.3 us -> 10.3 us  [swap(): return lax.ppermute(pack, axis, [(i, i ^ 1 << stage) for i in range(count)])]
  transfers between devices with their start and end apart: 8 -> 5, of which waited for: 4 -> 5; matrix products, arithmetic and copies ran while one was open for 0% -> 0% of each run, Pallas kernels for 0% -> 0%
where the time goes in v2:
time: 37.5 us; the launch traced here: 37.4 us
  Pallas kernels  13.7 us (37%)
  starting transfers between devices  10.3 us (27%)
  waiting for transfers between devices  10 us (27%)
  local copies, waits for them, and re-layouts  2.32 us (6%)
  between operations  0.68 us (2%)
    ppermute x5, starting transfers between devices, swap(): return lax.ppermute(pack, axis, [(i, i ^ 1 << stage) for i in range(count)])  10.3 us
    ppermute x5, waiting for transfers between devices, swap(): return lax.ppermute(pack, axis, [(i, i ^ 1 << stage) for i in range(count)])  10 us
    pallas_call x1, Pallas kernels, per_device(): call(local_kernel, 'local', [shape(rows + 2 * SUB, cols), shape(rows + 2...  9.08 us
    pallas_call x1, Pallas kernels, per_device(): call(functools.partial(last_kernel, stage, 32), 'combine', [shape(rows, c...  3.84 us
    unnamed x6, local copies, waits for them, and re-layouts  2.27 us
  transfers between devices with their start and end apart: 5, of which 5 were waited for; matrix products, arithmetic and copies ran while one was open for 0% of the time, Pallas kernels for 0%

profile of v2, /device:TPU:0, one launch (start us, length us, event | category | flops | bytes accessed | tf_op | source)
XLA Modules:
  0.0 37.4 jit_solution(2775146346392019048)
XLA Ops:
  0.6 0.2 add_cosine_fusion.1
  0.9 0.1 compare_select_fusion
  1.1 0.0 copy-start
  1.1 1.6 %copy-done = f32[256,2048]{1,0:T(8,128)S(1)} copy-done((f32[256,2048]{1,0:T(8,128)S(1)}, f32[256,2048]{1,0:T(8,128)}, u32[]{:S(2)}) %copy-start) | copy-done | bytes 2097176
  2.7 0.0 copy-start.2
  2.7 0.7 %copy-done.2 = s32[2,16]{1,0:T(2,128)S(1)} copy-done((s32[2,16]{1,0:T(2,128)S(1)}, s32[2,16]{1,0:T(2,128)}, u32[]{:S(2)}) %copy-start.2) | copy-done | bytes 152
  3.3 0.0 copy-start.1
  3.3 9.1 %local.1 = (f32[272,2048]{1,0:T(8,128)S(1)}, f32[272,2048]{1,0:T(8,128)S(1)}, f32[256,2048]{1,0:T(8,128)S(1)}, f32[256,2048]{1,0:T(8,128)S(1)}, f32[8,2432]{1,0:T(8,128)S(1)}) custom-call(s32[2,16]{1,0:T(2,128)S(1)} %copy-done.2, f32[8,1024]{1,0:T(8,128)S(1)} %stack.5.tabs, f32[256,2048]{1,0:T(8,128)S(1)} %copy-done), custom_call_target="tpu_custom_call" | custom-call | tf_op jit(solution)/shard_map/local/pallas_call | solution.py:504
  12.4 0.5 %collective-permute-start = (f32[8,2432]{1,0:T(8,128)S(1)}, f32[8,2432]{1,0:T(8,128)S(1)}, u32[]{:S(2)}, u32[]{:S(2)}) collective-permute-start(f32[8,2432]{1,0:T(8,128)S(1)} %get-tuple-element.15.own.ext_in.edges), channel_id=1, source_target_pairs={{0,8},{8,0},{16,24},{24,16},{1,9},{9,1},{17,25},{25,17},{2,10},{10... | collective-permute-start | bytes 233480 | tf_op jit(solution)/shard_map/ppermute | solution.py:522
  12.9 0.9 %collective-permute-done.other = f32[8,2432]{1,0:T(8,128)S(1)} collective-permute-done((f32[8,2432]{1,0:T(8,128)S(1)}, f32[8,2432]{1,0:T(8,128)S(1)}, u32[]{:S(2)}, u32[]{:S(2)}) %collective-permute-start) | collective-permute-done | bytes 77856 | tf_op jit(solution)/shard_map/ppermute | solution.py:522
  13.8 0.3 lat_merge0.1
  14.1 2.9 %collective-permute-start.1 = (f32[8,2688]{1,0:T(8,128)S(1)}, f32[8,2688]{1,0:T(8,128)S(1)}, u32[]{:S(2)}, u32[]{:S(2)}) collective-permute-start(f32[8,2688]{1,0:T(8,128)S(1)} %get-tuple-element.16.own), channel_id=1, source_target_pairs={{0,16},{8,24},{16,0},{24,8},{1,17},{9,25},{17,1},{25,9},{2,18},{10... | collective-permute-start | bytes 258056 | tf_op jit(solution)/shard_map/ppermute | solution.py:522
  17.0 2.9 %collective-permute-done.1.other = f32[8,2688]{1,0:T(8,128)S(1)} collective-permute-done((f32[8,2688]{1,0:T(8,128)S(1)}, f32[8,2688]{1,0:T(8,128)S(1)}, u32[]{:S(2)}, u32[]{:S(2)}) %collective-permute-start.1) | collective-permute-done | bytes 86048 | tf_op jit(solution)/shard_map/ppermute | solution.py:522
  19.8 0.2 lat_merge1.1
  20.1 1.8 %collective-permute-start.2 = (f32[8,1152]{1,0:T(8,128)S(1)}, f32[8,1152]{1,0:T(8,128)S(1)}, u32[]{:S(2)}, u32[]{:S(2)}) collective-permute-start(f32[8,1152]{1,0:T(8,128)S(1)} %get-tuple-element.18.own.ext_in), channel_id=1, source_target_pairs={{0,1},{1,0},{2,3},{3,2},{4,5},{5,4},{6,7},{7,6},{8,9},{9,8},{10,11... | collective-permute-start | bytes 110600 | tf_op jit(solution)/shard_map/ppermute | solution.py:522
  21.9 2.2 %collective-permute-done.2.other = f32[8,1152]{1,0:T(8,128)S(1)} collective-permute-done((f32[8,1152]{1,0:T(8,128)S(1)}, f32[8,1152]{1,0:T(8,128)S(1)}, u32[]{:S(2)}, u32[]{:S(2)}) %collective-permute-start.2) | collective-permute-done | bytes 36896 | tf_op jit(solution)/shard_map/ppermute | solution.py:522
  24.1 0.1 lon_merge0.1
  24.3 1.9 %collective-permute-start.3 = (f32[8,1152]{1,0:T(8,128)S(1)}, f32[8,1152]{1,0:T(8,128)S(1)}, u32[]{:S(2)}, u32[]{:S(2)}) collective-permute-start(f32[8,1152]{1,0:T(8,128)S(1)} %get-tuple-element.19.own), channel_id=1, source_target_pairs={{0,2},{1,3},{2,0},{3,1},{4,6},{5,7},{6,4},{7,5},{8,10},{9,11},{10,... | collective-permute-start | bytes 110600 | tf_op jit(solution)/shard_map/ppermute | solution.py:522
  26.1 2.1 %collective-permute-done.3.other = f32[8,1152]{1,0:T(8,128)S(1)} collective-permute-done((f32[8,1152]{1,0:T(8,128)S(1)}, f32[8,1152]{1,0:T(8,128)S(1)}, u32[]{:S(2)}, u32[]{:S(2)}) %collective-permute-start.3) | collective-permute-done | bytes 36896 | tf_op jit(solution)/shard_map/ppermute | solution.py:522
  28.3 0.1 lon_merge1.1
  28.4 3.2 %collective-permute-start.4 = (f32[8,1152]{1,0:T(8,128)S(1)}, f32[8,1152]{1,0:T(8,128)S(1)}, u32[]{:S(2)}, u32[]{:S(2)}) collective-permute-start(f32[8,1152]{1,0:T(8,128)S(1)} %get-tuple-element.21.own), channel_id=1, source_target_pairs={{0,4},{1,5},{2,6},{3,7},{4,0},{5,1},{6,2},{7,3},{8,12},{9,13},{10,... | collective-permute-start | bytes 110600 | tf_op jit(solution)/shard_map/ppermute | solution.py:522
  31.6 1.9 %collective-permute-done.4.other = f32[8,1152]{1,0:T(8,128)S(1)} collective-permute-done((f32[8,1152]{1,0:T(8,128)S(1)}, f32[8,1152]{1,0:T(8,128)S(1)}, u32[]{:S(2)}, u32[]{:S(2)}) %collective-permute-start.4) | collective-permute-done | bytes 36896 | tf_op jit(solution)/shard_map/ppermute | solution.py:522
  33.5 0.0 copy-done.1
  33.5 3.8 %combine.1 = (f32[256,2048]{1,0:T(8,128)}, f32[256,2048]{1,0:T(8,128)}) custom-call(f32[8,1024]{1,0:T(8,128)S(1)} %stack.5.tabs, f32[8,1152]{1,0:T(8,128)S(1)} %get-tuple-element.21.own, f32[8,1152]{1,0:T(8,128)S(1)} %collective-permute-done.4.other, f32[8,1024]{1,0:T(8,128)S(1)} %get-tuple-element.22.ext_in, ...), custom_call_target="tpu_custom_call" | custom-call | tf_op jit(solution)/shard_map/combine/pallas_call | solution.py:546
  (2 shorter events, 0.0 us)
Async XLA Ops:
  1.1 1.6 %copy-start = (f32[256,2048]{1,0:T(8,128)S(1)}, f32[256,2048]{1,0:T(8,128)}, u32[]{:S(2)}) copy-start(f32[256,2048]{1,0:T(8,128)} %src.3) | copy-start | bytes 6291460
  2.7 0.7 %copy-start.2 = (s32[2,16]{1,0:T(2,128)S(1)}, s32[2,16]{1,0:T(2,128)}, u32[]{:S(2)}) copy-start(s32[2,16]{1,0:T(2,128)} %flags.1) | copy-start | bytes 388
  3.3 30.2 %copy-start.1 = (f32[256,2048]{1,0:T(8,128)S(1)}, f32[256,2048]{1,0:T(8,128)}, u32[]{:S(2)}) copy-start(f32[256,2048]{1,0:T(8,128)} %src.3) | copy-start | bytes 6291460
  12.4 1.4 %collective-permute-start = (f32[8,2432]{1,0:T(8,128)S(1)}, f32[8,2432]{1,0:T(8,128)S(1)}, u32[]{:S(2)}, u32[]{:S(2)}) collective-permute-start(f32[8,2432]{1,0:T(8,128)S(1)} %get-tuple-element.15.own.ext_in.edges), channel_id=1, source_target_pairs={{0,8},{8,0},{16,24},{24,16},{1,9},{9,1},{17,25},{25,17},{2,10},{10... | collective-permute-start | bytes 233480 | tf_op jit(solution)/shard_map/ppermute | solution.py:522
  14.1 5.8 %collective-permute-start.1 = (f32[8,2688]{1,0:T(8,128)S(1)}, f32[8,2688]{1,0:T(8,128)S(1)}, u32[]{:S(2)}, u32[]{:S(2)}) collective-permute-start(f32[8,2688]{1,0:T(8,128)S(1)} %get-tuple-element.16.own), channel_id=1, source_target_pairs={{0,16},{8,24},{16,0},{24,8},{1,17},{9,25},{17,1},{25,9},{2,18},{10... | collective-permute-start | bytes 258056 | tf_op jit(solution)/shard_map/ppermute | solution.py:522
  20.1 4.0 %collective-permute-start.2 = (f32[8,1152]{1,0:T(8,128)S(1)}, f32[8,1152]{1,0:T(8,128)S(1)}, u32[]{:S(2)}, u32[]{:S(2)}) collective-permute-start(f32[8,1152]{1,0:T(8,128)S(1)} %get-tuple-element.18.own.ext_in), channel_id=1, source_target_pairs={{0,1},{1,0},{2,3},{3,2},{4,5},{5,4},{6,7},{7,6},{8,9},{9,8},{10,11... | collective-permute-start | bytes 110600 | tf_op jit(solution)/shard_map/ppermute | solution.py:522
  24.3 4.0 %collective-permute-start.3 = (f32[8,1152]{1,0:T(8,128)S(1)}, f32[8,1152]{1,0:T(8,128)S(1)}, u32[]{:S(2)}, u32[]{:S(2)}) collective-permute-start(f32[8,1152]{1,0:T(8,128)S(1)} %get-tuple-element.19.own), channel_id=1, source_target_pairs={{0,2},{1,3},{2,0},{3,1},{4,6},{5,7},{6,4},{7,5},{8,10},{9,11},{10,... | collective-permute-start | bytes 110600 | tf_op jit(solution)/shard_map/ppermute | solution.py:522
  28.4 5.1 %collective-permute-start.4 = (f32[8,1152]{1,0:T(8,128)S(1)}, f32[8,1152]{1,0:T(8,128)S(1)}, u32[]{:S(2)}, u32[]{:S(2)}) collective-permute-start(f32[8,1152]{1,0:T(8,128)S(1)} %get-tuple-element.21.own), channel_id=1, source_target_pairs={{0,4},{1,5},{2,6},{3,7},{4,0},{5,1},{6,2},{7,3},{8,12},{9,13},{10,... | collective-permute-start | bytes 110600 | tf_op jit(solution)/shard_map/ppermute | solution.py:522

commit v3 on v2

--- a/solution.py
+++ b/solution.py
@@ -12,19 +12,18 @@
 TILE = 128
 SUB = 8
 VMEM_SPEC = pl.BlockSpec(memory_space=pltpu.VMEM)
-SMEM_SPEC = pl.BlockSpec(memory_space=pltpu.SMEM)
+HBM_SPEC = pl.BlockSpec(memory_space=pltpu.HBM)
+LOADS = 4
 Z0, U0, V0, Z1, U1, V1, I0, I1 = range(8)
 EAST_WEST, UPPER, LOWER, INNER = range(4)
 
 
 def coefficient_table(total_rows):
-    row_pos = jnp.arange(total_rows, dtype=jnp.int32).astype(jnp.float32)
-    east_west = jnp.cos((row_pos + 0.5) / total_rows * ARC_SPAN - 0.5 * ARC_SPAN)
-    upper = jnp.cos(row_pos / total_rows * ARC_SPAN - 0.5 * ARC_SPAN)
-    lower = jnp.cos((row_pos + 1.0) / total_rows * ARC_SPAN - 0.5 * ARC_SPAN)
-    inner = jnp.where(row_pos == total_rows - 1, 0.0, lower)
-    zero = jnp.zeros_like(lower)
-    return jnp.stack([east_west, upper, lower, inner, zero, zero, zero, zero])
+    row_pos = lax.broadcasted_iota(jnp.int32, (SUB, total_rows), 1).astype(jnp.float32)
+    kind = lax.broadcasted_iota(jnp.int32, (SUB, total_rows), 0)
+    ahead = jnp.where(kind == EAST_WEST, 0.5, jnp.where(kind == UPPER, 0.0, 1.0))
+    table = jnp.cos((row_pos + ahead) / total_rows * ARC_SPAN - 0.5 * ARC_SPAN)
+    return jnp.where((kind == INNER) & (row_pos == total_rows - 1), 0.0, table)
 
 
 def fold(row):
@@ -50,10 +49,22 @@
     return lax.broadcasted_iota(jnp.int32, (rows, width), 1)
 
 
-def local_kernel(flags, tabs, src, z, u, w, v, pack, inv, ew_t, up_t, lo_t):
+def local_kernel(
+    flags_in, source, z, u, w, v, pack, tabs, src, inv, ew_t, up_t, lo_t, flags, sems
+):
     rows, cols = src.shape
     tiles = cols // TILE
     blocks = TILE // SUB
+    parts = sems.shape[0] - 1
+    chunk = rows // parts
+    flag_copy = pltpu.make_async_copy(flags_in, flags, sems.at[parts])
+    flag_copy.start()
+    loads = []
+    for i in range(parts):
+        part = pl.ds(i * chunk, chunk)
+        loads.append(pltpu.make_async_copy(source.at[part, :], src.at[part, :], sems.at[i]))
+        loads[-1].start()
+    tabs[...] = coefficient_table(tabs.shape[1])
     start = pl.multiple_of(lax.axis_index("lat") * rows, rows)
     band = jnp.transpose(tabs[:, pl.ds(start, rows)])
     ew = wide(band[:, EAST_WEST : EAST_WEST + 1])
@@ -71,6 +82,7 @@
     zero = jnp.zeros((SUB, TILE), jnp.float32)
     row_id = lax.broadcasted_iota(jnp.int32, (SUB, TILE), 0)
     lane = lane_ids(SUB)
+    flag_copy.wait()
     kinds = [
         [
             jnp.where(flags[band_row, c] == 0, 0, jnp.where(flags[band_row, c] == 1, 1, 2))
@@ -92,28 +104,17 @@
         e, a, b = coeffs
         return e * (right + left) + a * above + b * below
 
-    def sweep(body, count):
-        sums = (zero,) * count
-        for band_row in range(rows // TILE):
-
-            def step(k, carry, band_row=band_row):
-                at = pl.multiple_of(band_row * TILE + k * SUB, SUB)
-                return body(at, kinds[band_row], carry)
-
-            sums = lax.fori_loop(0, blocks, step, sums)
-        return sums
-
-    def first_pass(at, kind, carry):
-        (m0,) = carry
+    def first_pass(at, kind, sums):
+        part = zero
         for c in range(tiles):
             b = src[pl.ds(at, SUB), columns(c)]
             value = b * inv[kind[c], pl.ds(at, SUB), :]
             z[pl.ds(at + SUB, SUB), columns(c)] = value
-            m0 = m0 + b * value
-        return (m0,)
-
-    def second_pass(at, kind, carry):
-        m1, m2 = carry
+            part = part + b * value
+        return (sums[0] + part,) + sums[1:]
+
+    def second_pass(at, kind, sums):
+        part1, part2 = zero, zero
         here_rows = pl.ds(at, SUB)
         coeffs = ew_t[here_rows, :], up_t[here_rows, :], lo_t[here_rows, :]
         line = [zero] + [z[pl.ds(at + SUB, SUB), columns(c)] for c in range(tiles)] + [zero]
@@ -124,12 +125,12 @@
             scaled = image * inv[kind[c], here_rows, :]
             w[here_rows, columns(c)] = image
             u[pl.ds(at + SUB, SUB), columns(c)] = scaled
-            m1 = m1 + here * image
-            m2 = m2 + scaled * image
-        return m1, m2
-
-    def third_pass(at, kind, carry):
-        (m3,) = carry
+            part1 = part1 + here * image
+            part2 = part2 + scaled * image
+        return sums[0], sums[1] + part1, sums[2] + part2, sums[3]
+
+    def third_pass(at, kind, sums):
+        part = zero
         here_rows = pl.ds(at, SUB)
         coeffs = ew_t[here_rows, :], up_t[here_rows, :], lo_t[here_rows, :]
         line = [zero] + [u[pl.ds(at + SUB, SUB), columns(c)] for c in range(tiles)] + [zero]
@@ -138,12 +139,27 @@
             near = around(u, at, c, here, line[c], line[c + 2], coeffs)
             image = w[here_rows, columns(c)] - near
             v[here_rows, columns(c)] = image
-            m3 = m3 + here * image
-        return (m3,)
-
-    (m0,) = sweep(first_pass, 1)
-    m1, m2 = sweep(second_pass, 2)
-    (m3,) = sweep(third_pass, 1)
+            part = part + here * image
+        return sums[:3] + (sums[3] + part,)
+
+    count = rows // SUB
+    done = [0, 0, 0]
+    sums = (zero,) * 4
+    for i in range(parts):
+        loads[i].wait()
+        ready = (i + 1) * (chunk // SUB)
+        for which, body in enumerate((first_pass, second_pass, third_pass)):
+            upto = ready - which if i + 1 < parts else count
+            while done[which] < upto:
+                band_row = done[which] // blocks
+                stop = min(upto, (band_row + 1) * blocks)
+
+                def step(k, carry, body=body, band_row=band_row):
+                    return body(pl.multiple_of(k * SUB, SUB), kinds[band_row], carry)
+
+                sums = lax.fori_loop(done[which], stop, step, sums, unroll=stop - done[which])
+                done[which] = stop
+    m0, m1, m2, m3 = sums
 
     last = rows - 1
     pack[Z0 : Z0 + 1, :cols] = z[SUB : SUB + 1, :]
@@ -201,8 +217,12 @@
         out[i + 1 : i + 2, at : at + TILE] += change
 
 
-def lat_kernel(stage, final, cols, tabs, own, other, ext_in, out, ext):
-    height = own.shape[1] - cols - TILE
+def lat_kernel(stage, stages, cols, tabs, own, other, ext_in, out, ext):
+    facing = 0 < stage == stages - 1
+    final = stage == stages - 1
+    half = cols // 2
+    span = half if facing else cols
+    height = own.shape[1] - span - TILE
     index = lax.axis_index("lat")
     top, bottom, at_end, at_start = sides(own, other, index, stage)
     size = 2**stage
@@ -215,8 +235,18 @@
     next_b = wide(low[LOWER : LOWER + 1, :1])
     next_t = wide(high[UPPER : UPPER + 1, TILE - 1 :])
 
-    zt, ut, vt, it = (row_of(top, i, 0, cols) for i in (Z1, U1, V1, I1))
-    zb, ub, vb, ib = (row_of(bottom, i, 0, cols) for i in (Z0, U0, V0, I0))
+    if facing:
+
+        def joined(pack, i):
+            return jnp.concatenate(
+                [row_of(pack, i, 0, half), row_of(pack, i + 4, 0, half)], axis=1
+            )
+
+        zt, ut, vt, it = (joined(top, i) for i in range(4))
+        zb, ub, vb, ib = (joined(bottom, i) for i in range(4))
+    else:
+        zt, ut, vt, it = (row_of(top, i, 0, cols) for i in (Z1, U1, V1, I1))
+        zb, ub, vb, ib = (row_of(bottom, i, 0, cols) for i in (Z0, U0, V0, I0))
     et, eb = -cross * zb, -cross * zt
     dt, db = it * et, ib * eb
     full_t, full_b = ut + dt, ub + db
@@ -228,14 +258,23 @@
     third = fold(dt * (2.0 * vt + et) + db * (2.0 * vb + eb) - 2.0 * cross * full_t * full_b)
     third = third - 2.0 * (ew_t * fold(pair_t) + ew_b * fold(pair_b))
 
-    base = 0 if final else cols
-    if not final:
-        top_rows = (lax.broadcasted_iota(jnp.int32, (SUB, cols), 0) < Z1) | (
-            lax.broadcasted_iota(jnp.int32, (SUB, cols), 0) == I0
-        )
-        out[:, :cols] = jnp.where(top_rows, top[:, :cols], bottom[:, :cols])
-    out[:, base : base + height] = top[:, cols : cols + height]
-    out[:, base + height : base + 2 * height] = bottom[:, cols : cols + height]
+    if final:
+        base = 0
+    elif stage + 1 == stages - 1:
+        base = half
+        up_next = lax.rem(lax.div(index, 2 * size), 2) == 0
+        for i, (first_row, last_row) in enumerate(((Z0, Z1), (U0, U1), (V0, V1), (I0, I1))):
+            row = jnp.where(
+                up_next, row_of(bottom, last_row, 0, cols), row_of(top, first_row, 0, cols)
+            )
+            out[i : i + 1, :half] = row[:, :half]
+            out[i + 4 : i + 5, :half] = row[:, half:]
+    else:
+        base = cols
+        ids = lax.broadcasted_iota(jnp.int32, (SUB, cols), 0)
+        out[:, :cols] = jnp.where((ids < Z1) | (ids == I0), top[:, :cols], bottom[:, :cols])
+    out[:, base : base + height] = top[:, span : span + height]
+    out[:, base + height : base + 2 * height] = bottom[:, span : span + height]
     add_moments(out, base + 2 * height, top, bottom, (2.0 * twice, second, third))
 
     lane = lane_ids(1)
@@ -461,8 +500,8 @@
         return carry
 
     parts = rows // chunk
-    for i in range(parts):
-        lax.fori_loop(i * blocks, (i + 1) * blocks, step, 0)
+    for i in list(range(1, parts)) + [0]:
+        lax.fori_loop(i * blocks, (i + 1) * blocks, step, 0, unroll=blocks)
         if i == 0:
             dx, dr, dr_next = row_mods[0]
             field_x[0:1, :] += dx
@@ -484,12 +523,12 @@
     return jax.ShapeDtypeStruct(dims, jnp.float32)
 
 
-def call(kernel, name, out_shape, n_in, smem=0, out_specs=None, scratch=(), limit=32):
+def call(kernel, name, out_shape, in_specs, out_specs=None, scratch=(), limit=32):
     return pl.pallas_call(
         kernel,
         name=name,
         out_shape=out_shape,
-        in_specs=[SMEM_SPEC] * smem + [VMEM_SPEC] * (n_in - smem),
+        in_specs=in_specs,
         out_specs=out_specs or [VMEM_SPEC] * len(out_shape),
         scratch_shapes=list(scratch),
         compiler_params=pltpu.CompilerParams(vmem_limit_bytes=limit << 20),
@@ -500,8 +539,7 @@
     rows, cols = source.shape
     bands, sectors = lax.axis_size("lat"), lax.axis_size("lon")
     height = rows * bands
-    tabs = coefficient_table(height)
-    z, u, w, v, edges = call(
+    z, u, w, v, edges, tabs, src = call(
         local_kernel,
         "local",
         [
@@ -510,12 +548,14 @@
             shape(rows, cols),
             shape(rows, cols),
             shape(SUB, cols + rows + TILE),
+            shape(SUB, height),
+            shape(rows, cols),
         ],
-        3,
-        smem=1,
+        [HBM_SPEC, HBM_SPEC],
         scratch=[pltpu.VMEM((3, rows, TILE), jnp.float32)]
-        + [pltpu.VMEM((rows, TILE), jnp.float32)] * 3,
-    )(flags, tabs, source)
+        + [pltpu.VMEM((rows, TILE), jnp.float32)] * 3
+        + [pltpu.SMEM(flags.shape, jnp.int32), pltpu.SemaphoreType.DMA((LOADS + 1,))],
+    )(*(pltpu.with_memory_space_constraint(a, pltpu.HBM) for a in (flags, source)))
 
     def swap(pack, axis, stage):
         count = lax.axis_size(axis)
@@ -525,13 +565,13 @@
     lon_stages = sectors.bit_length() - 1
     pack, row_ext = edges, edges
     for stage in range(lat_stages):
-        final = stage == lat_stages - 1
-        tall = (rows << (stage + 1)) + TILE + (0 if final else cols)
+        left = lat_stages - 1 - stage
+        tall = (rows << (stage + 1)) + TILE + (cols, cols // 2, 0)[max(0, 2 - left)]
         pack, row_ext = call(
-            functools.partial(lat_kernel, stage, final, cols),
+            functools.partial(lat_kernel, stage, lat_stages, cols),
             f"lat_merge{stage}",
             [shape(SUB, tall), shape(SUB, cols)],
-            4,
+            [VMEM_SPEC] * 4,
         )(tabs, pack, swap(pack, "lat", stage), row_ext)
     col_ext = pack
     for stage in range(lon_stages - 1):
@@ -539,16 +579,15 @@
             functools.partial(lon_kernel, stage),
             f"lon_merge{stage}",
             [shape(SUB, height + TILE), shape(SUB, height)],
-            4,
+            [VMEM_SPEC] * 4,
         )(tabs, pack, swap(pack, "lon", stage), col_ext)
     stage = lon_stages - 1
-    any_spec = pl.BlockSpec(memory_space=pl.ANY)
     x, r = call(
         functools.partial(last_kernel, stage, 32),
         "combine",
         [shape(rows, cols), shape(rows, cols)],
-        11,
-        out_specs=[any_spec, any_spec],
+        [VMEM_SPEC] * 11,
+        out_specs=[HBM_SPEC, HBM_SPEC],
         scratch=[
             pltpu.VMEM((SUB, TILE), jnp.float32),
             pltpu.VMEM((SUB, height), jnp.float32),
@@ -557,7 +596,7 @@
             pltpu.VMEM((rows, SUB), jnp.float32),
             pltpu.SemaphoreType.DMA((2,)),
         ],
-    )(tabs, pack, swap(pack, "lon", stage), col_ext, edges, row_ext, source, z, u, w, v)
+    )(tabs, pack, swap(pack, "lon", stage), col_ext, edges, row_ext, src, z, u, w, v)
     return x, r
 
 

time: 37.5 us -> 28.5 us (0.76)
  Pallas kernels: 13.7 us -> 7.84 us
  local copies, waits for them, and re-layouts: 2.32 us -> 0 us
  waiting for transfers between devices: 10 us -> 8.88 us
  starting transfers between devices: 10.3 us -> 10.9 us
    pallas_call x1, Pallas kernels: 9.08 us -> 4.34 us  [per_device(): call(local_kernel, 'local', [shape(rows + 2 * SUB, cols), shape(rows + 2...]
    unnamed x6 -> x0, local copies, waits for them, and re-layouts: 2.27 us -> none
    ppermute x5, waiting for transfers between devices: 10 us -> 8.88 us  [swap(): return lax.ppermute(pack, axis, [(i, i ^ 1 << stage) for i in range(count)])]
    pallas_call x1, Pallas kernels: 3.84 us -> 2.74 us  [per_device(): call(functools.partial(last_kernel, stage, 32), 'combine', [shape(rows, c...]
    ppermute x5, starting transfers between devices: 10.3 us -> 10.9 us  [swap(): return lax.ppermute(pack, axis, [(i, i ^ 1 << stage) for i in range(count)])]
where the time goes in v3:
time: 28.5 us; the launch traced here: 28.3 us
  starting transfers between devices  10.9 us (38%)
  waiting for transfers between devices  8.88 us (31%)
  Pallas kernels  7.84 us (28%)
  between operations  0.67 us (2%)
    ppermute x5, starting transfers between devices, swap(): return lax.ppermute(pack, axis, [(i, i ^ 1 << stage) for i in range(count)])  10.9 us
    ppermute x5, waiting for transfers between devices, swap(): return lax.ppermute(pack, axis, [(i, i ^ 1 << stage) for i in range(count)])  8.88 us
    pallas_call x1, Pallas kernels, per_device(): call(local_kernel, 'local', [shape(rows + 2 * SUB, cols), shape(rows + 2...  4.34 us
    pallas_call x1, Pallas kernels, per_device(): call(functools.partial(last_kernel, stage, 32), 'combine', [shape(rows, c...  2.74 us
  transfers between devices with their start and end apart: 5, of which 5 were waited for; matrix products, arithmetic and copies ran while one was open for 0% of the time, Pallas kernels for 0%

profile of v3, /device:TPU:0, one launch (start us, length us, event | category | flops | bytes accessed | tf_op | source)
XLA Modules:
  0.0 28.3 jit_solution(560995255273318800)
XLA Ops:
  0.6 4.3 %local.1 = (f32[272,2048]{1,0:T(8,128)S(1)}, f32[272,2048]{1,0:T(8,128)S(1)}, f32[256,2048]{1,0:T(8,128)S(1)}, f32[256,2048]{1,0:T(8,128)S(1)}, f32[8,2432]{1,0:...) custom-call(s32[2,16]{1,0:T(2,128)} %flags_in.1, f32[256,2048]{1,0:T(8,128)} %source.1), custom_call_target="tpu_custom_call" | custom-call | tf_op jit(solution)/shard_map/local/pallas_call | solution.py:542
  5.0 0.5 %collective-permute-start = (f32[8,2432]{1,0:T(8,128)S(1)}, f32[8,2432]{1,0:T(8,128)S(1)}, u32[]{:S(2)}, u32[]{:S(2)}) collective-permute-start(f32[8,2432]{1,0:T(8,128)S(1)} %get-tuple-element.18.own.ext_in.edges), channel_id=1, source_target_pairs={{0,8},{8,0},{16,24},{24,16},{1,9},{9,1},{17,25},{25,17},{2,10},{10... | collective-permute-start | bytes 233480 | tf_op jit(solution)/shard_map/ppermute | solution.py:562
  5.5 0.9 %collective-permute-done.other = f32[8,2432]{1,0:T(8,128)S(1)} collective-permute-done((f32[8,2432]{1,0:T(8,128)S(1)}, f32[8,2432]{1,0:T(8,128)S(1)}, u32[]{:S(2)}, u32[]{:S(2)}) %collective-permute-start) | collective-permute-done | bytes 77856 | tf_op jit(solution)/shard_map/ppermute | solution.py:562
  6.4 0.3 lat_merge0.1
  6.7 2.9 %collective-permute-start.1 = (f32[8,1664]{1,0:T(8,128)S(1)}, f32[8,1664]{1,0:T(8,128)S(1)}, u32[]{:S(2)}, u32[]{:S(2)}) collective-permute-start(f32[8,1664]{1,0:T(8,128)S(1)} %get-tuple-element.19.own), channel_id=1, source_target_pairs={{0,16},{8,24},{16,0},{24,8},{1,17},{9,25},{17,1},{25,9},{2,18},{10... | collective-permute-start | bytes 159752 | tf_op jit(solution)/shard_map/ppermute | solution.py:562
  9.6 2.1 %collective-permute-done.1.other = f32[8,1664]{1,0:T(8,128)S(1)} collective-permute-done((f32[8,1664]{1,0:T(8,128)S(1)}, f32[8,1664]{1,0:T(8,128)S(1)}, u32[]{:S(2)}, u32[]{:S(2)}) %collective-permute-start.1) | collective-permute-done | bytes 53280 | tf_op jit(solution)/shard_map/ppermute | solution.py:562
  11.7 0.2 lat_merge1.1
  12.0 2.1 %collective-permute-start.2 = (f32[8,1152]{1,0:T(8,128)S(1)}, f32[8,1152]{1,0:T(8,128)S(1)}, u32[]{:S(2)}, u32[]{:S(2)}) collective-permute-start(f32[8,1152]{1,0:T(8,128)S(1)} %get-tuple-element.21.own.ext_in), channel_id=1, source_target_pairs={{0,1},{1,0},{2,3},{3,2},{4,5},{5,4},{6,7},{7,6},{8,9},{9,8},{10,11... | collective-permute-start | bytes 110600 | tf_op jit(solution)/shard_map/ppermute | solution.py:562
  14.0 1.9 %collective-permute-done.2.other = f32[8,1152]{1,0:T(8,128)S(1)} collective-permute-done((f32[8,1152]{1,0:T(8,128)S(1)}, f32[8,1152]{1,0:T(8,128)S(1)}, u32[]{:S(2)}, u32[]{:S(2)}) %collective-permute-start.2) | collective-permute-done | bytes 36896 | tf_op jit(solution)/shard_map/ppermute | solution.py:562
  16.0 0.1 lon_merge0.1
  16.1 2.1 %collective-permute-start.3 = (f32[8,1152]{1,0:T(8,128)S(1)}, f32[8,1152]{1,0:T(8,128)S(1)}, u32[]{:S(2)}, u32[]{:S(2)}) collective-permute-start(f32[8,1152]{1,0:T(8,128)S(1)} %get-tuple-element.22.own), channel_id=1, source_target_pairs={{0,2},{1,3},{2,0},{3,1},{4,6},{5,7},{6,4},{7,5},{8,10},{9,11},{10,... | collective-permute-start | bytes 110600 | tf_op jit(solution)/shard_map/ppermute | solution.py:562
  18.3 1.9 %collective-permute-done.3.other = f32[8,1152]{1,0:T(8,128)S(1)} collective-permute-done((f32[8,1152]{1,0:T(8,128)S(1)}, f32[8,1152]{1,0:T(8,128)S(1)}, u32[]{:S(2)}, u32[]{:S(2)}) %collective-permute-start.3) | collective-permute-done | bytes 36896 | tf_op jit(solution)/shard_map/ppermute | solution.py:562
  20.2 0.1 lon_merge1.1
  20.3 3.3 %collective-permute-start.4 = (f32[8,1152]{1,0:T(8,128)S(1)}, f32[8,1152]{1,0:T(8,128)S(1)}, u32[]{:S(2)}, u32[]{:S(2)}) collective-permute-start(f32[8,1152]{1,0:T(8,128)S(1)} %get-tuple-element.24.own), channel_id=1, source_target_pairs={{0,4},{1,5},{2,6},{3,7},{4,0},{5,1},{6,2},{7,3},{8,12},{9,13},{10,... | collective-permute-start | bytes 110600 | tf_op jit(solution)/shard_map/ppermute | solution.py:562
  23.6 1.9 %collective-permute-done.4.other = f32[8,1152]{1,0:T(8,128)S(1)} collective-permute-done((f32[8,1152]{1,0:T(8,128)S(1)}, f32[8,1152]{1,0:T(8,128)S(1)}, u32[]{:S(2)}, u32[]{:S(2)}) %collective-permute-start.4) | collective-permute-done | bytes 36896 | tf_op jit(solution)/shard_map/ppermute | solution.py:562
  25.6 2.7 %combine.1 = (f32[256,2048]{1,0:T(8,128)}, f32[256,2048]{1,0:T(8,128)}) custom-call(f32[8,1024]{1,0:T(8,128)S(1)} %get-tuple-element.17.tabs, f32[8,1152]{1,0:T(8,128)S(1)} %get-tuple-element.24.own, f32[8,1152]{1,0:T(8,128)S(1)} %collective-permute-done.4.other, f32[8,1024]{1,0:T(8,128)S(1)} %get-tuple-element.25.ext_in, ...), custom_call_target="tpu_custom_call" | custom-call | tf_op jit(solution)/shard_map/combine/pallas_call | solution.py:585
Async XLA Ops:
  5.0 1.4 %collective-permute-start = (f32[8,2432]{1,0:T(8,128)S(1)}, f32[8,2432]{1,0:T(8,128)S(1)}, u32[]{:S(2)}, u32[]{:S(2)}) collective-permute-start(f32[8,2432]{1,0:T(8,128)S(1)} %get-tuple-element.18.own.ext_in.edges), channel_id=1, source_target_pairs={{0,8},{8,0},{16,24},{24,16},{1,9},{9,1},{17,25},{25,17},{2,10},{10... | collective-permute-start | bytes 233480 | tf_op jit(solution)/shard_map/ppermute | solution.py:562
  6.7 5.1 %collective-permute-start.1 = (f32[8,1664]{1,0:T(8,128)S(1)}, f32[8,1664]{1,0:T(8,128)S(1)}, u32[]{:S(2)}, u32[]{:S(2)}) collective-permute-start(f32[8,1664]{1,0:T(8,128)S(1)} %get-tuple-element.19.own), channel_id=1, source_target_pairs={{0,16},{8,24},{16,0},{24,8},{1,17},{9,25},{17,1},{25,9},{2,18},{10... | collective-permute-start | bytes 159752 | tf_op jit(solution)/shard_map/ppermute | solution.py:562
  12.0 4.0 %collective-permute-start.2 = (f32[8,1152]{1,0:T(8,128)S(1)}, f32[8,1152]{1,0:T(8,128)S(1)}, u32[]{:S(2)}, u32[]{:S(2)}) collective-permute-start(f32[8,1152]{1,0:T(8,128)S(1)} %get-tuple-element.21.own.ext_in), channel_id=1, source_target_pairs={{0,1},{1,0},{2,3},{3,2},{4,5},{5,4},{6,7},{7,6},{8,9},{9,8},{10,11... | collective-permute-start | bytes 110600 | tf_op jit(solution)/shard_map/ppermute | solution.py:562
  16.1 4.1 %collective-permute-start.3 = (f32[8,1152]{1,0:T(8,128)S(1)}, f32[8,1152]{1,0:T(8,128)S(1)}, u32[]{:S(2)}, u32[]{:S(2)}) collective-permute-start(f32[8,1152]{1,0:T(8,128)S(1)} %get-tuple-element.22.own), channel_id=1, source_target_pairs={{0,2},{1,3},{2,0},{3,1},{4,6},{5,7},{6,4},{7,5},{8,10},{9,11},{10,... | collective-permute-start | bytes 110600 | tf_op jit(solution)/shard_map/ppermute | solution.py:562
  20.3 5.2 %collective-permute-start.4 = (f32[8,1152]{1,0:T(8,128)S(1)}, f32[8,1152]{1,0:T(8,128)S(1)}, u32[]{:S(2)}, u32[]{:S(2)}) collective-permute-start(f32[8,1152]{1,0:T(8,128)S(1)} %get-tuple-element.24.own), channel_id=1, source_target_pairs={{0,4},{1,5},{2,6},{3,7},{4,0},{5,1},{6,2},{7,3},{8,12},{9,13},{10,... | collective-permute-start | bytes 110600 | tf_op jit(solution)/shard_map/ppermute | solution.py:562

commit v4 on v3

--- a/solution.py
+++ b/solution.py
@@ -13,6 +13,7 @@
 SUB = 8
 VMEM_SPEC = pl.BlockSpec(memory_space=pltpu.VMEM)
 HBM_SPEC = pl.BlockSpec(memory_space=pltpu.HBM)
+ANY_SPEC = pl.BlockSpec(memory_space=pl.ANY)
 LOADS = 4
 Z0, U0, V0, Z1, U1, V1, I0, I1 = range(8)
 EAST_WEST, UPPER, LOWER, INNER = range(4)
@@ -49,8 +50,41 @@
     return lax.broadcasted_iota(jnp.int32, (rows, width), 1)
 
 
+def columns(c):
+    return pl.ds(c * TILE, TILE)
+
+
+def line_of(field, at, tiles):
+    zero = jnp.zeros((SUB, TILE), jnp.float32)
+    return [zero] + [field[pl.ds(at + SUB, SUB), columns(c)] for c in range(tiles)] + [zero]
+
+
+def ahead_of(field, at, c, line, coeffs):
+    row_id = lax.broadcasted_iota(jnp.int32, (SUB, TILE), 0)
+    here = line[c + 1]
+    later = field[pl.ds(at + 2 * SUB, SUB), columns(c)]
+    below = pltpu.roll(jnp.where(row_id == 0, later, here), SUB - 1, 0)
+    right = pltpu.roll(jnp.where(lane_ids(SUB) == 0, line[c + 2], here), TILE - 1, 1)
+    return right, coeffs[2] * below
+
+
+def behind_of(field, at, c, line, coeffs):
+    row_id = lax.broadcasted_iota(jnp.int32, (SUB, TILE), 0)
+    here = line[c + 1]
+    prev = field[pl.ds(at, SUB), columns(c)]
+    above = pltpu.roll(jnp.where(row_id == SUB - 1, prev, here), 1, 0)
+    left = pltpu.roll(jnp.where(lane_ids(SUB) == TILE - 1, line[c], here), 1, 1)
+    return left, coeffs[1] * above
+
+
+def around(field, at, c, line, coeffs):
+    right, below = ahead_of(field, at, c, line, coeffs)
+    left, above = behind_of(field, at, c, line, coeffs)
+    return coeffs[0] * (right + left) + (above + below)
+
+
 def local_kernel(
-    flags_in, source, z, u, w, v, pack, tabs, src, inv, ew_t, up_t, lo_t, flags, sems
+    flags_in, source, z, u, w, pack, tabs, src, coef, inv, v_edge, flags, sems
 ):
     rows, cols = src.shape
     tiles = cols // TILE
@@ -63,16 +97,16 @@
     for i in range(parts):
         part = pl.ds(i * chunk, chunk)
         loads.append(pltpu.make_async_copy(source.at[part, :], src.at[part, :], sems.at[i]))
-        loads[-1].start()
+        if i < 2:
+            loads[-1].start()
     tabs[...] = coefficient_table(tabs.shape[1])
     start = pl.multiple_of(lax.axis_index("lat") * rows, rows)
     band = jnp.transpose(tabs[:, pl.ds(start, rows)])
     ew = wide(band[:, EAST_WEST : EAST_WEST + 1])
     up = wide(band[:, UPPER : UPPER + 1])
     lo = wide(band[:, LOWER : LOWER + 1])
-    ew_t[...] = ew
-    up_t[...] = up
-    lo_t[...] = lo
+    for i, values in enumerate((ew, up, lo)):
+        coef[i] = values
     for kind, screen in enumerate((0.05, 0.4, 2.0)):
         inv[kind] = 1.0 / (screen + 2.0 * ew + up + lo)
     nothing = jnp.zeros((SUB, cols), jnp.float32)
@@ -80,8 +114,6 @@
         padded[:SUB] = nothing
         padded[rows + SUB :] = nothing
     zero = jnp.zeros((SUB, TILE), jnp.float32)
-    row_id = lax.broadcasted_iota(jnp.int32, (SUB, TILE), 0)
-    lane = lane_ids(SUB)
     flag_copy.wait()
     kinds = [
         [
@@ -91,19 +123,6 @@
         for band_row in range(rows // TILE)
     ]
 
-    def columns(c):
-        return pl.ds(c * TILE, TILE)
-
-    def around(field, at, c, here, west, east, coeffs):
-        prev = field[pl.ds(at, SUB), columns(c)]
-        later = field[pl.ds(at + 2 * SUB, SUB), columns(c)]
-        above = pltpu.roll(jnp.where(row_id == SUB - 1, prev, here), 1, 0)
-        below = pltpu.roll(jnp.where(row_id == 0, later, here), SUB - 1, 0)
-        right = pltpu.roll(jnp.where(lane == 0, east, here), TILE - 1, 1)
-        left = pltpu.roll(jnp.where(lane == TILE - 1, west, here), 1, 1)
-        e, a, b = coeffs
-        return e * (right + left) + a * above + b * below
-
     def first_pass(at, kind, sums):
         part = zero
         for c in range(tiles):
@@ -116,30 +135,31 @@
     def second_pass(at, kind, sums):
         part1, part2 = zero, zero
         here_rows = pl.ds(at, SUB)
-        coeffs = ew_t[here_rows, :], up_t[here_rows, :], lo_t[here_rows, :]
-        line = [zero] + [z[pl.ds(at + SUB, SUB), columns(c)] for c in range(tiles)] + [zero]
+        coeffs = [coef[i, here_rows, :] for i in range(3)]
+        line = line_of(z, at, tiles)
         for c in range(tiles):
-            here = line[c + 1]
-            near = around(z, at, c, here, line[c], line[c + 2], coeffs)
-            image = src[here_rows, columns(c)] - near
+            image = src[here_rows, columns(c)] - around(z, at, c, line, coeffs)
             scaled = image * inv[kind[c], here_rows, :]
             w[here_rows, columns(c)] = image
             u[pl.ds(at + SUB, SUB), columns(c)] = scaled
-            part1 = part1 + here * image
+            part1 = part1 + line[c + 1] * image
             part2 = part2 + scaled * image
         return sums[0], sums[1] + part1, sums[2] + part2, sums[3]
 
     def third_pass(at, kind, sums):
         part = zero
         here_rows = pl.ds(at, SUB)
-        coeffs = ew_t[here_rows, :], up_t[here_rows, :], lo_t[here_rows, :]
-        line = [zero] + [u[pl.ds(at + SUB, SUB), columns(c)] for c in range(tiles)] + [zero]
+        coeffs = [coef[i, here_rows, :] for i in range(3)]
+        line = line_of(u, at, tiles)
         for c in range(tiles):
-            here = line[c + 1]
-            near = around(u, at, c, here, line[c], line[c + 2], coeffs)
-            image = w[here_rows, columns(c)] - near
-            v[here_rows, columns(c)] = image
-            part = part + here * image
+            right, below = ahead_of(u, at, c, line, coeffs)
+            near = coeffs[0] * right + below
+            image = w[here_rows, columns(c)]
+            part = part + line[c + 1] * (image - (near + near))
+            if c in (0, tiles - 1):
+                left, above = behind_of(u, at, c, line, coeffs)
+                edge = pl.ds(0 if c == 0 else TILE, TILE)
+                v_edge[here_rows, edge] = image - near - (coeffs[0] * left + above)
         return sums[:3] + (sums[3] + part,)
 
     count = rows // SUB
@@ -147,6 +167,8 @@
     sums = (zero,) * 4
     for i in range(parts):
         loads[i].wait()
+        if i + 2 < parts:
+            loads[i + 2].start()
         ready = (i + 1) * (chunk // SUB)
         for which, body in enumerate((first_pass, second_pass, third_pass)):
             upto = ready - which if i + 1 < parts else count
@@ -164,10 +186,14 @@
     last = rows - 1
     pack[Z0 : Z0 + 1, :cols] = z[SUB : SUB + 1, :]
     pack[U0 : U0 + 1, :cols] = u[SUB : SUB + 1, :]
-    pack[V0 : V0 + 1, :cols] = v[:1, :]
     pack[Z1 : Z1 + 1, :cols] = z[last + SUB : last + SUB + 1, :]
     pack[U1 : U1 + 1, :cols] = u[last + SUB : last + SUB + 1, :]
-    pack[V1 : V1 + 1, :cols] = v[last:, :]
+    for at, v_row, place in ((0, V0, 0), (rows - SUB, V1, SUB - 1)):
+        line = line_of(u, at, tiles)
+        coeffs = [coef[i, at : at + SUB, :] for i in range(3)]
+        for c in range(tiles):
+            image = w[at : at + SUB, columns(c)] - around(u, at, c, line, coeffs)
+            pack[v_row : v_row + 1, columns(c)] = image[place : place + 1, :]
     for c in range(tiles):
         pack[I0 : I0 + 1, c * TILE : (c + 1) * TILE] = inv[kinds[0][c], :1, :]
         pack[I1 : I1 + 1, c * TILE : (c + 1) * TILE] = inv[kinds[-1][c], last:, :]
@@ -179,10 +205,10 @@
         ids = lane_ids(TILE)
         mix = inv[kinds[band_row][-1], here_rows, :]
         mix = jnp.where(ids == I0, inv[kinds[band_row][0], here_rows, :], mix)
-        mix = jnp.where(ids == V1, pltpu.roll(v[here_rows, east], V1 + 1, 1), mix)
+        mix = jnp.where(ids == V1, pltpu.roll(v_edge[here_rows, TILE:], V1 + 1, 1), mix)
         mix = jnp.where(ids == U1, pltpu.roll(u[inner_rows, east], U1 + 1, 1), mix)
         mix = jnp.where(ids == Z1, pltpu.roll(z[inner_rows, east], Z1 + 1, 1), mix)
-        mix = jnp.where(ids == V0, pltpu.roll(v[here_rows, :TILE], V0, 1), mix)
+        mix = jnp.where(ids == V0, pltpu.roll(v_edge[here_rows, :TILE], V0, 1), mix)
         mix = jnp.where(ids == U0, pltpu.roll(u[inner_rows, :TILE], U0, 1), mix)
         mix = jnp.where(ids == Z0, z[inner_rows, :TILE], mix)
         at = cols + band_row * TILE
@@ -192,6 +218,61 @@
     pack[:, at:] = zero
     for i, m in enumerate((m0, m1, m2, m3)):
         pack[i : i + 1, at:] = jnp.sum(m, axis=0, keepdims=True)
+
+
+def image_kernel(u, w, coef, after_stage, v):
+    del after_stage
+    rows, cols = w.shape
+    tiles = cols // TILE
+    unroll = 8
+
+    def step(k, carry):
+        at = pl.multiple_of(k * SUB, SUB)
+        here_rows = pl.ds(at, SUB)
+        coeffs = [coef[i, here_rows, :] for i in range(3)]
+        line = line_of(u, at, tiles)
+        for c in range(tiles):
+            v[here_rows, columns(c)] = w[here_rows, columns(c)] - around(u, at, c, line, coeffs)
+        return carry
+
+    lax.fori_loop(0, rows // SUB, step, 0, unroll=unroll)
+
+
+def row_kernel(rows, tabs, edges, row_ext, parts, corner):
+    cols = row_ext.shape[1]
+    height = tabs.shape[1]
+    start = pl.multiple_of(lax.axis_index("lat") * rows, rows)
+    col_lane = lane_ids(1, cols)
+    first = tabs[:, pl.ds(start, TILE)]
+    final = tabs[:, pl.ds(start + rows - TILE, TILE)]
+    tab_n = tabs[:, pl.ds(pl.multiple_of(jnp.maximum(start - TILE, 0), TILE), TILE)]
+    tab_s = tabs[:, pl.ds(pl.multiple_of(jnp.minimum(start + rows, height - TILE), TILE), TILE)]
+    for which in range(2):
+        at = 3 * which
+        if which == 0:
+            lane, own_tab, next_tab, next_lane = 0, first, tab_n, TILE - 1
+            cross_row, inner_row, inv_row = UPPER, LOWER, I0
+        else:
+            lane, own_tab, next_tab, next_lane = TILE - 1, final, tab_s, 0
+            cross_row, inner_row, inv_row = LOWER, UPPER, I1
+
+        def scalar(tab, row, place):
+            return wide(tab[row : row + 1, place : place + 1], cols)
+
+        cross = scalar(own_tab, cross_row, lane)
+        inner = scalar(own_tab, inner_row, lane)
+        ew_own = scalar(own_tab, EAST_WEST, lane)
+        ew_next = scalar(next_tab, EAST_WEST, next_lane)
+        e = -cross * row_ext[at : at + 1, :]
+        d = edges[inv_row : inv_row + 1, :cols] * e
+        right = jnp.where(col_lane == cols - 1, 0.0, after(d))
+        left = jnp.where(col_lane == 0, 0.0, before(d))
+        dv = e - ew_own * (right + left) - cross * row_ext[at + 1 : at + 2, :]
+        for i, row in enumerate((d, e, dv, inner * d)):
+            parts[4 * which + i : 4 * which + i + 1, :] = row
+        k = cross * ew_next * row_ext[at + 2 : at + 3, :]
+        ids = lane_ids(1)
+        corner[which : which + 1, :] = jnp.where(ids == 0, k[:, :TILE], k[:, cols - TILE :])
 
 
 def sides(own, other, index, stage):
@@ -360,7 +441,7 @@
 
 
 def last_kernel(
-    stage, chunk, tabs, own, other, ext_in, edges, row_ext, src, z, u, w, v,
+    stage, chunk, tabs, own, other, ext_in, edges, row_parts, corner, src, z, u, w, v,
     out_x, out_r, mom, ext, field_x, field_r, cols_t, sems,
 ):
     rows, cols = src.shape
@@ -427,43 +508,20 @@
     near_c = jnp.concatenate([near1] * tiles, axis=1)
     far_c = jnp.concatenate([far1] * tiles, axis=1)
     col_lane = lane_ids(1, cols)
-    first = tabs[:, pl.ds(start, TILE)]
-    final = tabs[:, pl.ds(start + rows - TILE, TILE)]
     clamp_n = pl.multiple_of(jnp.maximum(start - TILE, 0), TILE)
     clamp_s = pl.multiple_of(jnp.minimum(start + rows, height - TILE), TILE)
-    tab_n, tab_s = tabs[:, pl.ds(clamp_n, TILE)], tabs[:, pl.ds(clamp_s, TILE)]
-    ext_n, ext_s = ext[:, pl.ds(clamp_n, TILE)], ext[:, pl.ds(clamp_s, TILE)]
     row_mods = []
-    for which in range(2):
-        at = 3 * which
-        if which == 0:
-            lane = 0
-            own_tab, next_tab, next_ext, next_lane = first, tab_n, ext_n, TILE - 1
-            cross_row, inner_row, inv_row = UPPER, LOWER, I0
-        else:
-            lane = TILE - 1
-            own_tab, next_tab, next_ext, next_lane = final, tab_s, ext_s, 0
-            cross_row, inner_row, inv_row = LOWER, UPPER, I1
-
-        def scalar(tab, row, place):
-            return wide(tab[row : row + 1, place : place + 1], cols)
-
-        cross = scalar(own_tab, cross_row, lane)
-        inner = scalar(own_tab, inner_row, lane)
-        ew_own = scalar(own_tab, EAST_WEST, lane)
-        ew_next = scalar(next_tab, EAST_WEST, next_lane)
-        z_next = row_ext[at : at + 1, :]
-        u_next = row_ext[at + 1 : at + 2, :]
-        i_next = row_ext[at + 2 : at + 3, :]
-        corner = jnp.where(col_lane == 0, scalar(next_ext, 0, next_lane), 0.0)
-        corner = jnp.where(col_lane == cols - 1, scalar(next_ext, 2, next_lane), corner)
-        u_next = u_next - i_next * ew_next * corner
-        e = -cross * z_next
-        d = edges[inv_row : inv_row + 1, :cols] * e
-        right = jnp.where(col_lane == cols - 1, 0.0, after(d))
-        left = jnp.where(col_lane == 0, 0.0, before(d))
-        dv = e - ew_own * (right + left) - cross * u_next
-        row_mods.append((-far_c * d, far_c * dv - near_c * e, -far_c * inner * d))
+    for which, (clamp, place) in enumerate(((clamp_n, TILE - 1), (clamp_s, 0))):
+        next_ext = ext[:, pl.ds(clamp, TILE)]
+        d, e, dv, inner_d = (row_parts[4 * which + i : 4 * which + i + 1, :] for i in range(4))
+
+        def corner_of(row, lane):
+            cell = corner[which : which + 1, lane : lane + 1] * next_ext[row : row + 1, place : place + 1]
+            return wide(cell, cols)
+
+        dv = dv + jnp.where(col_lane == 0, corner_of(0, 0), 0.0)
+        dv = dv + jnp.where(col_lane == cols - 1, corner_of(2, TILE - 1), 0.0)
+        row_mods.append((-far_c * d, far_c * dv - near_c * e, -far_c * inner_d))
 
     lane = lane_ids(SUB)
     blocks = chunk // SUB
@@ -523,7 +581,7 @@
     return jax.ShapeDtypeStruct(dims, jnp.float32)
 
 
-def call(kernel, name, out_shape, in_specs, out_specs=None, scratch=(), limit=32):
+def call(kernel, name, out_shape, in_specs, out_specs=None, scratch=(), limit=32, cost=None):
     return pl.pallas_call(
         kernel,
         name=name,
@@ -531,6 +589,7 @@
         in_specs=in_specs,
         out_specs=out_specs or [VMEM_SPEC] * len(out_shape),
         scratch_shapes=list(scratch),
+        cost_estimate=cost,
         compiler_params=pltpu.CompilerParams(vmem_limit_bytes=limit << 20),
     )
 
@@ -539,21 +598,21 @@
     rows, cols = source.shape
     bands, sectors = lax.axis_size("lat"), lax.axis_size("lon")
     height = rows * bands
-    z, u, w, v, edges, tabs, src = call(
+    z, u, w, edges, tabs, src, coef = call(
         local_kernel,
         "local",
         [
             shape(rows + 2 * SUB, cols),
             shape(rows + 2 * SUB, cols),
             shape(rows, cols),
-            shape(rows, cols),
             shape(SUB, cols + rows + TILE),
             shape(SUB, height),
             shape(rows, cols),
+            shape(3, rows, TILE),
         ],
         [HBM_SPEC, HBM_SPEC],
         scratch=[pltpu.VMEM((3, rows, TILE), jnp.float32)]
-        + [pltpu.VMEM((rows, TILE), jnp.float32)] * 3
+        + [pltpu.VMEM((rows, 2 * TILE), jnp.float32)]
         + [pltpu.SMEM(flags.shape, jnp.int32), pltpu.SemaphoreType.DMA((LOADS + 1,))],
     )(*(pltpu.with_memory_space_constraint(a, pltpu.HBM) for a in (flags, source)))
 
@@ -573,6 +632,23 @@
             [shape(SUB, tall), shape(SUB, cols)],
             [VMEM_SPEC] * 4,
         )(tabs, pack, swap(pack, "lat", stage), row_ext)
+        if stage == 0:
+            v = call(
+                image_kernel,
+                "image",
+                [shape(rows, cols)],
+                [VMEM_SPEC] * 3 + [ANY_SPEC],
+                cost=pl.CostEstimate(
+                    flops=8 * rows * cols, bytes_accessed=12 * rows * cols, transcendentals=0
+                ),
+            )(u, w, coef, row_ext)[0]
+    row_parts, corner = call(
+        functools.partial(row_kernel, rows),
+        "row_parts",
+        [shape(SUB, cols), shape(SUB, TILE)],
+        [VMEM_SPEC] * 3,
+        cost=pl.CostEstimate(flops=60 * cols, bytes_accessed=64 * cols, transcendentals=0),
+    )(tabs, edges, row_ext)
     col_ext = pack
     for stage in range(lon_stages - 1):
         pack, col_ext = call(
@@ -586,7 +662,7 @@
         functools.partial(last_kernel, stage, 32),
         "combine",
         [shape(rows, cols), shape(rows, cols)],
-        [VMEM_SPEC] * 11,
+        [VMEM_SPEC] * 12,
         out_specs=[HBM_SPEC, HBM_SPEC],
         scratch=[
             pltpu.VMEM((SUB, TILE), jnp.float32),
@@ -596,7 +672,7 @@
             pltpu.VMEM((rows, SUB), jnp.float32),
             pltpu.SemaphoreType.DMA((2,)),
         ],
-    )(tabs, pack, swap(pack, "lon", stage), col_ext, edges, row_ext, src, z, u, w, v)
+    )(tabs, pack, swap(pack, "lon", stage), col_ext, edges, row_parts, corner, src, z, u, w, v)
     return x, r
 
 

time: 28.5 us -> 28.1 us (0.986)
  waiting for transfers between devices: 8.88 us -> 7.17 us
  Pallas kernels: 7.84 us -> 9.13 us
    ppermute x5, waiting for transfers between devices: 8.88 us -> 7.17 us  [swap(): return lax.ppermute(pack, axis, [(i, i ^ 1 << stage) for i in range(count)])]
    pallas_call x0 -> x2, Pallas kernels: none -> 1.7 us  [the longest x1 1.46 us: per_device(): call(image_kernel, 'image', [shape(rows, cols)], [VMEM_SPEC] * 3 + [ANY_S...]
    pallas_call x1, Pallas kernels: 4.34 us -> 4.04 us  [per_device(): call(local_kernel, 'local', [shape(rows + 2 * SUB, cols), shape(rows + 2...]
  transfers between devices with their start and end apart: 5 -> 5, of which waited for: 5 -> 5; matrix products, arithmetic and copies ran while one was open for 0% -> 0% of each run, Pallas kernels for 0% -> 6%
where the time goes in v4:
time: 28.1 us; the launch traced here: 27.9 us
  starting transfers between devices  10.9 us (39%)
  Pallas kernels  9.13 us (32%)
  waiting for transfers between devices  7.17 us (26%)
  between operations  0.68 us (2%)
    ppermute x5, starting transfers between devices, swap(): return lax.ppermute(pack, axis, [(i, i ^ 1 << stage) for i in range(count)])  10.9 us
    ppermute x5, waiting for transfers between devices, swap(): return lax.ppermute(pack, axis, [(i, i ^ 1 << stage) for i in range(count)])  7.17 us
    pallas_call x1, Pallas kernels, per_device(): call(local_kernel, 'local', [shape(rows + 2 * SUB, cols), shape(rows + 2...  4.04 us
    pallas_call x1, Pallas kernels, per_device(): call(functools.partial(last_kernel, stage, 32), 'combine', [shape(rows, c...  2.63 us
    pallas_call x1, Pallas kernels, per_device(): call(image_kernel, 'image', [shape(rows, cols)], [VMEM_SPEC] * 3 + [ANY_S...  1.46 us
  transfers between devices with their start and end apart: 5, of which 5 were waited for; matrix products, arithmetic and copies ran while one was open for 0% of the time, Pallas kernels for 6%

profile of v4, /device:TPU:0, one launch (start us, length us, event | category | flops | bytes accessed | tf_op | source)
XLA Modules:
  0.0 27.9 jit_solution(10578631773009106239)
XLA Ops:
  0.6 4.0 %local.1 = (f32[272,2048]{1,0:T(8,128)S(1)}, f32[272,2048]{1,0:T(8,128)S(1)}, f32[256,2048]{1,0:T(8,128)S(1)}, f32[8,2432]{1,0:T(8,128)S(1)}, f32[8,1024]{1,0:T(...) custom-call(s32[2,16]{1,0:T(2,128)} %flags_in.1, f32[256,2048]{1,0:T(8,128)} %source.1), custom_call_target="tpu_custom_call" | custom-call | tf_op jit(solution)/shard_map/local/pallas_call | solution.py:601
  4.7 0.5 %collective-permute-start = (f32[8,2432]{1,0:T(8,128)S(1)}, f32[8,2432]{1,0:T(8,128)S(1)}, u32[]{:S(2)}, u32[]{:S(2)}) collective-permute-start(f32[8,2432]{1,0:T(8,128)S(1)} %get-tuple-element.20.own.ext_in.edges), channel_id=1, source_target_pairs={{0,8},{8,0},{16,24},{24,16},{1,9},{9,1},{17,25},{25,17},{2,10},{10... | collective-permute-start | bytes 233480 | tf_op jit(solution)/shard_map/ppermute | solution.py:621
  5.2 0.9 %collective-permute-done.other = f32[8,2432]{1,0:T(8,128)S(1)} collective-permute-done((f32[8,2432]{1,0:T(8,128)S(1)}, f32[8,2432]{1,0:T(8,128)S(1)}, u32[]{:S(2)}, u32[]{:S(2)}) %collective-permute-start) | collective-permute-done | bytes 77856 | tf_op jit(solution)/shard_map/ppermute | solution.py:621
  6.1 0.3 lat_merge0.1
  6.4 2.9 %collective-permute-start.1 = (f32[8,1664]{1,0:T(8,128)S(1)}, f32[8,1664]{1,0:T(8,128)S(1)}, u32[]{:S(2)}, u32[]{:S(2)}) collective-permute-start(f32[8,1664]{1,0:T(8,128)S(1)} %get-tuple-element.21.own), channel_id=1, source_target_pairs={{0,16},{8,24},{16,0},{24,8},{1,17},{9,25},{17,1},{25,9},{2,18},{10... | collective-permute-start | bytes 159752 | tf_op jit(solution)/shard_map/ppermute | solution.py:621
  9.3 2.1 %collective-permute-done.1.other = f32[8,1664]{1,0:T(8,128)S(1)} collective-permute-done((f32[8,1664]{1,0:T(8,128)S(1)}, f32[8,1664]{1,0:T(8,128)S(1)}, u32[]{:S(2)}, u32[]{:S(2)}) %collective-permute-start.1) | collective-permute-done | bytes 53280 | tf_op jit(solution)/shard_map/ppermute | solution.py:621
  11.4 0.2 lat_merge1.1
  11.7 2.1 %collective-permute-start.2 = (f32[8,1152]{1,0:T(8,128)S(1)}, f32[8,1152]{1,0:T(8,128)S(1)}, u32[]{:S(2)}, u32[]{:S(2)}) collective-permute-start(f32[8,1152]{1,0:T(8,128)S(1)} %get-tuple-element.23.own.ext_in), channel_id=1, source_target_pairs={{0,1},{1,0},{2,3},{3,2},{4,5},{5,4},{6,7},{7,6},{8,9},{9,8},{10,11... | collective-permute-start | bytes 110600 | tf_op jit(solution)/shard_map/ppermute | solution.py:621
  13.7 1.9 %collective-permute-done.2.other = f32[8,1152]{1,0:T(8,128)S(1)} collective-permute-done((f32[8,1152]{1,0:T(8,128)S(1)}, f32[8,1152]{1,0:T(8,128)S(1)}, u32[]{:S(2)}, u32[]{:S(2)}) %collective-permute-start.2) | collective-permute-done | bytes 36896 | tf_op jit(solution)/shard_map/ppermute | solution.py:621
  15.7 0.1 lon_merge0.1
  15.8 2.1 %collective-permute-start.3 = (f32[8,1152]{1,0:T(8,128)S(1)}, f32[8,1152]{1,0:T(8,128)S(1)}, u32[]{:S(2)}, u32[]{:S(2)}) collective-permute-start(f32[8,1152]{1,0:T(8,128)S(1)} %get-tuple-element.24.own), channel_id=1, source_target_pairs={{0,2},{1,3},{2,0},{3,1},{4,6},{5,7},{6,4},{7,5},{8,10},{9,11},{10,... | collective-permute-start | bytes 110600 | tf_op jit(solution)/shard_map/ppermute | solution.py:621
  18.0 1.9 %collective-permute-done.3.other = f32[8,1152]{1,0:T(8,128)S(1)} collective-permute-done((f32[8,1152]{1,0:T(8,128)S(1)}, f32[8,1152]{1,0:T(8,128)S(1)}, u32[]{:S(2)}, u32[]{:S(2)}) %collective-permute-start.3) | collective-permute-done | bytes 36896 | tf_op jit(solution)/shard_map/ppermute | solution.py:621
  19.9 0.1 lon_merge1.1
  20.0 3.3 %collective-permute-start.4 = (f32[8,1152]{1,0:T(8,128)S(1)}, f32[8,1152]{1,0:T(8,128)S(1)}, u32[]{:S(2)}, u32[]{:S(2)}) collective-permute-start(f32[8,1152]{1,0:T(8,128)S(1)} %get-tuple-element.26.own), channel_id=1, source_target_pairs={{0,4},{1,5},{2,6},{3,7},{4,0},{5,1},{6,2},{7,3},{8,12},{9,13},{10,... | collective-permute-start | bytes 110600 | tf_op jit(solution)/shard_map/ppermute | solution.py:621
  23.3 1.5 %image.1.v = f32[256,2048]{1,0:T(8,128)S(1)} custom-call(f32[272,2048]{1,0:T(8,128)S(1)} %get-tuple-element.33.u, f32[256,2048]{1,0:T(8,128)S(1)} %get-tuple-element.34.w, f32[3,256,128]{2,1,0:T(8,128)S(1)} %get-tuple-element.35.coef, f32[8,2048]{1,0:T(8,128)S(1)} %get-tuple-element.22.ext_in.after_stage), custom_call_target="tpu_custom_call" | custom-call | flops 4194304 | bytes 6291456 | tf_op jit(solution)/shard_map/image/pallas_call | solution.py:636
  24.8 0.2 row_parts.1
  25.0 0.2 collective-permute-done.4.other
  25.3 2.6 %combine.1 = (f32[256,2048]{1,0:T(8,128)}, f32[256,2048]{1,0:T(8,128)}) custom-call(f32[8,1024]{1,0:T(8,128)S(1)} %get-tuple-element.19.tabs, f32[8,1152]{1,0:T(8,128)S(1)} %get-tuple-element.26.own, f32[8,1152]{1,0:T(8,128)S(1)} %collective-permute-done.4.other, f32[8,1024]{1,0:T(8,128)S(1)} %get-tuple-element.27.ext_in, ...), custom_call_target="tpu_custom_call" | custom-call | tf_op jit(solution)/shard_map/combine/pallas_call | solution.py:661
Async XLA Ops:
  4.7 1.4 %collective-permute-start = (f32[8,2432]{1,0:T(8,128)S(1)}, f32[8,2432]{1,0:T(8,128)S(1)}, u32[]{:S(2)}, u32[]{:S(2)}) collective-permute-start(f32[8,2432]{1,0:T(8,128)S(1)} %get-tuple-element.20.own.ext_in.edges), channel_id=1, source_target_pairs={{0,8},{8,0},{16,24},{24,16},{1,9},{9,1},{17,25},{25,17},{2,10},{10... | collective-permute-start | bytes 233480 | tf_op jit(solution)/shard_map/ppermute | solution.py:621
  6.4 5.1 %collective-permute-start.1 = (f32[8,1664]{1,0:T(8,128)S(1)}, f32[8,1664]{1,0:T(8,128)S(1)}, u32[]{:S(2)}, u32[]{:S(2)}) collective-permute-start(f32[8,1664]{1,0:T(8,128)S(1)} %get-tuple-element.21.own), channel_id=1, source_target_pairs={{0,16},{8,24},{16,0},{24,8},{1,17},{9,25},{17,1},{25,9},{2,18},{10... | collective-permute-start | bytes 159752 | tf_op jit(solution)/shard_map/ppermute | solution.py:621
  11.7 4.0 %collective-permute-start.2 = (f32[8,1152]{1,0:T(8,128)S(1)}, f32[8,1152]{1,0:T(8,128)S(1)}, u32[]{:S(2)}, u32[]{:S(2)}) collective-permute-start(f32[8,1152]{1,0:T(8,128)S(1)} %get-tuple-element.23.own.ext_in), channel_id=1, source_target_pairs={{0,1},{1,0},{2,3},{3,2},{4,5},{5,4},{6,7},{7,6},{8,9},{9,8},{10,11... | collective-permute-start | bytes 110600 | tf_op jit(solution)/shard_map/ppermute | solution.py:621
  15.8 4.1 %collective-permute-start.3 = (f32[8,1152]{1,0:T(8,128)S(1)}, f32[8,1152]{1,0:T(8,128)S(1)}, u32[]{:S(2)}, u32[]{:S(2)}) collective-permute-start(f32[8,1152]{1,0:T(8,128)S(1)} %get-tuple-element.24.own), channel_id=1, source_target_pairs={{0,2},{1,3},{2,0},{3,1},{4,6},{5,7},{6,4},{7,5},{8,10},{9,11},{10,... | collective-permute-start | bytes 110600 | tf_op jit(solution)/shard_map/ppermute | solution.py:621
  20.0 5.2 %collective-permute-start.4 = (f32[8,1152]{1,0:T(8,128)S(1)}, f32[8,1152]{1,0:T(8,128)S(1)}, u32[]{:S(2)}, u32[]{:S(2)}) collective-permute-start(f32[8,1152]{1,0:T(8,128)S(1)} %get-tuple-element.26.own), channel_id=1, source_target_pairs={{0,4},{1,5},{2,6},{3,7},{4,0},{5,1},{6,2},{7,3},{8,12},{9,13},{10,... | collective-permute-start | bytes 110600 | tf_op jit(solution)/shard_map/ppermute | solution.py:621

commit v5 on v4

--- a/solution.py
+++ b/solution.py
@@ -17,6 +17,8 @@
 LOADS = 4
 Z0, U0, V0, Z1, U1, V1, I0, I1 = range(8)
 EAST_WEST, UPPER, LOWER, INNER = range(4)
+WEST_KINDS, EAST_KINDS = 4, 5
+SCREENS = (0.05, 0.4, 2.0)
 
 
 def coefficient_table(total_rows):
@@ -56,23 +58,19 @@
 
 def line_of(field, at, tiles):
     zero = jnp.zeros((SUB, TILE), jnp.float32)
-    return [zero] + [field[pl.ds(at + SUB, SUB), columns(c)] for c in range(tiles)] + [zero]
+    return [zero] + [field[c, pl.ds(at + SUB, SUB), :] for c in range(tiles)] + [zero]
 
 
 def ahead_of(field, at, c, line, coeffs):
-    row_id = lax.broadcasted_iota(jnp.int32, (SUB, TILE), 0)
     here = line[c + 1]
-    later = field[pl.ds(at + 2 * SUB, SUB), columns(c)]
-    below = pltpu.roll(jnp.where(row_id == 0, later, here), SUB - 1, 0)
+    below = field[c, pl.ds(at + SUB + 1, SUB), :]
     right = pltpu.roll(jnp.where(lane_ids(SUB) == 0, line[c + 2], here), TILE - 1, 1)
     return right, coeffs[2] * below
 
 
 def behind_of(field, at, c, line, coeffs):
-    row_id = lax.broadcasted_iota(jnp.int32, (SUB, TILE), 0)
     here = line[c + 1]
-    prev = field[pl.ds(at, SUB), columns(c)]
-    above = pltpu.roll(jnp.where(row_id == SUB - 1, prev, here), 1, 0)
+    above = field[c, pl.ds(at + SUB - 1, SUB), :]
     left = pltpu.roll(jnp.where(lane_ids(SUB) == TILE - 1, line[c], here), 1, 1)
     return left, coeffs[1] * above
 
@@ -83,8 +81,20 @@
     return coeffs[0] * (right + left) + (above + below)
 
 
+def folded_tables(tabs, folded):
+    quarter = folded.shape[1] // 5
+    base = [tabs[i : i + 1, :] for i in (EAST_WEST, UPPER, LOWER)]
+    rows = [base[0], tabs[INNER : INNER + 1, :]]
+    rows += [1.0 / (screen + 2.0 * base[0] + base[1] + base[2]) for screen in SCREENS]
+    for i, row in enumerate(rows):
+        for q in range(4):
+            piece = row[:, q * quarter : (q + 1) * quarter]
+            folded[q : q + 1, i * quarter : (i + 1) * quarter] = piece
+            folded[q + 4 : q + 5, i * quarter : (i + 1) * quarter] = piece
+
+
 def local_kernel(
-    flags_in, source, z, u, w, pack, tabs, src, coef, inv, v_edge, flags, sems
+    flags_in, source, z, u, w, pack, tabs, src, coef, folded, inv, v_edge, flags, sems
 ):
     rows, cols = src.shape
     tiles = cols // TILE
@@ -100,6 +110,7 @@
         if i < 2:
             loads[-1].start()
     tabs[...] = coefficient_table(tabs.shape[1])
+    folded_tables(tabs[...], folded)
     start = pl.multiple_of(lax.axis_index("lat") * rows, rows)
     band = jnp.transpose(tabs[:, pl.ds(start, rows)])
     ew = wide(band[:, EAST_WEST : EAST_WEST + 1])
@@ -107,12 +118,12 @@
     lo = wide(band[:, LOWER : LOWER + 1])
     for i, values in enumerate((ew, up, lo)):
         coef[i] = values
-    for kind, screen in enumerate((0.05, 0.4, 2.0)):
+    for kind, screen in enumerate(SCREENS):
         inv[kind] = 1.0 / (screen + 2.0 * ew + up + lo)
-    nothing = jnp.zeros((SUB, cols), jnp.float32)
+    nothing = jnp.zeros((tiles, SUB, TILE), jnp.float32)
     for padded in (z, u):
-        padded[:SUB] = nothing
-        padded[rows + SUB :] = nothing
+        padded[:, :SUB, :] = nothing
+        padded[:, rows + SUB :, :] = nothing
     zero = jnp.zeros((SUB, TILE), jnp.float32)
     flag_copy.wait()
     kinds = [
@@ -128,7 +139,7 @@
         for c in range(tiles):
             b = src[pl.ds(at, SUB), columns(c)]
             value = b * inv[kind[c], pl.ds(at, SUB), :]
-            z[pl.ds(at + SUB, SUB), columns(c)] = value
+            z[c, pl.ds(at + SUB, SUB), :] = value
             part = part + b * value
         return (sums[0] + part,) + sums[1:]
 
@@ -141,7 +152,7 @@
             image = src[here_rows, columns(c)] - around(z, at, c, line, coeffs)
             scaled = image * inv[kind[c], here_rows, :]
             w[here_rows, columns(c)] = image
-            u[pl.ds(at + SUB, SUB), columns(c)] = scaled
+            u[c, pl.ds(at + SUB, SUB), :] = scaled
             part1 = part1 + line[c + 1] * image
             part2 = part2 + scaled * image
         return sums[0], sums[1] + part1, sums[2] + part2, sums[3]
@@ -184,10 +195,10 @@
     m0, m1, m2, m3 = sums
 
     last = rows - 1
-    pack[Z0 : Z0 + 1, :cols] = z[SUB : SUB + 1, :]
-    pack[U0 : U0 + 1, :cols] = u[SUB : SUB + 1, :]
-    pack[Z1 : Z1 + 1, :cols] = z[last + SUB : last + SUB + 1, :]
-    pack[U1 : U1 + 1, :cols] = u[last + SUB : last + SUB + 1, :]
+    for c in range(tiles):
+        for field, first_row, last_row in ((z, Z0, Z1), (u, U0, U1)):
+            pack[first_row : first_row + 1, columns(c)] = field[c, SUB : SUB + 1, :]
+            pack[last_row : last_row + 1, columns(c)] = field[c, last + SUB : last + SUB + 1, :]
     for at, v_row, place in ((0, V0, 0), (rows - SUB, V1, SUB - 1)):
         line = line_of(u, at, tiles)
         coeffs = [coef[i, at : at + SUB, :] for i in range(3)]
@@ -201,16 +212,15 @@
     for band_row in range(rows // TILE):
         here_rows = slice(band_row * TILE, (band_row + 1) * TILE)
         inner_rows = slice(band_row * TILE + SUB, (band_row + 1) * TILE + SUB)
-        east = slice(cols - TILE, cols)
         ids = lane_ids(TILE)
         mix = inv[kinds[band_row][-1], here_rows, :]
         mix = jnp.where(ids == I0, inv[kinds[band_row][0], here_rows, :], mix)
         mix = jnp.where(ids == V1, pltpu.roll(v_edge[here_rows, TILE:], V1 + 1, 1), mix)
-        mix = jnp.where(ids == U1, pltpu.roll(u[inner_rows, east], U1 + 1, 1), mix)
-        mix = jnp.where(ids == Z1, pltpu.roll(z[inner_rows, east], Z1 + 1, 1), mix)
+        mix = jnp.where(ids == U1, pltpu.roll(u[tiles - 1, inner_rows, :], U1 + 1, 1), mix)
+        mix = jnp.where(ids == Z1, pltpu.roll(z[tiles - 1, inner_rows, :], Z1 + 1, 1), mix)
         mix = jnp.where(ids == V0, pltpu.roll(v_edge[here_rows, :TILE], V0, 1), mix)
-        mix = jnp.where(ids == U0, pltpu.roll(u[inner_rows, :TILE], U0, 1), mix)
-        mix = jnp.where(ids == Z0, z[inner_rows, :TILE], mix)
+        mix = jnp.where(ids == U0, pltpu.roll(u[0, inner_rows, :], U0, 1), mix)
+        mix = jnp.where(ids == Z0, z[0, inner_rows, :], mix)
         at = cols + band_row * TILE
         pack[:, at : at + TILE] = jnp.transpose(mix)[:SUB, :]
 
@@ -218,6 +228,13 @@
     pack[:, at:] = zero
     for i, m in enumerate((m0, m1, m2, m3)):
         pack[i : i + 1, at:] = jnp.sum(m, axis=0, keepdims=True)
+    band_start = lax.axis_index("lat") * (rows // TILE)
+    for i, c in ((WEST_KINDS, 0), (EAST_KINDS, tiles - 1)):
+        line = jnp.zeros((1, TILE), jnp.float32)
+        for band_row in range(rows // TILE):
+            kind = jnp.full((1, TILE), kinds[band_row][c], jnp.int32).astype(jnp.float32)
+            line = jnp.where(lane_ids(1) == band_start + band_row, kind, line)
+        pack[i : i + 1, at:] = line
 
 
 def image_kernel(u, w, coef, after_stage, v):
@@ -298,7 +315,8 @@
         out[i + 1 : i + 2, at : at + TILE] += change
 
 
-def lat_kernel(stage, stages, cols, tabs, own, other, ext_in, out, ext):
+def lat_kernel(stage, stages, cols, tabs, own, other, ext_in, result, ext, *scratch):
+    out = scratch[0] if scratch else result
     facing = 0 < stage == stages - 1
     final = stage == stages - 1
     half = cols // 2
@@ -381,6 +399,15 @@
             lane == 0, v_bottom, jnp.where(lane == 1, -next_b * d_bottom, 0.0)
         )
 
+    if final:
+        quarter = 2 * height // 4
+        for i, row in enumerate((Z0, U0, V0, Z1, U1, V1)):
+            part = slice((i % 3) * quarter, (i % 3 + 1) * quarter)
+            for q in range(4):
+                to = q + 4 * (i // 3)
+                result[to : to + 1, part] = out[row : row + 1, q * quarter : (q + 1) * quarter]
+        result[:, 3 * quarter :] = out[:, 2 * height :]
+
     if stage == 0:
         ext[...] = jnp.zeros((SUB, cols), jnp.float32)
     else:
@@ -399,80 +426,100 @@
         ext[5:6, :] = ib
 
 
-def column_border(west, east, tabs):
-    height = west.shape[1] - TILE
-    zw, uw, vw, iw = (row_of(west, i, 0, height) for i in (Z1, U1, V1, I1))
-    ze, ue, ve, ie = (row_of(east, i, 0, height) for i in (Z0, U0, V0, I0))
-    ew = tabs[EAST_WEST : EAST_WEST + 1, :]
-    inner = tabs[INNER : INNER + 1, :]
-    to_w, to_e = -ew * ze, -ew * zw
-    dw, de = iw * to_w, ie * to_e
-    full_w, full_e = uw + dw, ue + de
-    first = 2.0 * fold(zw * to_w)
-    second = fold((2.0 * uw + dw) * to_w + (2.0 * ue + de) * to_e)
-    third = fold(
-        dw * (2.0 * vw + to_w)
-        + de * (2.0 * ve + to_e)
-        - 2.0 * inner * (dw * after(dw) + de * after(de))
-        - 2.0 * ew * full_w * full_e
+def halves(quarter):
+    return lax.broadcasted_iota(jnp.int32, (SUB, quarter), 0) < 4
+
+
+def column_border(west, east, folded):
+    quarter = (west.shape[1] - TILE) // 3
+    low = halves(quarter)
+    z, u, v = (
+        jnp.where(low, east[:, part], west[:, part])
+        for part in (slice(i * quarter, (i + 1) * quarter) for i in range(3))
     )
-    return (first, second, third), (zw, full_w), (ze, full_e)
-
-
-def lon_kernel(stage, tabs, own, other, ext_in, out, ext):
-    height = own.shape[1] - TILE
+    ew, inner, *inverses = (folded[:, i * quarter : (i + 1) * quarter] for i in range(5))
+    tiles = 4 * quarter // TILE
+    each = tiles // 4
+    east_kinds = jnp.broadcast_to(east[WEST_KINDS : WEST_KINDS + 1, 3 * quarter :], (SUB, TILE))
+    west_kinds = jnp.broadcast_to(west[EAST_KINDS : EAST_KINDS + 1, 3 * quarter :], (SUB, TILE))
+    kinds = jnp.where(halves(TILE), east_kinds, west_kinds)
+    sub = lax.broadcasted_iota(jnp.int32, (SUB, TILE), 0)
+    first = each * jnp.where(sub < 4, sub, sub - 4)
+    spread = []
+    for h in range(each):
+        here = jnp.where(lane_ids(SUB) == first + h, kinds, 0.0)
+        spread.append(wide(jnp.sum(here, axis=1, keepdims=True)))
+    kind = jnp.concatenate(spread, axis=1)
+    inv = jnp.where(kind < 0.5, inverses[0], jnp.where(kind < 1.5, inverses[1], inverses[2]))
+
+    def across(x):
+        return pltpu.roll(x, 4, 0)
+
+    e = -ew * across(z)
+    d = inv * e
+    full = u + d
+    moved = pltpu.roll(d, quarter - 1, 1)
+    along = jnp.where(lane_ids(SUB, quarter) == quarter - 1, pltpu.roll(moved, SUB - 1, 0), moved)
+    first_sum = fold(z * e)
+    second = fold((u + full) * e)
+    third = fold(d * (2.0 * v + e) - 2.0 * inner * d * along - ew * full * across(full))
+    changes = [jnp.sum(x, axis=0, keepdims=True) for x in (first_sum, second, third)]
+    return changes, jnp.concatenate([z, full], axis=1)
+
+
+def merge_tiles(west, east):
+    at = west.shape[1] - TILE
+    ids = lax.broadcasted_iota(jnp.int32, (SUB, TILE), 0)
+    kinds = jnp.where(ids == WEST_KINDS, west[:, at:], east[:, at:])
+    return jnp.where(ids < WEST_KINDS, west[:, at:] + east[:, at:], kinds)
+
+
+def keep_ext(ext, found, at_start, at_end):
+    @pl.when(at_end)
+    def _():
+        ext[:4, :] = found[:4, :]
+
+    @pl.when(at_start)
+    def _():
+        ext[4:, :] = found[4:, :]
+
+
+def lon_kernel(stage, folded, own, other, ext_in, out, ext):
+    at = own.shape[1] - TILE
     west, east, at_end, at_start = sides(own, other, lax.axis_index("lon"), stage)
-    changes, from_west, from_east = column_border(west, east, tabs)
-    ids = lax.broadcasted_iota(jnp.int32, (SUB, height), 0)
-    out[:, :height] = jnp.where((ids < Z1) | (ids == I0), west[:, :height], east[:, :height])
-    add_moments(out, height, west, east, changes)
+    changes, found = column_border(west, east, folded)
+    out[:, :at] = jnp.where(halves(at), west[:, :at], east[:, :at])
+    out[:, at:] = merge_tiles(west, east)
+    for i, change in enumerate(changes):
+        out[i + 1 : i + 2, at:] += change
     if stage == 0:
-        ext[...] = jnp.zeros((SUB, height), jnp.float32)
+        ext[...] = jnp.zeros(ext.shape, jnp.float32)
     else:
         ext[...] = ext_in[...]
-
-    @pl.when(at_start)
-    def _():
-        ext[0:1, :], ext[1:2, :] = from_west
-
-    @pl.when(at_end)
-    def _():
-        ext[2:3, :], ext[3:4, :] = from_east
+    keep_ext(ext, found, at_start, at_end)
 
 
 def last_kernel(
-    stage, chunk, tabs, own, other, ext_in, edges, row_parts, corner, src, z, u, w, v,
+    stage, chunk, tabs, folded, own, other, ext_in, edges, row_parts, corner, src, z, u, w, v,
     out_x, out_r, mom, ext, field_x, field_r, cols_t, sems,
 ):
     rows, cols = src.shape
-    height = own.shape[1] - TILE
+    height = tabs.shape[1]
     tiles = cols // TILE
     sectors = lax.axis_size("lon")
     index = lax.axis_index("lon")
     west, east, at_end, at_start = sides(own, other, index, stage)
-    changes, from_west, from_east = column_border(west, east, tabs)
-    wrap, round_west, round_east = column_border(east, west, tabs)
-    add_moments(mom, 0, west, east, [a + b for a, b in zip(changes, wrap)])
+    changes, found = column_border(west, east, folded)
+    wrap, round_found = column_border(east, west, folded)
+    mom[...] = merge_tiles(west, east)
+    for i, (change, other_change) in enumerate(zip(changes, wrap)):
+        mom[i + 1 : i + 2, :] += change + other_change
     if stage == 0:
-        ext[...] = jnp.zeros((SUB, height), jnp.float32)
+        ext[...] = jnp.zeros(ext.shape, jnp.float32)
     else:
         ext[...] = ext_in[...]
-
-    @pl.when(at_start)
-    def _():
-        ext[0:1, :], ext[1:2, :] = from_west
-
-    @pl.when(at_end)
-    def _():
-        ext[2:3, :], ext[3:4, :] = from_east
-
-    @pl.when(index == 0)
-    def _():
-        ext[0:1, :], ext[1:2, :] = round_west
-
-    @pl.when(index == sectors - 1)
-    def _():
-        ext[2:3, :], ext[3:4, :] = round_east
+    keep_ext(ext, found, at_start, at_end)
+    keep_ext(ext, round_found, index == 0, index == sectors - 1)
 
     sums = jnp.broadcast_to(jnp.sum(mom[...], axis=1, keepdims=True), (SUB, TILE))
     m0, m1, m2, m3 = (sums[i : i + 1, :] for i in range(4))
@@ -495,12 +542,12 @@
     near_r = jnp.concatenate([near1] * (rows // TILE), axis=1)
     far_r = jnp.concatenate([far1] * (rows // TILE), axis=1)
     mods = []
-    for z_row, inv_row in ((0, I0), (2, I1)):
-        e = -ew * ext[z_row : z_row + 1, here]
+    for ext_row, inv_row in ((4 + lat, I0), (lat, I1)):
+        e = -ew * ext[pl.ds(ext_row, 1), :rows]
         d = edges[inv_row : inv_row + 1, cols : cols + rows] * e
         above = jnp.where(row_lane == 0, 0.0, before(d))
         below = jnp.where(row_lane == rows - 1, 0.0, after(d))
-        dv = e - up * above - lo * below - ew * ext[z_row + 1 : z_row + 2, here]
+        dv = e - up * above - lo * below - ew * ext[pl.ds(ext_row, 1), rows:]
         mods += [-far_r * d, far_r * dv - near_r * e, -far_r * ew * d]
     mods += [jnp.zeros((1, rows), jnp.float32)] * 2
     cols_t[...] = jnp.transpose(jnp.concatenate(mods, axis=0))
@@ -508,19 +555,19 @@
     near_c = jnp.concatenate([near1] * tiles, axis=1)
     far_c = jnp.concatenate([far1] * tiles, axis=1)
     col_lane = lane_ids(1, cols)
-    clamp_n = pl.multiple_of(jnp.maximum(start - TILE, 0), TILE)
-    clamp_s = pl.multiple_of(jnp.minimum(start + rows, height - TILE), TILE)
     row_mods = []
-    for which, (clamp, place) in enumerate(((clamp_n, TILE - 1), (clamp_s, 0))):
-        next_ext = ext[:, pl.ds(clamp, TILE)]
+    for which, (band, place) in enumerate(
+        ((jnp.maximum(lat - 1, 0), rows - 1), (jnp.minimum(lat + 1, 3), 0))
+    ):
+        beyond = [ext[pl.ds(4 + band, 1), :rows], ext[pl.ds(band, 1), :rows]]
         d, e, dv, inner_d = (row_parts[4 * which + i : 4 * which + i + 1, :] for i in range(4))
 
-        def corner_of(row, lane):
-            cell = corner[which : which + 1, lane : lane + 1] * next_ext[row : row + 1, place : place + 1]
+        def corner_of(side, lane):
+            cell = corner[which : which + 1, lane : lane + 1] * beyond[side][:, place : place + 1]
             return wide(cell, cols)
 
         dv = dv + jnp.where(col_lane == 0, corner_of(0, 0), 0.0)
-        dv = dv + jnp.where(col_lane == cols - 1, corner_of(2, TILE - 1), 0.0)
+        dv = dv + jnp.where(col_lane == cols - 1, corner_of(1, TILE - 1), 0.0)
         row_mods.append((-far_c * d, far_c * dv - near_c * e, -far_c * inner_d))
 
     lane = lane_ids(SUB)
@@ -539,7 +586,7 @@
         lines = cols_t[here, :]
         for c in range(tiles):
             part = pl.ds(c * TILE, TILE)
-            x = near * z[pl.ds(at + SUB, SUB), part] - far * u[pl.ds(at + SUB, SUB), part]
+            x = near * z[c, pl.ds(at + SUB, SUB), :] - far * u[c, pl.ds(at + SUB, SUB), :]
             r = src[here, part] - near * w[here, part] + far * v[here, part]
             if c == 0:
                 x = x + jnp.where(lane == 0, wide(lines[:, 0:1]), 0.0)
@@ -598,17 +645,19 @@
     rows, cols = source.shape
     bands, sectors = lax.axis_size("lat"), lax.axis_size("lon")
     height = rows * bands
-    z, u, w, edges, tabs, src, coef = call(
+    assert bands == 4
+    z, u, w, edges, tabs, src, coef, folded = call(
         local_kernel,
         "local",
         [
-            shape(rows + 2 * SUB, cols),
-            shape(rows + 2 * SUB, cols),
+            shape(cols // TILE, rows + 2 * SUB, TILE),
+            shape(cols // TILE, rows + 2 * SUB, TILE),
             shape(rows, cols),
             shape(SUB, cols + rows + TILE),
             shape(SUB, height),
             shape(rows, cols),
             shape(3, rows, TILE),
+            shape(SUB, 5 * rows),
         ],
         [HBM_SPEC, HBM_SPEC],
         scratch=[pltpu.VMEM((3, rows, TILE), jnp.float32)]
@@ -629,8 +678,9 @@
         pack, row_ext = call(
             functools.partial(lat_kernel, stage, lat_stages, cols),
             f"lat_merge{stage}",
-            [shape(SUB, tall), shape(SUB, cols)],
+            [shape(SUB, 3 * rows + TILE if left == 0 else tall), shape(SUB, cols)],
             [VMEM_SPEC] * 4,
+            scratch=[pltpu.VMEM((SUB, tall), jnp.float32)] if left == 0 else (),
         )(tabs, pack, swap(pack, "lat", stage), row_ext)
         if stage == 0:
             v = call(
@@ -654,25 +704,25 @@
         pack, col_ext = call(
             functools.partial(lon_kernel, stage),
             f"lon_merge{stage}",
-            [shape(SUB, height + TILE), shape(SUB, height)],
+            [shape(SUB, 3 * rows + TILE), shape(SUB, 2 * rows)],
             [VMEM_SPEC] * 4,
-        )(tabs, pack, swap(pack, "lon", stage), col_ext)
+        )(folded, pack, swap(pack, "lon", stage), col_ext)
     stage = lon_stages - 1
     x, r = call(
         functools.partial(last_kernel, stage, 32),
         "combine",
         [shape(rows, cols), shape(rows, cols)],
-        [VMEM_SPEC] * 12,
+        [VMEM_SPEC] * 13,
         out_specs=[HBM_SPEC, HBM_SPEC],
         scratch=[
             pltpu.VMEM((SUB, TILE), jnp.float32),
-            pltpu.VMEM((SUB, height), jnp.float32),
+            pltpu.VMEM((SUB, 2 * rows), jnp.float32),
             pltpu.VMEM((rows, cols), jnp.float32),
             pltpu.VMEM((rows, cols), jnp.float32),
             pltpu.VMEM((rows, SUB), jnp.float32),
             pltpu.SemaphoreType.DMA((2,)),
         ],
-    )(tabs, pack, swap(pack, "lon", stage), col_ext, edges, row_parts, corner, src, z, u, w, v)
+    )(tabs, folded, pack, swap(pack, "lon", stage), col_ext, edges, row_parts, corner, src, z, u, w, v)
     return x, r
 
 

time: 28.1 us -> 27.4 us (0.975)
  Pallas kernels: 9.13 us -> 8.8 us
    pallas_call x1, Pallas kernels: 4.04 us -> 3.73 us  [per_device(): call(local_kernel, 'local', [shape(cols // TILE, rows + 2 * SUB, TILE), s...]
where the time goes in v5:
time: 27.4 us; the launch traced here: 27.2 us
  starting transfers between devices  10.8 us (39%)
  Pallas kernels  8.8 us (32%)
  waiting for transfers between devices  7 us (26%)
  between operations  0.66 us (2%)
    ppermute x5, starting transfers between devices, swap(): return lax.ppermute(pack, axis, [(i, i ^ 1 << stage) for i in range(count)])  10.8 us
    ppermute x5, waiting for transfers between devices, swap(): return lax.ppermute(pack, axis, [(i, i ^ 1 << stage) for i in range(count)])  7 us
    pallas_call x1, Pallas kernels, per_device(): call(local_kernel, 'local', [shape(cols // TILE, rows + 2 * SUB, TILE), s...  3.73 us
    pallas_call x1, Pallas kernels, per_device(): call(functools.partial(last_kernel, stage, 32), 'combine', [shape(rows, c...  2.63 us
    pallas_call x1, Pallas kernels, per_device(): call(image_kernel, 'image', [shape(rows, cols)], [VMEM_SPEC] * 3 + [ANY_S...  1.37 us
  transfers between devices with their start and end apart: 5, of which 5 were waited for; matrix products, arithmetic and copies ran while one was open for 0% of the time, Pallas kernels for 6%

profile of v5, /device:TPU:0, one launch (start us, length us, event | category | flops | bytes accessed | tf_op | source)
XLA Modules:
  0.0 27.2 jit_solution(2906077076856691180)
XLA Ops:
  0.6 3.7 %local.1 = (f32[16,272,128]{2,1,0:T(8,128)S(1)}, f32[16,272,128]{2,1,0:T(8,128)S(1)}, f32[256,2048]{1,0:T(8,128)S(1)}, f32[8,2432]{1,0:T(8,128)S(1)}, f32[8,1024...) custom-call(s32[2,16]{1,0:T(2,128)} %flags_in.1, f32[256,2048]{1,0:T(8,128)} %source.1), custom_call_target="tpu_custom_call" | custom-call | tf_op jit(solution)/shard_map/local/pallas_call | solution.py:649
  4.4 0.5 %collective-permute-start = (f32[8,2432]{1,0:T(8,128)S(1)}, f32[8,2432]{1,0:T(8,128)S(1)}, u32[]{:S(2)}, u32[]{:S(2)}) collective-permute-start(f32[8,2432]{1,0:T(8,128)S(1)} %get-tuple-element.22.own.ext_in.edges), channel_id=1, source_target_pairs={{0,8},{8,0},{16,24},{24,16},{1,9},{9,1},{17,25},{25,17},{2,10},{10... | collective-permute-start | bytes 233480 | tf_op jit(solution)/shard_map/ppermute | solution.py:670
  4.9 0.9 %collective-permute-done.other = f32[8,2432]{1,0:T(8,128)S(1)} collective-permute-done((f32[8,2432]{1,0:T(8,128)S(1)}, f32[8,2432]{1,0:T(8,128)S(1)}, u32[]{:S(2)}, u32[]{:S(2)}) %collective-permute-start) | collective-permute-done | bytes 77856 | tf_op jit(solution)/shard_map/ppermute | solution.py:670
  5.8 0.3 lat_merge0.1
  6.1 2.9 %collective-permute-start.1 = (f32[8,1664]{1,0:T(8,128)S(1)}, f32[8,1664]{1,0:T(8,128)S(1)}, u32[]{:S(2)}, u32[]{:S(2)}) collective-permute-start(f32[8,1664]{1,0:T(8,128)S(1)} %get-tuple-element.23.own), channel_id=1, source_target_pairs={{0,16},{8,24},{16,0},{24,8},{1,17},{9,25},{17,1},{25,9},{2,18},{10... | collective-permute-start | bytes 159752 | tf_op jit(solution)/shard_map/ppermute | solution.py:670
  9.0 2.1 %collective-permute-done.1.other = f32[8,1664]{1,0:T(8,128)S(1)} collective-permute-done((f32[8,1664]{1,0:T(8,128)S(1)}, f32[8,1664]{1,0:T(8,128)S(1)}, u32[]{:S(2)}, u32[]{:S(2)}) %collective-permute-start.1) | collective-permute-done | bytes 53280 | tf_op jit(solution)/shard_map/ppermute | solution.py:670
  11.1 0.2 lat_merge1.1
  11.4 2.1 %collective-permute-start.2 = (f32[8,896]{1,0:T(8,128)S(1)}, f32[8,896]{1,0:T(8,128)S(1)}, u32[]{:S(2)}, u32[]{:S(2)}) collective-permute-start(f32[8,896]{1,0:T(8,128)S(1)} %get-tuple-element.25.own.ext_in), channel_id=1, source_target_pairs={{0,1},{1,0},{2,3},{3,2},{4,5},{5,4},{6,7},{7,6},{8,9},{9,8},{10,11... | collective-permute-start | bytes 86024 | tf_op jit(solution)/shard_map/ppermute | solution.py:670
  13.4 1.9 %collective-permute-done.2.other = f32[8,896]{1,0:T(8,128)S(1)} collective-permute-done((f32[8,896]{1,0:T(8,128)S(1)}, f32[8,896]{1,0:T(8,128)S(1)}, u32[]{:S(2)}, u32[]{:S(2)}) %collective-permute-start.2) | collective-permute-done | bytes 28704 | tf_op jit(solution)/shard_map/ppermute | solution.py:670
  15.3 0.2 lon_merge0.1
  15.5 2.1 %collective-permute-start.3 = (f32[8,896]{1,0:T(8,128)S(1)}, f32[8,896]{1,0:T(8,128)S(1)}, u32[]{:S(2)}, u32[]{:S(2)}) collective-permute-start(f32[8,896]{1,0:T(8,128)S(1)} %get-tuple-element.26.own), channel_id=1, source_target_pairs={{0,2},{1,3},{2,0},{3,1},{4,6},{5,7},{6,4},{7,5},{8,10},{9,11},{10,... | collective-permute-start | bytes 86024 | tf_op jit(solution)/shard_map/ppermute | solution.py:670
  17.6 1.9 %collective-permute-done.3.other = f32[8,896]{1,0:T(8,128)S(1)} collective-permute-done((f32[8,896]{1,0:T(8,128)S(1)}, f32[8,896]{1,0:T(8,128)S(1)}, u32[]{:S(2)}, u32[]{:S(2)}) %collective-permute-start.3) | collective-permute-done | bytes 28704 | tf_op jit(solution)/shard_map/ppermute | solution.py:670
  19.5 0.2 lon_merge1.1
  19.6 3.1 %collective-permute-start.4 = (f32[8,896]{1,0:T(8,128)S(1)}, f32[8,896]{1,0:T(8,128)S(1)}, u32[]{:S(2)}, u32[]{:S(2)}) collective-permute-start(f32[8,896]{1,0:T(8,128)S(1)} %get-tuple-element.28.own), channel_id=1, source_target_pairs={{0,4},{1,5},{2,6},{3,7},{4,0},{5,1},{6,2},{7,3},{8,12},{9,13},{10,... | collective-permute-start | bytes 86024 | tf_op jit(solution)/shard_map/ppermute | solution.py:670
  22.8 1.4 %image.1.v = f32[256,2048]{1,0:T(8,128)S(1)} custom-call(f32[16,272,128]{2,1,0:T(8,128)S(1)} %get-tuple-element.35.u, f32[256,2048]{1,0:T(8,128)S(1)} %get-tuple-element.36.w, f32[3,256,128]{2,1,0:T(8,128)S(1)} %get-tuple-element.37.coef, f32[8,2048]{1,0:T(8,128)S(1)} %get-tuple-element.24.ext_in.after_stage), custom_call_target="tpu_custom_call" | custom-call | flops 4194304 | bytes 6291456 | tf_op jit(solution)/shard_map/image/pallas_call | solution.py:686
  24.1 0.2 row_parts.1
  24.4 0.2 collective-permute-done.4.other
  24.6 2.6 %combine.1 = (f32[256,2048]{1,0:T(8,128)}, f32[256,2048]{1,0:T(8,128)}) custom-call(f32[8,1024]{1,0:T(8,128)S(1)} %get-tuple-element.20.tabs, f32[8,1280]{1,0:T(8,128)S(1)} %get-tuple-element.21.folded, f32[8,896]{1,0:T(8,128)S(1)} %get-tuple-element.28.own, f32[8,896]{1,0:T(8,128)S(1)} %collective-permute-done.4.other, ...), custom_call_target="tpu_custom_call" | custom-call | tf_op jit(solution)/shard_map/combine/pallas_call | solution.py:711
Async XLA Ops:
  4.4 1.4 %collective-permute-start = (f32[8,2432]{1,0:T(8,128)S(1)}, f32[8,2432]{1,0:T(8,128)S(1)}, u32[]{:S(2)}, u32[]{:S(2)}) collective-permute-start(f32[8,2432]{1,0:T(8,128)S(1)} %get-tuple-element.22.own.ext_in.edges), channel_id=1, source_target_pairs={{0,8},{8,0},{16,24},{24,16},{1,9},{9,1},{17,25},{25,17},{2,10},{10... | collective-permute-start | bytes 233480 | tf_op jit(solution)/shard_map/ppermute | solution.py:670
  6.1 5.1 %collective-permute-start.1 = (f32[8,1664]{1,0:T(8,128)S(1)}, f32[8,1664]{1,0:T(8,128)S(1)}, u32[]{:S(2)}, u32[]{:S(2)}) collective-permute-start(f32[8,1664]{1,0:T(8,128)S(1)} %get-tuple-element.23.own), channel_id=1, source_target_pairs={{0,16},{8,24},{16,0},{24,8},{1,17},{9,25},{17,1},{25,9},{2,18},{10... | collective-permute-start | bytes 159752 | tf_op jit(solution)/shard_map/ppermute | solution.py:670
  11.4 3.9 %collective-permute-start.2 = (f32[8,896]{1,0:T(8,128)S(1)}, f32[8,896]{1,0:T(8,128)S(1)}, u32[]{:S(2)}, u32[]{:S(2)}) collective-permute-start(f32[8,896]{1,0:T(8,128)S(1)} %get-tuple-element.25.own.ext_in), channel_id=1, source_target_pairs={{0,1},{1,0},{2,3},{3,2},{4,5},{5,4},{6,7},{7,6},{8,9},{9,8},{10,11... | collective-permute-start | bytes 86024 | tf_op jit(solution)/shard_map/ppermute | solution.py:670
  15.5 4.0 %collective-permute-start.3 = (f32[8,896]{1,0:T(8,128)S(1)}, f32[8,896]{1,0:T(8,128)S(1)}, u32[]{:S(2)}, u32[]{:S(2)}) collective-permute-start(f32[8,896]{1,0:T(8,128)S(1)} %get-tuple-element.26.own), channel_id=1, source_target_pairs={{0,2},{1,3},{2,0},{3,1},{4,6},{5,7},{6,4},{7,5},{8,10},{9,11},{10,... | collective-permute-start | bytes 86024 | tf_op jit(solution)/shard_map/ppermute | solution.py:670
  19.6 5.0 %collective-permute-start.4 = (f32[8,896]{1,0:T(8,128)S(1)}, f32[8,896]{1,0:T(8,128)S(1)}, u32[]{:S(2)}, u32[]{:S(2)}) collective-permute-start(f32[8,896]{1,0:T(8,128)S(1)} %get-tuple-element.28.own), channel_id=1, source_target_pairs={{0,4},{1,5},{2,6},{3,7},{4,0},{5,1},{6,2},{7,3},{8,12},{9,13},{10,... | collective-permute-start | bytes 86024 | tf_op jit(solution)/shard_map/ppermute | solution.py:670

commit v6 on v5

--- a/solution.py
+++ b/solution.py
@@ -79,6 +79,27 @@
     right, below = ahead_of(field, at, c, line, coeffs)
     left, above = behind_of(field, at, c, line, coeffs)
     return coeffs[0] * (right + left) + (above + below)
+
+
+def fold_place(row, c, eighth):
+    sub, at = divmod(c * TILE, eighth)
+    at += row * eighth
+    return slice(sub, sub + 1), slice(at, at + TILE)
+
+
+def next_cell(row):
+    moved = pltpu.roll(row, row.shape[1] - 1, 1)
+    ids = lane_ids(SUB, row.shape[1])
+    return jnp.where(ids == row.shape[1] - 1, pltpu.roll(moved, SUB - 1, 0), moved)
+
+
+def last_cell(row):
+    moved = pltpu.roll(row, 1, 1)
+    return jnp.where(lane_ids(SUB, row.shape[1]) == 0, pltpu.roll(moved, 1, 0), moved)
+
+
+def cell_ids(width):
+    return lax.broadcasted_iota(jnp.int32, (SUB, width), 0) * width + lane_ids(SUB, width)
 
 
 def folded_tables(tabs, folded):
@@ -195,19 +216,22 @@
     m0, m1, m2, m3 = sums
 
     last = rows - 1
+    def put(row, c, value):
+        sub, lanes = fold_place(row, c, cols // SUB)
+        pack[sub, lanes] = value
+
     for c in range(tiles):
         for field, first_row, last_row in ((z, Z0, Z1), (u, U0, U1)):
-            pack[first_row : first_row + 1, columns(c)] = field[c, SUB : SUB + 1, :]
-            pack[last_row : last_row + 1, columns(c)] = field[c, last + SUB : last + SUB + 1, :]
+            put(first_row, c, field[c, SUB : SUB + 1, :])
+            put(last_row, c, field[c, last + SUB : last + SUB + 1, :])
+        put(I0, c, inv[kinds[0][c], :1, :])
+        put(I1, c, inv[kinds[-1][c], last:, :])
     for at, v_row, place in ((0, V0, 0), (rows - SUB, V1, SUB - 1)):
         line = line_of(u, at, tiles)
         coeffs = [coef[i, at : at + SUB, :] for i in range(3)]
         for c in range(tiles):
             image = w[at : at + SUB, columns(c)] - around(u, at, c, line, coeffs)
-            pack[v_row : v_row + 1, columns(c)] = image[place : place + 1, :]
-    for c in range(tiles):
-        pack[I0 : I0 + 1, c * TILE : (c + 1) * TILE] = inv[kinds[0][c], :1, :]
-        pack[I1 : I1 + 1, c * TILE : (c + 1) * TILE] = inv[kinds[-1][c], last:, :]
+            put(v_row, c, image[place : place + 1, :])
 
     for band_row in range(rows // TILE):
         here_rows = slice(band_row * TILE, (band_row + 1) * TILE)
@@ -256,10 +280,11 @@
 
 
 def row_kernel(rows, tabs, edges, row_ext, parts, corner):
-    cols = row_ext.shape[1]
+    eighth = row_ext.shape[1] // 6
+    cols = eighth * SUB
     height = tabs.shape[1]
     start = pl.multiple_of(lax.axis_index("lat") * rows, rows)
-    col_lane = lane_ids(1, cols)
+    cell = cell_ids(eighth)
     first = tabs[:, pl.ds(start, TILE)]
     final = tabs[:, pl.ds(start + rows - TILE, TILE)]
     tab_n = tabs[:, pl.ds(pl.multiple_of(jnp.maximum(start - TILE, 0), TILE), TILE)]
@@ -274,22 +299,30 @@
             cross_row, inner_row, inv_row = LOWER, UPPER, I1
 
         def scalar(tab, row, place):
-            return wide(tab[row : row + 1, place : place + 1], cols)
+            return jnp.broadcast_to(tab[row : row + 1, place : place + 1], (SUB, eighth))
+
+        def beyond(i):
+            return row_ext[:, (at + i) * eighth : (at + i + 1) * eighth]
 
         cross = scalar(own_tab, cross_row, lane)
         inner = scalar(own_tab, inner_row, lane)
         ew_own = scalar(own_tab, EAST_WEST, lane)
         ew_next = scalar(next_tab, EAST_WEST, next_lane)
-        e = -cross * row_ext[at : at + 1, :]
-        d = edges[inv_row : inv_row + 1, :cols] * e
-        right = jnp.where(col_lane == cols - 1, 0.0, after(d))
-        left = jnp.where(col_lane == 0, 0.0, before(d))
-        dv = e - ew_own * (right + left) - cross * row_ext[at + 1 : at + 2, :]
+        e = -cross * beyond(0)
+        d = edges[:, inv_row * eighth : (inv_row + 1) * eighth] * e
+        right = jnp.where(cell == cols - 1, 0.0, next_cell(d))
+        left = jnp.where(cell == 0, 0.0, last_cell(d))
+        dv = e - ew_own * (right + left) - cross * beyond(1)
         for i, row in enumerate((d, e, dv, inner * d)):
-            parts[4 * which + i : 4 * which + i + 1, :] = row
-        k = cross * ew_next * row_ext[at + 2 : at + 3, :]
+            to = 4 * which + i
+            for c in range(cols // TILE):
+                sub, lanes = fold_place(0, c, eighth)
+                parts[to : to + 1, columns(c)] = row[sub, lanes]
+        k = cross * ew_next * beyond(2)
         ids = lane_ids(1)
-        corner[which : which + 1, :] = jnp.where(ids == 0, k[:, :TILE], k[:, cols - TILE :])
+        corner[which : which + 1, :] = jnp.where(
+            ids == 0, k[:1, :TILE], k[SUB - 1 :, eighth - TILE :]
+        )
 
 
 def sides(own, other, index, stage):
@@ -319,8 +352,8 @@
     out = scratch[0] if scratch else result
     facing = 0 < stage == stages - 1
     final = stage == stages - 1
-    half = cols // 2
-    span = half if facing else cols
+    eighth = cols // SUB
+    span = 4 * eighth if facing else cols
     height = own.shape[1] - span - TILE
     index = lax.axis_index("lat")
     top, bottom, at_end, at_start = sides(own, other, index, stage)
@@ -328,50 +361,46 @@
     border = pl.multiple_of((lax.div(index, 2 * size) * 2 * size + size) * (height // size), TILE)
     low = tabs[:, pl.ds(border, TILE)]
     high = tabs[:, pl.ds(border - TILE, TILE)]
-    cross = wide(low[UPPER : UPPER + 1, :1], cols)
+    cross = jnp.broadcast_to(low[UPPER : UPPER + 1, :1], (SUB, eighth))
     ew_b = wide(low[EAST_WEST : EAST_WEST + 1, :1])
     ew_t = wide(high[EAST_WEST : EAST_WEST + 1, TILE - 1 :])
     next_b = wide(low[LOWER : LOWER + 1, :1])
     next_t = wide(high[UPPER : UPPER + 1, TILE - 1 :])
 
-    if facing:
-
-        def joined(pack, i):
-            return jnp.concatenate(
-                [row_of(pack, i, 0, half), row_of(pack, i + 4, 0, half)], axis=1
-            )
-
-        zt, ut, vt, it = (joined(top, i) for i in range(4))
-        zb, ub, vb, ib = (joined(bottom, i) for i in range(4))
-    else:
-        zt, ut, vt, it = (row_of(top, i, 0, cols) for i in (Z1, U1, V1, I1))
-        zb, ub, vb, ib = (row_of(bottom, i, 0, cols) for i in (Z0, U0, V0, I0))
+    def block(pack, i):
+        return pack[:, i * eighth : (i + 1) * eighth]
+
+    zt, ut, vt, it = (block(top, i) for i in (range(4) if facing else (Z1, U1, V1, I1)))
+    zb, ub, vb, ib = (block(bottom, i) for i in (range(4) if facing else (Z0, U0, V0, I0)))
     et, eb = -cross * zb, -cross * zt
     dt, db = it * et, ib * eb
     full_t, full_b = ut + dt, ub + db
-    inside = lane_ids(1, cols) < cols - 1
-    pair_t = jnp.where(inside, dt * after(dt), 0.0)
-    pair_b = jnp.where(inside, db * after(db), 0.0)
-    twice = fold(zt * et)
-    second = fold((2.0 * ut + dt) * et + (2.0 * ub + db) * eb)
-    third = fold(dt * (2.0 * vt + et) + db * (2.0 * vb + eb) - 2.0 * cross * full_t * full_b)
-    third = third - 2.0 * (ew_t * fold(pair_t) + ew_b * fold(pair_b))
+    inside = cell_ids(eighth) < cols - 1
+    pair_t = jnp.where(inside, dt * next_cell(dt), 0.0)
+    pair_b = jnp.where(inside, db * next_cell(db), 0.0)
+
+    def total(x):
+        return jnp.sum(fold(x), axis=0, keepdims=True)
+
+    twice = total(zt * et)
+    second = total((2.0 * ut + dt) * et + (2.0 * ub + db) * eb)
+    third = total(dt * (2.0 * vt + et) + db * (2.0 * vb + eb) - 2.0 * cross * full_t * full_b)
+    third = third - 2.0 * (ew_t * total(pair_t) + ew_b * total(pair_b))
 
     if final:
         base = 0
     elif stage + 1 == stages - 1:
-        base = half
+        base = 4 * eighth
         up_next = lax.rem(lax.div(index, 2 * size), 2) == 0
         for i, (first_row, last_row) in enumerate(((Z0, Z1), (U0, U1), (V0, V1), (I0, I1))):
-            row = jnp.where(
-                up_next, row_of(bottom, last_row, 0, cols), row_of(top, first_row, 0, cols)
+            out[:, i * eighth : (i + 1) * eighth] = jnp.where(
+                up_next, block(bottom, last_row), block(top, first_row)
             )
-            out[i : i + 1, :half] = row[:, :half]
-            out[i + 4 : i + 5, :half] = row[:, half:]
     else:
         base = cols
-        ids = lax.broadcasted_iota(jnp.int32, (SUB, cols), 0)
-        out[:, :cols] = jnp.where((ids < Z1) | (ids == I0), top[:, :cols], bottom[:, :cols])
+        for i in range(8):
+            side = top if i in (Z0, U0, V0, I0) else bottom
+            out[:, i * eighth : (i + 1) * eighth] = block(side, i)
     out[:, base : base + height] = top[:, span : span + height]
     out[:, base + height : base + 2 * height] = bottom[:, span : span + height]
     add_moments(out, base + 2 * height, top, bottom, (2.0 * twice, second, third))
@@ -379,11 +408,12 @@
     lane = lane_ids(1)
     upper_at = base + height - TILE
     lower_at = base + height
-    c = cross[:, :TILE]
+    c = cross[:1, :TILE]
     for edge, inner, u_row, v_row in ((0, 1, U0, V0), (cols - 1, cols - 2, U1, V1)):
 
         def pick(row, place):
-            return wide(row[:, place : place + 1])
+            sub, lane_at = divmod(place, eighth)
+            return wide(row[sub : sub + 1, lane_at : lane_at + 1])
 
         d_top, d_bottom = pick(dt, edge), pick(db, edge)
         v_top = pick(et, edge) - ew_t * pick(dt, inner) - c * pick(full_b, edge)
@@ -409,21 +439,22 @@
         result[:, 3 * quarter :] = out[:, 2 * height :]
 
     if stage == 0:
-        ext[...] = jnp.zeros((SUB, cols), jnp.float32)
+        ext[...] = jnp.zeros(ext.shape, jnp.float32)
     else:
         ext[...] = ext_in[...]
 
+    def keep(first_block, values):
+        for i, value in enumerate(values):
+            at = (first_block + i) * eighth
+            ext[:, at : at + eighth] = value
+
     @pl.when(at_start)
     def _():
-        ext[0:1, :] = zt
-        ext[1:2, :] = full_t
-        ext[2:3, :] = it
+        keep(0, (zt, full_t, it))
 
     @pl.when(at_end)
     def _():
-        ext[3:4, :] = zb
-        ext[4:5, :] = full_b
-        ext[5:6, :] = ib
+        keep(3, (zb, full_b, ib))
 
 
 def halves(quarter):
@@ -458,8 +489,7 @@
     e = -ew * across(z)
     d = inv * e
     full = u + d
-    moved = pltpu.roll(d, quarter - 1, 1)
-    along = jnp.where(lane_ids(SUB, quarter) == quarter - 1, pltpu.roll(moved, SUB - 1, 0), moved)
+    along = next_cell(d)
     first_sum = fold(z * e)
     second = fold((u + full) * e)
     third = fold(d * (2.0 * v + e) - 2.0 * inner * d * along - ew * full * across(full))
@@ -678,7 +708,7 @@
         pack, row_ext = call(
             functools.partial(lat_kernel, stage, lat_stages, cols),
             f"lat_merge{stage}",
-            [shape(SUB, 3 * rows + TILE if left == 0 else tall), shape(SUB, cols)],
+            [shape(SUB, 3 * rows + TILE if left == 0 else tall), shape(SUB, 6 * cols // SUB)],
             [VMEM_SPEC] * 4,
             scratch=[pltpu.VMEM((SUB, tall), jnp.float32)] if left == 0 else (),
         )(tabs, pack, swap(pack, "lat", stage), row_ext)

time: 27.4 us -> 27.2 us (level)
  no operation moved by 1% of the time
where the time goes in v6:
time: 27.2 us; the launch traced here: 27 us
  starting transfers between devices  10.8 us (40%)
  Pallas kernels  8.57 us (32%)
  waiting for transfers between devices  7.05 us (26%)
  between operations  0.67 us (2%)
    ppermute x5, starting transfers between devices, swap(): return lax.ppermute(pack, axis, [(i, i ^ 1 << stage) for i in range(count)])  10.8 us
    ppermute x5, waiting for transfers between devices, swap(): return lax.ppermute(pack, axis, [(i, i ^ 1 << stage) for i in range(count)])  7.05 us
    pallas_call x1, Pallas kernels, per_device(): call(local_kernel, 'local', [shape(cols // TILE, rows + 2 * SUB, TILE), s...  3.73 us
    pallas_call x1, Pallas kernels, per_device(): call(functools.partial(last_kernel, stage, 32), 'combine', [shape(rows, c...  2.63 us
    pallas_call x1, Pallas kernels, per_device(): call(image_kernel, 'image', [shape(rows, cols)], [VMEM_SPEC] * 3 + [ANY_S...  1.37 us
  transfers between devices with their start and end apart: 5, of which 5 were waited for; matrix products, arithmetic and copies ran while one was open for 0% of the time, Pallas kernels for 6%

profile of v6, /device:TPU:0, one launch (start us, length us, event | category | flops | bytes accessed | tf_op | source)
XLA Modules:
  0.0 27.0 jit_solution(17362748580356624986)
XLA Ops:
  0.6 3.7 %local.1 = (f32[16,272,128]{2,1,0:T(8,128)S(1)}, f32[16,272,128]{2,1,0:T(8,128)S(1)}, f32[256,2048]{1,0:T(8,128)S(1)}, f32[8,2432]{1,0:T(8,128)S(1)}, f32[8,1024...) custom-call(s32[2,16]{1,0:T(2,128)} %flags_in.1, f32[256,2048]{1,0:T(8,128)} %source.1), custom_call_target="tpu_custom_call" | custom-call | tf_op jit(solution)/shard_map/local/pallas_call | solution.py:679
  4.4 0.5 %collective-permute-start = (f32[8,2432]{1,0:T(8,128)S(1)}, f32[8,2432]{1,0:T(8,128)S(1)}, u32[]{:S(2)}, u32[]{:S(2)}) collective-permute-start(f32[8,2432]{1,0:T(8,128)S(1)} %get-tuple-element.22.own.ext_in.edges), channel_id=1, source_target_pairs={{0,8},{8,0},{16,24},{24,16},{1,9},{9,1},{17,25},{25,17},{2,10},{10... | collective-permute-start | bytes 233480 | tf_op jit(solution)/shard_map/ppermute | solution.py:700
  4.9 0.9 %collective-permute-done.other = f32[8,2432]{1,0:T(8,128)S(1)} collective-permute-done((f32[8,2432]{1,0:T(8,128)S(1)}, f32[8,2432]{1,0:T(8,128)S(1)}, u32[]{:S(2)}, u32[]{:S(2)}) %collective-permute-start) | collective-permute-done | bytes 77856 | tf_op jit(solution)/shard_map/ppermute | solution.py:700
  5.8 0.1 lat_merge0.1
  6.0 2.9 %collective-permute-start.1 = (f32[8,1664]{1,0:T(8,128)S(1)}, f32[8,1664]{1,0:T(8,128)S(1)}, u32[]{:S(2)}, u32[]{:S(2)}) collective-permute-start(f32[8,1664]{1,0:T(8,128)S(1)} %get-tuple-element.23.own), channel_id=1, source_target_pairs={{0,16},{8,24},{16,0},{24,8},{1,17},{9,25},{17,1},{25,9},{2,18},{10... | collective-permute-start | bytes 159752 | tf_op jit(solution)/shard_map/ppermute | solution.py:700
  8.9 2.1 %collective-permute-done.1.other = f32[8,1664]{1,0:T(8,128)S(1)} collective-permute-done((f32[8,1664]{1,0:T(8,128)S(1)}, f32[8,1664]{1,0:T(8,128)S(1)}, u32[]{:S(2)}, u32[]{:S(2)}) %collective-permute-start.1) | collective-permute-done | bytes 53280 | tf_op jit(solution)/shard_map/ppermute | solution.py:700
  11.0 0.2 lat_merge1.1
  11.2 2.1 %collective-permute-start.2 = (f32[8,896]{1,0:T(8,128)S(1)}, f32[8,896]{1,0:T(8,128)S(1)}, u32[]{:S(2)}, u32[]{:S(2)}) collective-permute-start(f32[8,896]{1,0:T(8,128)S(1)} %get-tuple-element.25.own.ext_in), channel_id=1, source_target_pairs={{0,1},{1,0},{2,3},{3,2},{4,5},{5,4},{6,7},{7,6},{8,9},{9,8},{10,11... | collective-permute-start | bytes 86024 | tf_op jit(solution)/shard_map/ppermute | solution.py:700
  13.3 1.9 %collective-permute-done.2.other = f32[8,896]{1,0:T(8,128)S(1)} collective-permute-done((f32[8,896]{1,0:T(8,128)S(1)}, f32[8,896]{1,0:T(8,128)S(1)}, u32[]{:S(2)}, u32[]{:S(2)}) %collective-permute-start.2) | collective-permute-done | bytes 28704 | tf_op jit(solution)/shard_map/ppermute | solution.py:700
  15.1 0.2 lon_merge0.1
  15.3 2.1 %collective-permute-start.3 = (f32[8,896]{1,0:T(8,128)S(1)}, f32[8,896]{1,0:T(8,128)S(1)}, u32[]{:S(2)}, u32[]{:S(2)}) collective-permute-start(f32[8,896]{1,0:T(8,128)S(1)} %get-tuple-element.26.own), channel_id=1, source_target_pairs={{0,2},{1,3},{2,0},{3,1},{4,6},{5,7},{6,4},{7,5},{8,10},{9,11},{10,... | collective-permute-start | bytes 86024 | tf_op jit(solution)/shard_map/ppermute | solution.py:700
  17.4 1.9 %collective-permute-done.3.other = f32[8,896]{1,0:T(8,128)S(1)} collective-permute-done((f32[8,896]{1,0:T(8,128)S(1)}, f32[8,896]{1,0:T(8,128)S(1)}, u32[]{:S(2)}, u32[]{:S(2)}) %collective-permute-start.3) | collective-permute-done | bytes 28704 | tf_op jit(solution)/shard_map/ppermute | solution.py:700
  19.3 0.2 lon_merge1.1
  19.4 3.1 %collective-permute-start.4 = (f32[8,896]{1,0:T(8,128)S(1)}, f32[8,896]{1,0:T(8,128)S(1)}, u32[]{:S(2)}, u32[]{:S(2)}) collective-permute-start(f32[8,896]{1,0:T(8,128)S(1)} %get-tuple-element.28.own), channel_id=1, source_target_pairs={{0,4},{1,5},{2,6},{3,7},{4,0},{5,1},{6,2},{7,3},{8,12},{9,13},{10,... | collective-permute-start | bytes 86024 | tf_op jit(solution)/shard_map/ppermute | solution.py:700
  22.6 1.4 %image.1.v = f32[256,2048]{1,0:T(8,128)S(1)} custom-call(f32[16,272,128]{2,1,0:T(8,128)S(1)} %get-tuple-element.35.u, f32[256,2048]{1,0:T(8,128)S(1)} %get-tuple-element.36.w, f32[3,256,128]{2,1,0:T(8,128)S(1)} %get-tuple-element.37.coef, f32[8,1536]{1,0:T(8,128)S(1)} %get-tuple-element.24.ext_in.after_stage), custom_call_target="tpu_custom_call" | custom-call | flops 4194304 | bytes 6291456 | tf_op jit(solution)/shard_map/image/pallas_call | solution.py:716
  23.9 0.2 row_parts.1
  24.1 0.3 %collective-permute-done.4.other = f32[8,896]{1,0:T(8,128)S(1)} collective-permute-done((f32[8,896]{1,0:T(8,128)S(1)}, f32[8,896]{1,0:T(8,128)S(1)}, u32[]{:S(2)}, u32[]{:S(2)}) %collective-permute-start.4) | collective-permute-done | bytes 28704 | tf_op jit(solution)/shard_map/ppermute | solution.py:700
  24.4 2.6 %combine.1 = (f32[256,2048]{1,0:T(8,128)}, f32[256,2048]{1,0:T(8,128)}) custom-call(f32[8,1024]{1,0:T(8,128)S(1)} %get-tuple-element.20.tabs, f32[8,1280]{1,0:T(8,128)S(1)} %get-tuple-element.21.folded, f32[8,896]{1,0:T(8,128)S(1)} %get-tuple-element.28.own, f32[8,896]{1,0:T(8,128)S(1)} %collective-permute-done.4.other, ...), custom_call_target="tpu_custom_call" | custom-call | tf_op jit(solution)/shard_map/combine/pallas_call | solution.py:741
Async XLA Ops:
  4.4 1.4 %collective-permute-start = (f32[8,2432]{1,0:T(8,128)S(1)}, f32[8,2432]{1,0:T(8,128)S(1)}, u32[]{:S(2)}, u32[]{:S(2)}) collective-permute-start(f32[8,2432]{1,0:T(8,128)S(1)} %get-tuple-element.22.own.ext_in.edges), channel_id=1, source_target_pairs={{0,8},{8,0},{16,24},{24,16},{1,9},{9,1},{17,25},{25,17},{2,10},{10... | collective-permute-start | bytes 233480 | tf_op jit(solution)/shard_map/ppermute | solution.py:700
  6.0 5.1 %collective-permute-start.1 = (f32[8,1664]{1,0:T(8,128)S(1)}, f32[8,1664]{1,0:T(8,128)S(1)}, u32[]{:S(2)}, u32[]{:S(2)}) collective-permute-start(f32[8,1664]{1,0:T(8,128)S(1)} %get-tuple-element.23.own), channel_id=1, source_target_pairs={{0,16},{8,24},{16,0},{24,8},{1,17},{9,25},{17,1},{25,9},{2,18},{10... | collective-permute-start | bytes 159752 | tf_op jit(solution)/shard_map/ppermute | solution.py:700
  11.2 3.9 %collective-permute-start.2 = (f32[8,896]{1,0:T(8,128)S(1)}, f32[8,896]{1,0:T(8,128)S(1)}, u32[]{:S(2)}, u32[]{:S(2)}) collective-permute-start(f32[8,896]{1,0:T(8,128)S(1)} %get-tuple-element.25.own.ext_in), channel_id=1, source_target_pairs={{0,1},{1,0},{2,3},{3,2},{4,5},{5,4},{6,7},{7,6},{8,9},{9,8},{10,11... | collective-permute-start | bytes 86024 | tf_op jit(solution)/shard_map/ppermute | solution.py:700
  15.3 4.0 %collective-permute-start.3 = (f32[8,896]{1,0:T(8,128)S(1)}, f32[8,896]{1,0:T(8,128)S(1)}, u32[]{:S(2)}, u32[]{:S(2)}) collective-permute-start(f32[8,896]{1,0:T(8,128)S(1)} %get-tuple-element.26.own), channel_id=1, source_target_pairs={{0,2},{1,3},{2,0},{3,1},{4,6},{5,7},{6,4},{7,5},{8,10},{9,11},{10,... | collective-permute-start | bytes 86024 | tf_op jit(solution)/shard_map/ppermute | solution.py:700
  19.4 5.0 %collective-permute-start.4 = (f32[8,896]{1,0:T(8,128)S(1)}, f32[8,896]{1,0:T(8,128)S(1)}, u32[]{:S(2)}, u32[]{:S(2)}) collective-permute-start(f32[8,896]{1,0:T(8,128)S(1)} %get-tuple-element.28.own), channel_id=1, source_target_pairs={{0,4},{1,5},{2,6},{3,7},{4,0},{5,1},{6,2},{7,3},{8,12},{9,13},{10,... | collective-permute-start | bytes 86024 | tf_op jit(solution)/shard_map/ppermute | solution.py:700

commit v7 on v6

--- a/solution.py
+++ b/solution.py
@@ -544,13 +544,6 @@
     mom[...] = merge_tiles(west, east)
     for i, (change, other_change) in enumerate(zip(changes, wrap)):
         mom[i + 1 : i + 2, :] += change + other_change
-    if stage == 0:
-        ext[...] = jnp.zeros(ext.shape, jnp.float32)
-    else:
-        ext[...] = ext_in[...]
-    keep_ext(ext, found, at_start, at_end)
-    keep_ext(ext, round_found, index == 0, index == sectors - 1)
-
     sums = jnp.broadcast_to(jnp.sum(mom[...], axis=1, keepdims=True), (SUB, TILE))
     m0, m1, m2, m3 = (sums[i : i + 1, :] for i in range(4))
     alpha = m0 / m1
@@ -561,6 +554,53 @@
     near1, far1 = alpha + beta * grow, alpha * beta
     near = jnp.broadcast_to(near1, (SUB, TILE))
     far = jnp.broadcast_to(far1, (SUB, TILE))
+
+    lane = lane_ids(SUB)
+    blocks = chunk // SUB
+    parts = rows // chunk
+    early = (1, 2)
+    copies = []
+
+    def send(i, first_col, last_col):
+        here = pl.ds(i * chunk, chunk), pl.ds(first_col, last_col - first_col)
+        for k, (field, out) in enumerate(((field_x, out_x), (field_r, out_r))):
+            copies.append(pltpu.make_async_copy(field.at[here], out.at[here], sems.at[k]))
+            copies[-1].start()
+
+    def cells(at, c):
+        here, part = pl.ds(at, SUB), columns(c)
+        x = near * z[c, pl.ds(at + SUB, SUB), :] - far * u[c, pl.ds(at + SUB, SUB), :]
+        r = src[here, part] - near * w[here, part] + far * v[here, part]
+        return x, r
+
+    def inner(i):
+        for at in range(i * chunk, (i + 1) * chunk, SUB):
+            for c in range(1, tiles - 1):
+                x, r = cells(at, c)
+                field_x[at : at + SUB, columns(c)] = x
+                field_r[at : at + SUB, columns(c)] = r
+
+    def edge(i):
+        for at in range(i * chunk, (i + 1) * chunk, SUB):
+            lines = cols_t[at : at + SUB, :]
+            for c, k, end, inside in ((0, 0, 0, 1), (tiles - 1, 3, TILE - 1, TILE - 2)):
+                x, r = cells(at, c)
+                dx, dr, dr_next = (wide(lines[:, k + j : k + j + 1]) for j in range(3))
+                field_x[at : at + SUB, columns(c)] = x + jnp.where(lane == end, dx, 0.0)
+                field_r[at : at + SUB, columns(c)] = r + jnp.where(
+                    lane == end, dr, jnp.where(lane == inside, dr_next, 0.0)
+                )
+
+    for i in early:
+        inner(i)
+        send(i, TILE, cols - TILE)
+
+    if stage == 0:
+        ext[...] = jnp.zeros(ext.shape, jnp.float32)
+    else:
+        ext[...] = ext_in[...]
+    keep_ext(ext, found, at_start, at_end)
+    keep_ext(ext, round_found, index == 0, index == sectors - 1)
 
     lat = lax.axis_index("lat")
     start = pl.multiple_of(lat * rows, rows)
@@ -600,43 +640,9 @@
         dv = dv + jnp.where(col_lane == cols - 1, corner_of(1, TILE - 1), 0.0)
         row_mods.append((-far_c * d, far_c * dv - near_c * e, -far_c * inner_d))
 
-    lane = lane_ids(SUB)
-    blocks = chunk // SUB
-
-    def copies(i):
-        part = pl.ds(pl.multiple_of(i * chunk, SUB), chunk)
-        return (
-            pltpu.make_async_copy(field_x.at[part, :], out_x.at[part, :], sems.at[0]),
-            pltpu.make_async_copy(field_r.at[part, :], out_r.at[part, :], sems.at[1]),
-        )
-
-    def step(k, carry):
-        at = pl.multiple_of(k * SUB, SUB)
-        here = pl.ds(at, SUB)
-        lines = cols_t[here, :]
-        for c in range(tiles):
-            part = pl.ds(c * TILE, TILE)
-            x = near * z[c, pl.ds(at + SUB, SUB), :] - far * u[c, pl.ds(at + SUB, SUB), :]
-            r = src[here, part] - near * w[here, part] + far * v[here, part]
-            if c == 0:
-                x = x + jnp.where(lane == 0, wide(lines[:, 0:1]), 0.0)
-                r = r + jnp.where(
-                    lane == 0, wide(lines[:, 1:2]), jnp.where(lane == 1, wide(lines[:, 2:3]), 0.0)
-                )
-            if c == tiles - 1:
-                x = x + jnp.where(lane == TILE - 1, wide(lines[:, 3:4]), 0.0)
-                r = r + jnp.where(
-                    lane == TILE - 1,
-                    wide(lines[:, 4:5]),
-                    jnp.where(lane == TILE - 2, wide(lines[:, 5:6]), 0.0),
-                )
-            field_x[here, part] = x
-            field_r[here, part] = r
-        return carry
-
-    parts = rows // chunk
-    for i in list(range(1, parts)) + [0]:
-        lax.fori_loop(i * blocks, (i + 1) * blocks, step, 0, unroll=blocks)
+    for i in [i for i in range(1, parts) if i not in early] + [0]:
+        inner(i)
+        edge(i)
         if i == 0:
             dx, dr, dr_next = row_mods[0]
             field_x[0:1, :] += dx
@@ -647,11 +653,14 @@
             field_x[rows - 1 : rows, :] += dx
             field_r[rows - 1 : rows, :] += dr
             field_r[rows - 2 : rows - 1, :] += dr_next
-        for copy in copies(i):
-            copy.start()
-    for i in range(parts):
-        for copy in copies(i):
-            copy.wait()
+        send(i, 0, cols)
+        if i == parts - 1:
+            for k in early:
+                edge(k)
+                send(k, 0, TILE)
+                send(k, cols - TILE, cols)
+    for copy in copies:
+        copy.wait()
 
 
 def shape(*dims):

time: 27.2 us -> 27.1 us (level)
  no operation moved by 1% of the time
where the time goes in v7:
time: 27.1 us; the launch traced here: 27 us
  starting transfers between devices  10.8 us (40%)
  Pallas kernels  8.52 us (31%)
  waiting for transfers between devices  7.05 us (26%)
  between operations  0.67 us (2%)
    ppermute x5, starting transfers between devices, swap(): return lax.ppermute(pack, axis, [(i, i ^ 1 << stage) for i in range(count)])  10.8 us
    ppermute x5, waiting for transfers between devices, swap(): return lax.ppermute(pack, axis, [(i, i ^ 1 << stage) for i in range(count)])  7.05 us
    pallas_call x1, Pallas kernels, per_device(): call(local_kernel, 'local', [shape(cols // TILE, rows + 2 * SUB, TILE), s...  3.73 us
    pallas_call x1, Pallas kernels, per_device(): call(functools.partial(last_kernel, stage, 32), 'combine', [shape(rows, c...  2.57 us
    pallas_call x1, Pallas kernels, per_device(): call(image_kernel, 'image', [shape(rows, cols)], [VMEM_SPEC] * 3 + [ANY_S...  1.37 us
  transfers between devices with their start and end apart: 5, of which 5 were waited for; matrix products, arithmetic and copies ran while one was open for 0% of the time, Pallas kernels for 6%

profile of v7, /device:TPU:0, one launch (start us, length us, event | category | flops | bytes accessed | tf_op | source)
XLA Modules:
  0.0 27.0 jit_solution(15228041983544093205)
XLA Ops:
  0.6 3.7 %local.1 = (f32[16,272,128]{2,1,0:T(8,128)S(1)}, f32[16,272,128]{2,1,0:T(8,128)S(1)}, f32[256,2048]{1,0:T(8,128)S(1)}, f32[8,2432]{1,0:T(8,128)S(1)}, f32[8,1024...) custom-call(s32[2,16]{1,0:T(2,128)} %flags_in.1, f32[256,2048]{1,0:T(8,128)} %source.1), custom_call_target="tpu_custom_call" | custom-call | tf_op jit(solution)/shard_map/local/pallas_call | solution.py:688
  4.4 0.5 %collective-permute-start = (f32[8,2432]{1,0:T(8,128)S(1)}, f32[8,2432]{1,0:T(8,128)S(1)}, u32[]{:S(2)}, u32[]{:S(2)}) collective-permute-start(f32[8,2432]{1,0:T(8,128)S(1)} %get-tuple-element.22.own.ext_in.edges), channel_id=1, source_target_pairs={{0,8},{8,0},{16,24},{24,16},{1,9},{9,1},{17,25},{25,17},{2,10},{10... | collective-permute-start | bytes 233480 | tf_op jit(solution)/shard_map/ppermute | solution.py:709
  4.9 0.9 %collective-permute-done.other = f32[8,2432]{1,0:T(8,128)S(1)} collective-permute-done((f32[8,2432]{1,0:T(8,128)S(1)}, f32[8,2432]{1,0:T(8,128)S(1)}, u32[]{:S(2)}, u32[]{:S(2)}) %collective-permute-start) | collective-permute-done | bytes 77856 | tf_op jit(solution)/shard_map/ppermute | solution.py:709
  5.8 0.1 lat_merge0.1
  6.0 2.9 %collective-permute-start.1 = (f32[8,1664]{1,0:T(8,128)S(1)}, f32[8,1664]{1,0:T(8,128)S(1)}, u32[]{:S(2)}, u32[]{:S(2)}) collective-permute-start(f32[8,1664]{1,0:T(8,128)S(1)} %get-tuple-element.23.own), channel_id=1, source_target_pairs={{0,16},{8,24},{16,0},{24,8},{1,17},{9,25},{17,1},{25,9},{2,18},{10... | collective-permute-start | bytes 159752 | tf_op jit(solution)/shard_map/ppermute | solution.py:709
  8.9 2.1 %collective-permute-done.1.other = f32[8,1664]{1,0:T(8,128)S(1)} collective-permute-done((f32[8,1664]{1,0:T(8,128)S(1)}, f32[8,1664]{1,0:T(8,128)S(1)}, u32[]{:S(2)}, u32[]{:S(2)}) %collective-permute-start.1) | collective-permute-done | bytes 53280 | tf_op jit(solution)/shard_map/ppermute | solution.py:709
  11.0 0.2 lat_merge1.1
  11.2 2.1 %collective-permute-start.2 = (f32[8,896]{1,0:T(8,128)S(1)}, f32[8,896]{1,0:T(8,128)S(1)}, u32[]{:S(2)}, u32[]{:S(2)}) collective-permute-start(f32[8,896]{1,0:T(8,128)S(1)} %get-tuple-element.25.own.ext_in), channel_id=1, source_target_pairs={{0,1},{1,0},{2,3},{3,2},{4,5},{5,4},{6,7},{7,6},{8,9},{9,8},{10,11... | collective-permute-start | bytes 86024 | tf_op jit(solution)/shard_map/ppermute | solution.py:709
  13.3 1.9 %collective-permute-done.2.other = f32[8,896]{1,0:T(8,128)S(1)} collective-permute-done((f32[8,896]{1,0:T(8,128)S(1)}, f32[8,896]{1,0:T(8,128)S(1)}, u32[]{:S(2)}, u32[]{:S(2)}) %collective-permute-start.2) | collective-permute-done | bytes 28704 | tf_op jit(solution)/shard_map/ppermute | solution.py:709
  15.1 0.2 lon_merge0.1
  15.3 2.1 %collective-permute-start.3 = (f32[8,896]{1,0:T(8,128)S(1)}, f32[8,896]{1,0:T(8,128)S(1)}, u32[]{:S(2)}, u32[]{:S(2)}) collective-permute-start(f32[8,896]{1,0:T(8,128)S(1)} %get-tuple-element.26.own), channel_id=1, source_target_pairs={{0,2},{1,3},{2,0},{3,1},{4,6},{5,7},{6,4},{7,5},{8,10},{9,11},{10,... | collective-permute-start | bytes 86024 | tf_op jit(solution)/shard_map/ppermute | solution.py:709
  17.4 1.9 %collective-permute-done.3.other = f32[8,896]{1,0:T(8,128)S(1)} collective-permute-done((f32[8,896]{1,0:T(8,128)S(1)}, f32[8,896]{1,0:T(8,128)S(1)}, u32[]{:S(2)}, u32[]{:S(2)}) %collective-permute-start.3) | collective-permute-done | bytes 28704 | tf_op jit(solution)/shard_map/ppermute | solution.py:709
  19.3 0.2 lon_merge1.1
  19.4 3.1 %collective-permute-start.4 = (f32[8,896]{1,0:T(8,128)S(1)}, f32[8,896]{1,0:T(8,128)S(1)}, u32[]{:S(2)}, u32[]{:S(2)}) collective-permute-start(f32[8,896]{1,0:T(8,128)S(1)} %get-tuple-element.28.own), channel_id=1, source_target_pairs={{0,4},{1,5},{2,6},{3,7},{4,0},{5,1},{6,2},{7,3},{8,12},{9,13},{10,... | collective-permute-start | bytes 86024 | tf_op jit(solution)/shard_map/ppermute | solution.py:709
  22.6 1.4 %image.1.v = f32[256,2048]{1,0:T(8,128)S(1)} custom-call(f32[16,272,128]{2,1,0:T(8,128)S(1)} %get-tuple-element.35.u, f32[256,2048]{1,0:T(8,128)S(1)} %get-tuple-element.36.w, f32[3,256,128]{2,1,0:T(8,128)S(1)} %get-tuple-element.37.coef, f32[8,1536]{1,0:T(8,128)S(1)} %get-tuple-element.24.ext_in.after_stage), custom_call_target="tpu_custom_call" | custom-call | flops 4194304 | bytes 6291456 | tf_op jit(solution)/shard_map/image/pallas_call | solution.py:725
  23.9 0.2 row_parts.1
  24.1 0.3 %collective-permute-done.4.other = f32[8,896]{1,0:T(8,128)S(1)} collective-permute-done((f32[8,896]{1,0:T(8,128)S(1)}, f32[8,896]{1,0:T(8,128)S(1)}, u32[]{:S(2)}, u32[]{:S(2)}) %collective-permute-start.4) | collective-permute-done | bytes 28704 | tf_op jit(solution)/shard_map/ppermute | solution.py:709
  24.4 2.6 %combine.1 = (f32[256,2048]{1,0:T(8,128)}, f32[256,2048]{1,0:T(8,128)}) custom-call(f32[8,1024]{1,0:T(8,128)S(1)} %get-tuple-element.20.tabs, f32[8,1280]{1,0:T(8,128)S(1)} %get-tuple-element.21.folded, f32[8,896]{1,0:T(8,128)S(1)} %get-tuple-element.28.own, f32[8,896]{1,0:T(8,128)S(1)} %collective-permute-done.4.other, ...), custom_call_target="tpu_custom_call" | custom-call | tf_op jit(solution)/shard_map/combine/pallas_call | solution.py:750
Async XLA Ops:
  4.4 1.4 %collective-permute-start = (f32[8,2432]{1,0:T(8,128)S(1)}, f32[8,2432]{1,0:T(8,128)S(1)}, u32[]{:S(2)}, u32[]{:S(2)}) collective-permute-start(f32[8,2432]{1,0:T(8,128)S(1)} %get-tuple-element.22.own.ext_in.edges), channel_id=1, source_target_pairs={{0,8},{8,0},{16,24},{24,16},{1,9},{9,1},{17,25},{25,17},{2,10},{10... | collective-permute-start | bytes 233480 | tf_op jit(solution)/shard_map/ppermute | solution.py:709
  6.0 5.1 %collective-permute-start.1 = (f32[8,1664]{1,0:T(8,128)S(1)}, f32[8,1664]{1,0:T(8,128)S(1)}, u32[]{:S(2)}, u32[]{:S(2)}) collective-permute-start(f32[8,1664]{1,0:T(8,128)S(1)} %get-tuple-element.23.own), channel_id=1, source_target_pairs={{0,16},{8,24},{16,0},{24,8},{1,17},{9,25},{17,1},{25,9},{2,18},{10... | collective-permute-start | bytes 159752 | tf_op jit(solution)/shard_map/ppermute | solution.py:709
  11.2 3.9 %collective-permute-start.2 = (f32[8,896]{1,0:T(8,128)S(1)}, f32[8,896]{1,0:T(8,128)S(1)}, u32[]{:S(2)}, u32[]{:S(2)}) collective-permute-start(f32[8,896]{1,0:T(8,128)S(1)} %get-tuple-element.25.own.ext_in), channel_id=1, source_target_pairs={{0,1},{1,0},{2,3},{3,2},{4,5},{5,4},{6,7},{7,6},{8,9},{9,8},{10,11... | collective-permute-start | bytes 86024 | tf_op jit(solution)/shard_map/ppermute | solution.py:709
  15.3 4.0 %collective-permute-start.3 = (f32[8,896]{1,0:T(8,128)S(1)}, f32[8,896]{1,0:T(8,128)S(1)}, u32[]{:S(2)}, u32[]{:S(2)}) collective-permute-start(f32[8,896]{1,0:T(8,128)S(1)} %get-tuple-element.26.own), channel_id=1, source_target_pairs={{0,2},{1,3},{2,0},{3,1},{4,6},{5,7},{6,4},{7,5},{8,10},{9,11},{10,... | collective-permute-start | bytes 86024 | tf_op jit(solution)/shard_map/ppermute | solution.py:709
  19.4 5.0 %collective-permute-start.4 = (f32[8,896]{1,0:T(8,128)S(1)}, f32[8,896]{1,0:T(8,128)S(1)}, u32[]{:S(2)}, u32[]{:S(2)}) collective-permute-start(f32[8,896]{1,0:T(8,128)S(1)} %get-tuple-element.28.own), channel_id=1, source_target_pairs={{0,4},{1,5},{2,6},{3,7},{4,0},{5,1},{6,2},{7,3},{8,12},{9,13},{10,... | collective-permute-start | bytes 86024 | tf_op jit(solution)/shard_map/ppermute | solution.py:709

commit v8 on v6

--- a/solution.py
+++ b/solution.py
@@ -635,7 +635,7 @@
         return carry
 
     parts = rows // chunk
-    for i in list(range(1, parts)) + [0]:
+    for i in range(parts):
         lax.fori_loop(i * blocks, (i + 1) * blocks, step, 0, unroll=blocks)
         if i == 0:
             dx, dr, dr_next = row_mods[0]

time: 27.2 us -> 27.2 us (level)
  no operation moved by 1% of the time
where the time goes in v8:
time: 27.2 us; the launch traced here: 27 us
  starting transfers between devices  10.8 us (40%)
  Pallas kernels  8.56 us (31%)
  waiting for transfers between devices  7.05 us (26%)
  between operations  0.67 us (2%)
    ppermute x5, starting transfers between devices, swap(): return lax.ppermute(pack, axis, [(i, i ^ 1 << stage) for i in range(count)])  10.8 us
    ppermute x5, waiting for transfers between devices, swap(): return lax.ppermute(pack, axis, [(i, i ^ 1 << stage) for i in range(count)])  7.05 us
    pallas_call x1, Pallas kernels, per_device(): call(local_kernel, 'local', [shape(cols // TILE, rows + 2 * SUB, TILE), s...  3.73 us
    pallas_call x1, Pallas kernels, per_device(): call(functools.partial(last_kernel, stage, 32), 'combine', [shape(rows, c...  2.61 us
    pallas_call x1, Pallas kernels, per_device(): call(image_kernel, 'image', [shape(rows, cols)], [VMEM_SPEC] * 3 + [ANY_S...  1.37 us
  transfers between devices with their start and end apart: 5, of which 5 were waited for; matrix products, arithmetic and copies ran while one was open for 0% of the time, Pallas kernels for 6%

profile of v8, /device:TPU:0, one launch (start us, length us, event | category | flops | bytes accessed | tf_op | source)
XLA Modules:
  0.0 27.0 jit_solution(6986809493261245811)
XLA Ops:
  0.6 3.7 %local.1 = (f32[16,272,128]{2,1,0:T(8,128)S(1)}, f32[16,272,128]{2,1,0:T(8,128)S(1)}, f32[256,2048]{1,0:T(8,128)S(1)}, f32[8,2432]{1,0:T(8,128)S(1)}, f32[8,1024...) custom-call(s32[2,16]{1,0:T(2,128)} %flags_in.1, f32[256,2048]{1,0:T(8,128)} %source.1), custom_call_target="tpu_custom_call" | custom-call | tf_op jit(solution)/shard_map/local/pallas_call | solution.py:679
  4.4 0.5 %collective-permute-start = (f32[8,2432]{1,0:T(8,128)S(1)}, f32[8,2432]{1,0:T(8,128)S(1)}, u32[]{:S(2)}, u32[]{:S(2)}) collective-permute-start(f32[8,2432]{1,0:T(8,128)S(1)} %get-tuple-element.22.own.ext_in.edges), channel_id=1, source_target_pairs={{0,8},{8,0},{16,24},{24,16},{1,9},{9,1},{17,25},{25,17},{2,10},{10... | collective-permute-start | bytes 233480 | tf_op jit(solution)/shard_map/ppermute | solution.py:700
  4.9 0.9 %collective-permute-done.other = f32[8,2432]{1,0:T(8,128)S(1)} collective-permute-done((f32[8,2432]{1,0:T(8,128)S(1)}, f32[8,2432]{1,0:T(8,128)S(1)}, u32[]{:S(2)}, u32[]{:S(2)}) %collective-permute-start) | collective-permute-done | bytes 77856 | tf_op jit(solution)/shard_map/ppermute | solution.py:700
  5.8 0.1 lat_merge0.1
  6.0 2.9 %collective-permute-start.1 = (f32[8,1664]{1,0:T(8,128)S(1)}, f32[8,1664]{1,0:T(8,128)S(1)}, u32[]{:S(2)}, u32[]{:S(2)}) collective-permute-start(f32[8,1664]{1,0:T(8,128)S(1)} %get-tuple-element.23.own), channel_id=1, source_target_pairs={{0,16},{8,24},{16,0},{24,8},{1,17},{9,25},{17,1},{25,9},{2,18},{10... | collective-permute-start | bytes 159752 | tf_op jit(solution)/shard_map/ppermute | solution.py:700
  8.9 2.1 %collective-permute-done.1.other = f32[8,1664]{1,0:T(8,128)S(1)} collective-permute-done((f32[8,1664]{1,0:T(8,128)S(1)}, f32[8,1664]{1,0:T(8,128)S(1)}, u32[]{:S(2)}, u32[]{:S(2)}) %collective-permute-start.1) | collective-permute-done | bytes 53280 | tf_op jit(solution)/shard_map/ppermute | solution.py:700
  11.0 0.2 lat_merge1.1
  11.2 2.1 %collective-permute-start.2 = (f32[8,896]{1,0:T(8,128)S(1)}, f32[8,896]{1,0:T(8,128)S(1)}, u32[]{:S(2)}, u32[]{:S(2)}) collective-permute-start(f32[8,896]{1,0:T(8,128)S(1)} %get-tuple-element.25.own.ext_in), channel_id=1, source_target_pairs={{0,1},{1,0},{2,3},{3,2},{4,5},{5,4},{6,7},{7,6},{8,9},{9,8},{10,11... | collective-permute-start | bytes 86024 | tf_op jit(solution)/shard_map/ppermute | solution.py:700
  13.3 1.9 %collective-permute-done.2.other = f32[8,896]{1,0:T(8,128)S(1)} collective-permute-done((f32[8,896]{1,0:T(8,128)S(1)}, f32[8,896]{1,0:T(8,128)S(1)}, u32[]{:S(2)}, u32[]{:S(2)}) %collective-permute-start.2) | collective-permute-done | bytes 28704 | tf_op jit(solution)/shard_map/ppermute | solution.py:700
  15.1 0.2 lon_merge0.1
  15.3 2.1 %collective-permute-start.3 = (f32[8,896]{1,0:T(8,128)S(1)}, f32[8,896]{1,0:T(8,128)S(1)}, u32[]{:S(2)}, u32[]{:S(2)}) collective-permute-start(f32[8,896]{1,0:T(8,128)S(1)} %get-tuple-element.26.own), channel_id=1, source_target_pairs={{0,2},{1,3},{2,0},{3,1},{4,6},{5,7},{6,4},{7,5},{8,10},{9,11},{10,... | collective-permute-start | bytes 86024 | tf_op jit(solution)/shard_map/ppermute | solution.py:700
  17.4 1.9 %collective-permute-done.3.other = f32[8,896]{1,0:T(8,128)S(1)} collective-permute-done((f32[8,896]{1,0:T(8,128)S(1)}, f32[8,896]{1,0:T(8,128)S(1)}, u32[]{:S(2)}, u32[]{:S(2)}) %collective-permute-start.3) | collective-permute-done | bytes 28704 | tf_op jit(solution)/shard_map/ppermute | solution.py:700
  19.3 0.2 lon_merge1.1
  19.4 3.1 %collective-permute-start.4 = (f32[8,896]{1,0:T(8,128)S(1)}, f32[8,896]{1,0:T(8,128)S(1)}, u32[]{:S(2)}, u32[]{:S(2)}) collective-permute-start(f32[8,896]{1,0:T(8,128)S(1)} %get-tuple-element.28.own), channel_id=1, source_target_pairs={{0,4},{1,5},{2,6},{3,7},{4,0},{5,1},{6,2},{7,3},{8,12},{9,13},{10,... | collective-permute-start | bytes 86024 | tf_op jit(solution)/shard_map/ppermute | solution.py:700
  22.6 1.4 %image.1.v = f32[256,2048]{1,0:T(8,128)S(1)} custom-call(f32[16,272,128]{2,1,0:T(8,128)S(1)} %get-tuple-element.35.u, f32[256,2048]{1,0:T(8,128)S(1)} %get-tuple-element.36.w, f32[3,256,128]{2,1,0:T(8,128)S(1)} %get-tuple-element.37.coef, f32[8,1536]{1,0:T(8,128)S(1)} %get-tuple-element.24.ext_in.after_stage), custom_call_target="tpu_custom_call" | custom-call | flops 4194304 | bytes 6291456 | tf_op jit(solution)/shard_map/image/pallas_call | solution.py:716
  23.9 0.2 row_parts.1
  24.1 0.3 %collective-permute-done.4.other = f32[8,896]{1,0:T(8,128)S(1)} collective-permute-done((f32[8,896]{1,0:T(8,128)S(1)}, f32[8,896]{1,0:T(8,128)S(1)}, u32[]{:S(2)}, u32[]{:S(2)}) %collective-permute-start.4) | collective-permute-done | bytes 28704 | tf_op jit(solution)/shard_map/ppermute | solution.py:700
  24.4 2.6 %combine.1 = (f32[256,2048]{1,0:T(8,128)}, f32[256,2048]{1,0:T(8,128)}) custom-call(f32[8,1024]{1,0:T(8,128)S(1)} %get-tuple-element.20.tabs, f32[8,1280]{1,0:T(8,128)S(1)} %get-tuple-element.21.folded, f32[8,896]{1,0:T(8,128)S(1)} %get-tuple-element.28.own, f32[8,896]{1,0:T(8,128)S(1)} %collective-permute-done.4.other, ...), custom_call_target="tpu_custom_call" | custom-call | tf_op jit(solution)/shard_map/combine/pallas_call | solution.py:741
Async XLA Ops:
  4.4 1.4 %collective-permute-start = (f32[8,2432]{1,0:T(8,128)S(1)}, f32[8,2432]{1,0:T(8,128)S(1)}, u32[]{:S(2)}, u32[]{:S(2)}) collective-permute-start(f32[8,2432]{1,0:T(8,128)S(1)} %get-tuple-element.22.own.ext_in.edges), channel_id=1, source_target_pairs={{0,8},{8,0},{16,24},{24,16},{1,9},{9,1},{17,25},{25,17},{2,10},{10... | collective-permute-start | bytes 233480 | tf_op jit(solution)/shard_map/ppermute | solution.py:700
  6.0 5.1 %collective-permute-start.1 = (f32[8,1664]{1,0:T(8,128)S(1)}, f32[8,1664]{1,0:T(8,128)S(1)}, u32[]{:S(2)}, u32[]{:S(2)}) collective-permute-start(f32[8,1664]{1,0:T(8,128)S(1)} %get-tuple-element.23.own), channel_id=1, source_target_pairs={{0,16},{8,24},{16,0},{24,8},{1,17},{9,25},{17,1},{25,9},{2,18},{10... | collective-permute-start | bytes 159752 | tf_op jit(solution)/shard_map/ppermute | solution.py:700
  11.2 3.9 %collective-permute-start.2 = (f32[8,896]{1,0:T(8,128)S(1)}, f32[8,896]{1,0:T(8,128)S(1)}, u32[]{:S(2)}, u32[]{:S(2)}) collective-permute-start(f32[8,896]{1,0:T(8,128)S(1)} %get-tuple-element.25.own.ext_in), channel_id=1, source_target_pairs={{0,1},{1,0},{2,3},{3,2},{4,5},{5,4},{6,7},{7,6},{8,9},{9,8},{10,11... | collective-permute-start | bytes 86024 | tf_op jit(solution)/shard_map/ppermute | solution.py:700
  15.3 4.0 %collective-permute-start.3 = (f32[8,896]{1,0:T(8,128)S(1)}, f32[8,896]{1,0:T(8,128)S(1)}, u32[]{:S(2)}, u32[]{:S(2)}) collective-permute-start(f32[8,896]{1,0:T(8,128)S(1)} %get-tuple-element.26.own), channel_id=1, source_target_pairs={{0,2},{1,3},{2,0},{3,1},{4,6},{5,7},{6,4},{7,5},{8,10},{9,11},{10,... | collective-permute-start | bytes 86024 | tf_op jit(solution)/shard_map/ppermute | solution.py:700
  19.4 5.0 %collective-permute-start.4 = (f32[8,896]{1,0:T(8,128)S(1)}, f32[8,896]{1,0:T(8,128)S(1)}, u32[]{:S(2)}, u32[]{:S(2)}) collective-permute-start(f32[8,896]{1,0:T(8,128)S(1)} %get-tuple-element.28.own), channel_id=1, source_target_pairs={{0,4},{1,5},{2,6},{3,7},{4,0},{5,1},{6,2},{7,3},{8,12},{9,13},{10,... | collective-permute-start | bytes 86024 | tf_op jit(solution)/shard_map/ppermute | solution.py:700
